TPU v7x, 32 devices: a whole 2x2x4 slice. The times are simulated.
32 devices in a mesh: dp: 4 (over z), fsdp: 8 (over y, x, core).
Axes of the slice: x: 2, y: 2, z: 4, core: 2. Of those that a mesh axis runs over, the one named last changes fastest.
Arguments:
- tokens: bfloat16 [2, 32, 128, 2048], P(None, ('dp', 'fsdp')), may hold values from -6 to 6
- lengths: int32 [2, 32], replicated, may hold values from 1 to 128, 2560 in all within a row
- order: int32 [2, 32], replicated, may hold values from 0 to 31, as said below
- w_query: bfloat16 [2048, 2048], P(('dp', 'fsdp')), may hold values from -0.125 to 0.125
- w_key: bfloat16 [2048, 2048], P(('dp', 'fsdp')), may hold values from -0.125 to 0.125
- w_value: bfloat16 [2048, 2048], P(('dp', 'fsdp')), may hold values from -0.125 to 0.125
- w_output: bfloat16 [2048, 2048], P(('dp', 'fsdp')), may hold values from -1 to 1
- w_gate: bfloat16 [2048, 8192], P(('dp', 'fsdp')), may hold values from -0.125 to 0.125
- w_up: bfloat16 [2048, 8192], P(('dp', 'fsdp')), may hold values from -0.125 to 0.125
- w_down: bfloat16 [2048, 8192], P(('dp', 'fsdp')), may hold values from -0.0625 to 0.0625
- gain_attn: bfloat16 [2048], P(('dp', 'fsdp')), may hold values from 0.5 to 1.5
- gain_ffn: bfloat16 [2048], P(('dp', 'fsdp')), may hold values from 0.5 to 1.5
- cotangent: bfloat16 [2, 32, 128, 2048], P(None, ('dp', 'fsdp')), may hold values from -6 to 6
Outputs:
- output: bfloat16 [2, 32, 128, 2048], P(None, ('dp', 'fsdp'))
- grad_tokens: bfloat16 [2, 32, 128, 2048], P(None, ('dp', 'fsdp'))
- grad_w_query: float32 [2048, 2048], P(('dp', 'fsdp'))
- grad_w_key: float32 [2048, 2048], P(('dp', 'fsdp'))
- grad_w_value: float32 [2048, 2048], P(('dp', 'fsdp'))
- grad_w_output: float32 [2048, 2048], P(('dp', 'fsdp'))
- grad_w_gate: float32 [2048, 8192], P(('dp', 'fsdp'))
- grad_w_up: float32 [2048, 8192], P(('dp', 'fsdp'))
- grad_w_down: float32 [2048, 8192], P(('dp', 'fsdp'))
- grad_gain_attn: float32 [2048], P(('dp', 'fsdp'))
- grad_gain_ffn: float32 [2048], P(('dp', 'fsdp'))
Inputs may be any that keep to these rules, and one draw needn't show every extreme that they name: `order`: for each micro-batch, a permutation of 0 to 31 that maps every aligned block of 8 sequences onto itself.
All inputs are finite; a program needn't handle non-finite values.
Results may differ from a plain program's by a relative error of at most 0.014.
Values may be sent and summed in bfloat16 or wider, within the bound.
No kernel may reach another device: no remote copies, remote signals or barrier semaphores. Data moves between devices by JAX's collectives and lax.ppermute only.
A program may use at most 512 MiB of HBM per device.

v0:
```python
import math

import jax
import jax.numpy as jnp
from jax import lax
from jax.sharding import PartitionSpec as P

H = 16
HD = 128


epsilon = 1e-05


def rope_tables(length_cap, head_size):
    halfway = head_size // 2
    position = jnp.arange(length_cap, dtype=jnp.float32)
    inverse = 10000.0 ** (-2.0 * jnp.arange(halfway, dtype=jnp.float32) / head_size)
    angles = position[:, None] * inverse[None, :]
    return (jnp.cos(angles)[:, None, :], jnp.sin(angles)[:, None, :])


def rotate(values, cosine, sine):
    halfway = values.shape[-1] // 2
    first_half = values[..., :halfway]
    second_half = values[..., halfway:]
    return jnp.concatenate(
        [first_half * cosine - second_half * sine, second_half * cosine + first_half * sine],
        axis=-1,
    )


def matmul(left, right):
    return jnp.dot(left, right, preferred_element_type=jnp.float32)


def against_rows(left, right):
    return lax.dot_general(
        left, right, (((1,), (1,)), ((), ())), preferred_element_type=jnp.float32
    )


def norm_backward(upstream, gain_full, normalized, inverse_rms):
    weighted = upstream * gain_full[None, :]
    return inverse_rms * (
        weighted - normalized * jnp.mean(weighted * normalized, axis=-1, keepdims=True)
    )


def picker(wanted, portions):
    amount = portions[0].shape[1]
    row_ids = jnp.arange(amount, dtype=jnp.int32)
    chosen = (row_ids[None, :] == wanted[:, None])[:, :, None, None]
    return tuple(
        (
            jnp.sum(jnp.where(chosen, portion, jnp.zeros((), portion.dtype)), axis=1)
            for portion in portions
        )
    )


def weight_terms(saved_set):
    (
        normed_one,
        grad_query,
        grad_key,
        grad_value,
        mixed_rows,
        grad_attended,
        normed_two,
        grad_gate,
        grad_up,
        grad_returned,
        activated,
    ) = saved_set

    def outer(left, right):
        return lax.dot_general(
            left, right, (((0,), (0,)), ((), ())), preferred_element_type=jnp.float32
        )

    return jnp.concatenate(
        [
            outer(normed_one, grad_query),
            outer(normed_one, grad_key),
            outer(normed_one, grad_value),
            outer(mixed_rows, grad_attended),
            outer(normed_two, grad_gate),
            outer(normed_two, grad_up),
            outer(grad_returned, activated),
        ],
        axis=1,
    )


def per_device(
    tokens,
    lengths,
    order,
    w_query,
    w_key,
    w_value,
    w_output,
    w_gate,
    w_up,
    w_down,
    gain_attn,
    gain_ffn,
    cotangent,
):
    group_size = lax.axis_size("fsdp")
    member = lax.axis_index("fsdp")
    base_slot = lax.axis_index("dp") * group_size
    my_slot = base_slot + member
    micro_count = tokens.shape[0]
    length_cap = tokens.shape[2]
    model_width = tokens.shape[3]
    hidden_width = w_gate.shape[1]
    total_rows = micro_count * length_cap
    slot_ids = jnp.arange(order.shape[1], dtype=jnp.int32)
    source_rows = jnp.sum(jnp.where(order == my_slot, slot_ids[None, :], 0), axis=1) - base_slot
    target_rows = lax.dynamic_slice_in_dim(order, my_slot, 1, 1)[:, 0] - base_slot
    live_counts = lax.dynamic_slice_in_dim(lengths, my_slot, 1, 1)[:, 0]
    arrived, cotan_rows = picker(
        source_rows,
        (
            lax.all_gather(tokens, "fsdp", axis=1, tiled=True),
            lax.all_gather(cotangent, "fsdp", axis=1, tiled=True),
        ),
    )
    (
        full_query,
        full_key,
        full_value,
        full_output,
        full_gate,
        full_up,
        full_down,
        gain_one_low,
        gain_two_low,
    ) = (
        lax.all_gather(w_query, ("dp", "fsdp"), axis=0, tiled=True),
        lax.all_gather(w_key, ("dp", "fsdp"), axis=0, tiled=True),
        lax.all_gather(w_value, ("dp", "fsdp"), axis=0, tiled=True),
        lax.all_gather(w_output, ("dp", "fsdp"), axis=0, tiled=True),
        lax.all_gather(w_gate, ("dp", "fsdp"), axis=0, tiled=True),
        lax.all_gather(w_up, ("dp", "fsdp"), axis=0, tiled=True),
        lax.all_gather(w_down, ("dp", "fsdp"), axis=0, tiled=True),
        lax.all_gather(gain_attn, ("dp", "fsdp"), axis=0, tiled=True),
        lax.all_gather(gain_ffn, ("dp", "fsdp"), axis=0, tiled=True),
    )
    gain_one_full = gain_one_low.astype(jnp.float32)
    gain_two_full = gain_two_low.astype(jnp.float32)
    cosine, sine = rope_tables(length_cap, HD)
    score_scale = 1.0 / math.sqrt(HD)
    score_shift = -math.log(length_cap)
    position = jnp.arange(length_cap, dtype=jnp.int32)
    causal = (position[:, None] >= position[None, :]).astype(jnp.float32)
    row_live = (position[None, :] < live_counts[:, None]).astype(jnp.float32)
    live_flat = row_live.reshape(total_rows, 1)
    allowed = causal[None, None, :, :] * row_live[:, None, None, :]
    block_x = arrived.astype(jnp.float32).reshape(total_rows, model_width)
    inverse_one = lax.rsqrt(jnp.mean(block_x * block_x, axis=-1, keepdims=True) + epsilon)
    normal_one = block_x * inverse_one
    normed_one = (normal_one * gain_one_full[None, :]).astype(jnp.bfloat16)
    raw_query = matmul(normed_one, full_query)
    raw_key = matmul(normed_one, full_key)
    raw_value = matmul(normed_one, full_value)
    head_shape = (micro_count, length_cap, H, HD)
    queries = rotate(raw_query.reshape(head_shape), cosine, sine).astype(jnp.bfloat16)
    key_rows = rotate(raw_key.reshape(head_shape), cosine, sine).astype(jnp.bfloat16)
    value_rows = raw_value.reshape(head_shape).astype(jnp.bfloat16)
    logits = (
        jnp.einsum("mqhe,mkhe->mhqk", queries, key_rows, preferred_element_type=jnp.float32)
        * score_scale
        + score_shift
    )
    sigmoid_vals = jax.nn.sigmoid(logits)
    prob_rows = (sigmoid_vals * allowed).astype(jnp.bfloat16)
    mixed_rows = (
        jnp.einsum("mhqk,mkhe->mqhe", prob_rows, value_rows, preferred_element_type=jnp.float32)
        .reshape(total_rows, model_width)
        .astype(jnp.bfloat16)
    )
    attended = matmul(mixed_rows, full_output)
    hidden_one = block_x + attended
    inverse_two = lax.rsqrt(jnp.mean(hidden_one * hidden_one, axis=-1, keepdims=True) + epsilon)
    normal_two = hidden_one * inverse_two
    normed_two = (normal_two * gain_two_full[None, :]).astype(jnp.bfloat16)
    gate_rows = matmul(normed_two, full_gate)
    up_rows = matmul(normed_two, full_up)
    sigmoid_gate = jax.nn.sigmoid(gate_rows)
    swish = gate_rows * sigmoid_gate
    activated = (swish * up_rows).astype(jnp.bfloat16)
    returned = against_rows(activated, full_down)
    layer_out = ((hidden_one + returned) * live_flat).astype(jnp.bfloat16)
    upstream = cotan_rows.astype(jnp.float32).reshape(total_rows, model_width) * live_flat
    grad_returned = upstream.astype(jnp.bfloat16)
    grad_activated = matmul(grad_returned, full_down)
    grad_gate = (
        grad_activated * up_rows * (sigmoid_gate * (1.0 + gate_rows * (1.0 - sigmoid_gate)))
    ).astype(jnp.bfloat16)
    grad_up = (grad_activated * swish).astype(jnp.bfloat16)
    grad_normed_two = against_rows(grad_gate, full_gate) + against_rows(grad_up, full_up)
    gain_two_sum = jnp.sum(grad_normed_two * normal_two, axis=0)
    grad_hidden = upstream + norm_backward(grad_normed_two, gain_two_full, normal_two, inverse_two)
    grad_attended = grad_hidden.astype(jnp.bfloat16)
    grad_mixed = against_rows(grad_attended, full_output)
    grad_mixed = grad_mixed.astype(jnp.bfloat16).reshape(head_shape)
    grad_probs = jnp.einsum(
        "mqhe,mkhe->mhqk", grad_mixed, value_rows, preferred_element_type=jnp.float32
    )
    grad_logits = (grad_probs * sigmoid_vals * (1.0 - sigmoid_vals) * allowed).astype(jnp.bfloat16)
    grad_value = (
        jnp.einsum("mhqk,mqhe->mkhe", prob_rows, grad_mixed, preferred_element_type=jnp.float32)
        .reshape(total_rows, model_width)
        .astype(jnp.bfloat16)
    )
    turned_query = (
        jnp.einsum("mhqk,mkhe->mqhe", grad_logits, key_rows, preferred_element_type=jnp.float32)
        * score_scale
    )
    turned_key = (
        jnp.einsum("mhqk,mqhe->mkhe", grad_logits, queries, preferred_element_type=jnp.float32)
        * score_scale
    )
    grad_query = (
        rotate(turned_query, cosine, -sine).reshape(total_rows, model_width).astype(jnp.bfloat16)
    )
    grad_key = (
        rotate(turned_key, cosine, -sine).reshape(total_rows, model_width).astype(jnp.bfloat16)
    )
    grad_normed_one = (
        against_rows(grad_query, full_query)
        + against_rows(grad_key, full_key)
        + against_rows(grad_value, full_value)
    )
    gain_one_sum = jnp.sum(grad_normed_one * normal_one, axis=0)
    grad_input = (
        grad_hidden + norm_backward(grad_normed_one, gain_one_full, normal_one, inverse_one)
    ).astype(jnp.bfloat16)
    saved_all = (
        normed_one,
        grad_query,
        grad_key,
        grad_value,
        mixed_rows,
        grad_attended,
        normed_two,
        grad_gate,
        grad_up,
        grad_returned,
        activated,
    )
    grad_shard = lax.psum_scatter(
        weight_terms(saved_all), ("dp", "fsdp"), scatter_dimension=0, tiled=True
    )
    gain_one_part, gain_two_part = (
        lax.psum_scatter(gain_one_sum, ("dp", "fsdp"), scatter_dimension=0, tiled=True),
        lax.psum_scatter(gain_two_sum, ("dp", "fsdp"), scatter_dimension=0, tiled=True),
    )
    stacked_out = layer_out.reshape(micro_count, length_cap, model_width)[:, None]
    stacked_grad = grad_input.reshape(micro_count, length_cap, model_width)[:, None]
    output, grad_tokens = picker(
        target_rows,
        (
            lax.all_gather(stacked_out, "fsdp", axis=1, tiled=True),
            lax.all_gather(stacked_grad, "fsdp", axis=1, tiled=True),
        ),
    )
    edges = [
        0,
        model_width,
        2 * model_width,
        3 * model_width,
        4 * model_width,
        4 * model_width + hidden_width,
        4 * model_width + 2 * hidden_width,
        4 * model_width + 3 * hidden_width,
    ]
    pieces_out = [grad_shard[:, edges[member_id] : edges[member_id + 1]] for member_id in range(7)]
    return (
        output[:, None],
        grad_tokens[:, None],
        pieces_out[0],
        pieces_out[1],
        pieces_out[2],
        pieces_out[3],
        pieces_out[4],
        pieces_out[5],
        pieces_out[6],
        gain_one_part,
        gain_two_part,
    )


def solution(mesh):
    in_specs = (
        P(None, ("dp", "fsdp"), None, None),
        P(),
        P(),
        P(("dp", "fsdp"), None),
        P(("dp", "fsdp"), None),
        P(("dp", "fsdp"), None),
        P(("dp", "fsdp"), None),
        P(("dp", "fsdp"), None),
        P(("dp", "fsdp"), None),
        P(("dp", "fsdp"), None),
        P(("dp", "fsdp")),
        P(("dp", "fsdp")),
        P(None, ("dp", "fsdp"), None, None),
    )
    out_specs = (
        P(None, ("dp", "fsdp"), None, None),
        P(None, ("dp", "fsdp"), None, None),
        P(("dp", "fsdp"), None),
        P(("dp", "fsdp"), None),
        P(("dp", "fsdp"), None),
        P(("dp", "fsdp"), None),
        P(("dp", "fsdp"), None),
        P(("dp", "fsdp"), None),
        P(("dp", "fsdp"), None),
        P(("dp", "fsdp")),
        P(("dp", "fsdp")),
    )
    return jax.shard_map(
        per_device, mesh=mesh, in_specs=in_specs, out_specs=out_specs, check_vma=False
    )
```

profile of v0, /device:TPU:0, one launch (start us, length us, event | category | flops | bytes accessed | tf_op | source)
XLA Modules:
  0.0 4075.5 jit_solution(2658054686410234215)
XLA Ops:
  14.0 42.5 %all-reduce.5 = (bf16[2048]{0:T(1024)(128)(2,1)S(1)}, bf16[2048]{0:T(1024)(128)(2,1)S(1)}) all-reduce(bf16[2048]{0:T(1024)(128)(2,1)S(1)} %dynamic-update-slice, bf16[2048]{0:T(1024)(128)(2,1)S(1)} %dynamic-update-slice.1), channel_id=1, replica_groups=mesh['dp'=4,'fsdp'=8] {'dp','fsdp'}, use_global_device_ids=true, to_apply=%add | all-reduce | flops 4096 | bytes 16384
  57.9 10.2 all-gather.12.cloned.1.call-done
  68.1 56.2 %all-gather.30.cloned.1.call-done = bf16[2,8,128,2048]{3,2,1,0:T(8,128)(2,1)} async-done(((bf16[2,1,128,2048]{3,2,1,0:T(8,128)(2,1)}), bf16[2,8,128,2048]{3,2,1,0:T(8,128)(2,1)}) %all-gather.30.cloned.1.call-update) | async-done | bytes 8388624 | tf_op jit(solution)/shard_map/all_gather | solution.py:128
  124.3 10.8 select_reduce_fusion.1
  137.8 66.9 %all-gather.14.cloned.1.call-done = bf16[2048,2048]{1,0:T(8,128)(2,1)} async-done(((bf16[64,2048]{1,0:T(8,128)(2,1)}), bf16[2048,2048]{1,0:T(8,128)(2,1)}) %all-gather.14.cloned.1.call-update) | async-done | bytes 8388624 | tf_op jit(solution)/shard_map/all_gather | solution.py:144
  204.7 12.4 copy.56
  217.1 66.4 %all-gather.18.cloned.1.call-done = bf16[2048,2048]{1,0:T(8,128)(2,1)} async-done(((bf16[64,2048]{1,0:T(8,128)(2,1)}), bf16[2048,2048]{1,0:T(8,128)(2,1)}) %all-gather.18.cloned.1.call-update) | async-done | bytes 8388624 | tf_op jit(solution)/shard_map/all_gather | solution.py:143
  283.5 12.4 copy.58
  295.9 66.4 %all-gather.16.cloned.1.call-done = bf16[2048,2048]{1,0:T(8,128)(2,1)} async-done(((bf16[64,2048]{1,0:T(8,128)(2,1)}), bf16[2048,2048]{1,0:T(8,128)(2,1)}) %all-gather.16.cloned.1.call-update) | async-done | bytes 8388624 | tf_op jit(solution)/shard_map/all_gather | solution.py:142
  362.3 12.3 copy.57
  393.8 47.2 %all-gather.20.cloned.1.call-done = bf16[2048,2048]{1,0:T(8,128)(2,1)} async-done(((bf16[64,2048]{1,0:T(8,128)(2,1)}), bf16[2048,2048]{1,0:T(8,128)(2,1)}) %all-gather.20.cloned.1.call-update) | async-done | bytes 8388624 | tf_op jit(solution)/shard_map/all_gather | solution.py:145
  441.1 6.2 multiply_reduce_fusion.4
  447.6 189.8 %all-gather.26.cloned.1.call-done = bf16[2048,8192]{1,0:T(8,128)(2,1)} async-done(((bf16[64,8192]{1,0:T(8,128)(2,1)}), bf16[2048,8192]{1,0:T(8,128)(2,1)}) %all-gather.26.cloned.1.call-update) | async-done | bytes 33554448 | tf_op jit(solution)/shard_map/all_gather | solution.py:148
  637.3 18.5 fusion.45
  655.9 177.3 %all-gather.22.cloned.1.call-done = bf16[2048,8192]{1,0:T(8,128)(2,1)} async-done(((bf16[64,8192]{1,0:T(8,128)(2,1)}), bf16[2048,8192]{1,0:T(8,128)(2,1)}) %all-gather.22.cloned.1.call-update) | async-done | bytes 33554448 | tf_op jit(solution)/shard_map/all_gather | solution.py:146
  833.2 17.8 fusion.44
  851.0 178.0 %all-gather.24.cloned.1.call-done = bf16[2048,8192]{1,0:T(8,128)(2,1)} async-done(((bf16[64,8192]{1,0:T(8,128)(2,1)}), bf16[2048,8192]{1,0:T(8,128)(2,1)}) %all-gather.24.cloned.1.call-update) | async-done | bytes 33554448 | tf_op jit(solution)/shard_map/all_gather | solution.py:147
  1029.0 28.5 multiply_convert_fusion.2
  1057.6 17.0 fusion.2
  1074.6 18.2 fusion.46
  1092.8 19.9 multiply_reduce_fusion
  1148.5 5.9 convolution_add_fusion.3
  1159.7 10.3 convolution_dynamic-update-slice_fusion.6
  1170.0 8.8 convolution_dynamic-update-slice_fusion.5
  1178.8 9.3 convolution_dynamic-update-slice_fusion.4
  1188.2 8.3 convolution_dynamic-update-slice_fusion.3
  1196.5 24.3 convolution_dynamic-update-slice_fusion.2
  1220.8 23.7 convolution_dynamic-update-slice_fusion.1
  1244.4 23.5 convolution_dynamic-update-slice_fusion
  1268.8 56.5 %all-reduce.4 = (f32[2048]{0:T(1024)S(1)}, f32[2048]{0:T(1024)S(1)}) all-reduce(f32[2048]{0:T(1024)S(1)} %copy-done.39, f32[2048]{0:T(1024)S(1)} %copy-done.38), channel_id=3, replica_groups=mesh['dp'=4,'fsdp'=8] {'dp','fsdp'}, use_global_device_ids=true, to_apply=%region_11.12.clone | all-reduce | flops 4096 | bytes 32768
  1326.5 11.9 select_reduce_fusion
  1338.4 2721.1 %reduce-scatter.2.cloned.1.call-done = f32[64,32768]{1,0:T(8,128)} async-done(((f32[2048,32768]{1,0:T(8,128)}), f32[64,32768]{1,0:T(8,128)}) %reduce-scatter.2.cloned.1.call-update) | async-done | bytes 8388624 | tf_op jit(solution)/shard_map/reduce_scatter | solution.py:255
  (178 shorter events, 81.6 us)
Async XLA Ops:
  7.2 49.4 %copy-start = (s32[2,32]{1,0:T(2,128)S(1)}, s32[2,32]{1,0:T(2,128)}, u32[]{:S(2)}) copy-start(s32[2,32]{1,0:T(2,128)} %param.14) | copy-start | bytes 772
  7.2 60.9 %all-gather.12.cloned.1.call-start = ((), (), s32[]{:S(2)}) async-start(), calls=%async_computation.1 | async-start | bytes 9437184 | tf_op jit(solution)/shard_map/all_gather | solution.py:127
  7.9 116.4 %all-gather.30.cloned.1.call-start = ((), (), s32[]{:S(2)}) async-start(), calls=%async_computation.10 | async-start | bytes 9437184 | tf_op jit(solution)/shard_map/all_gather | solution.py:128
  8.7 48.1 %copy-start.41 = (s32[2,32]{1,0:T(2,128)S(1)}, s32[2,32]{1,0:T(2,128)}, u32[]{:S(2)}) copy-start(s32[2,32]{1,0:T(2,128)} %param.15) | copy-start | bytes 772
  8.7 196.0 %all-gather.14.cloned.1.call-start = ((), (), s32[]{:S(2)}) async-start(), calls=%async_computation.2 | async-start | bytes 8650752 | tf_op jit(solution)/shard_map/all_gather | solution.py:144
  9.4 274.1 %all-gather.18.cloned.1.call-start = ((), (), s32[]{:S(2)}) async-start(), calls=%async_computation.4 | async-start | bytes 8650752 | tf_op jit(solution)/shard_map/all_gather | solution.py:143
  10.0 352.3 %all-gather.16.cloned.1.call-start = ((), (), s32[]{:S(2)}) async-start(), calls=%async_computation.3 | async-start | bytes 8650752 | tf_op jit(solution)/shard_map/all_gather | solution.py:142
  10.6 430.5 %all-gather.20.cloned.1.call-start = ((), (), s32[]{:S(2)}) async-start(), calls=%async_computation.5 | async-start | bytes 8650752 | tf_op jit(solution)/shard_map/all_gather | solution.py:145
  11.2 626.2 %all-gather.26.cloned.1.call-start = ((), (), s32[]{:S(2)}) async-start(), calls=%async_computation.8 | async-start | bytes 34603008 | tf_op jit(solution)/shard_map/all_gather | solution.py:148
  11.9 821.2 %all-gather.22.cloned.1.call-start = ((), (), s32[]{:S(2)}) async-start(), calls=%async_computation.6 | async-start | bytes 34603008 | tf_op jit(solution)/shard_map/all_gather | solution.py:146
  12.7 1016.3 %all-gather.24.cloned.1.call-start = ((), (), s32[]{:S(2)}) async-start(), calls=%async_computation.7 | async-start | bytes 34603008 | tf_op jit(solution)/shard_map/all_gather | solution.py:147
  13.4 1313.1 %all-gather.28.cloned.1.call-start = ((), (), s32[]{:S(2)}) async-start(), calls=%async_computation.9 | async-start | bytes 9437184 | tf_op jit(solution)/shard_map/all_gather | solution.py:267
  56.6 81.0 %copy-start.36 = (f32[2048]{0:T(1024)}, f32[2048]{0:T(1024)S(1)}, u32[]{:S(2)}) copy-start(f32[2048]{0:T(1024)S(1)} %convert_element_type.194) | copy-start | bytes 24580
  57.9 325.1 %copy-start.33 = (f32[128,64]{0,1:T(8,128)}, f32[128,64]{0,1:T(8,128)S(1)}, u32[]{:S(2)}) copy-start(f32[128,64]{0,1:T(8,128)S(1)} %get-tuple-element.49) | copy-start | bytes 98308
  135.1 306.0 %copy-start.5 = (bf16[2,128,2048]{2,1,0:T(8,128)(2,1)}, bf16[2,128,2048]{2,1,0:T(8,128)(2,1)S(1)}, u32[]{:S(2)}) copy-start(bf16[2,128,2048]{2,1,0:T(8,128)(2,1)S(1)} %get-tuple-element.18) | copy-start | bytes 3145732
  137.8 247.1 %copy-start.3 = (bf16[2,128,2048]{2,1,0:T(8,128)(2,1)}, bf16[2,128,2048]{2,1,0:T(8,128)(2,1)S(1)}, u32[]{:S(2)}) copy-start(bf16[2,128,2048]{2,1,0:T(8,128)(2,1)S(1)} %multiply_convert_fusion.6) | copy-start | bytes 3145732
  447.3 610.3 %copy-start.11 = (f32[256,2048]{1,0:T(8,128)}, f32[256,2048]{1,0:T(8,128)S(1)}, u32[]{:S(2)}) copy-start(f32[256,2048]{1,0:T(8,128)S(1)} %get-tuple-element.53) | copy-start | bytes 6291460
  447.6 581.5 %copy-start.7 = (bf16[256,2048]{1,0:T(8,128)(2,1)}, bf16[256,2048]{1,0:T(8,128)(2,1)S(1)}, u32[]{:S(2)}) copy-start(bf16[256,2048]{1,0:T(8,128)(2,1)S(1)} %multiply_convert_fusion.4) | copy-start | bytes 3145732
  1074.5 251.9 %all-gather.32.cloned.1.call-start = ((), (), s32[]{:S(2)}) async-start(), calls=%async_computation.11 | async-start | bytes 9437184 | tf_op jit(solution)/shard_map/all_gather | solution.py:268
  1074.6 18.2 copy-start.12
  1092.8 19.9 copy-start.10
  1139.5 9.0 copy-start.21
  1142.5 11.9 slice-start
  1159.4 2900.1 %reduce-scatter.2.cloned.1.call-start = ((), (), s32[]{:S(2)}) async-start(), calls=%async_computation.12 | async-start | bytes 276824064 | tf_op jit(solution)/shard_map/reduce_scatter | solution.py:255
  1159.7 10.3 copy-start.23
  1170.0 8.8 copy-start.20
  1178.8 9.3 copy-start.18
  1188.2 8.3 copy-start.8
  1188.2 8.3 copy-start.17
  1196.5 24.3 copy-start.16
  1220.8 23.7 copy-start.14
  1220.8 23.7 copy-start.15
  (29 other events, 91.9 us)
Sparse Core Ops, SparseCore 0:
  9.9 58.1 all-gather.11
  70.0 54.2 all-gather.29
  127.2 77.4 all-gather.13
  207.4 76.0 all-gather.17
  286.2 76.0 all-gather.15
  365.0 76.0 all-gather.19
  443.9 193.3 all-gather.25
  640.2 192.9 all-gather.21
  836.0 192.9 all-gather.23
  1074.7 52.5 all-gather.27
  1159.6 52.9 all-gather.31
  1268.1 2791.4 reduce-scatter.1
where the time goes:
time: 4090 us; the launch traced here: 4080 us
  waiting for transfers between devices  3590 us (88%)
  matrix products  274 us (7%)
  blocking collectives  99 us (2%)
  local copies, waits for them, and re-layouts  66.8 us (2%)
    reduce_scatter x1, waiting for transfers between devices, per_device(): lax.psum_scatter(weight_terms(saved_all), ('dp', 'fsdp'), scatter_dimensi...  2720 us
    all_gather x1, waiting for transfers between devices, per_device(): lax.all_gather(w_down, ('dp', 'fsdp'), axis=0, tiled=True)  190 us
    all_gather x1, waiting for transfers between devices, per_device(): lax.all_gather(w_up, ('dp', 'fsdp'), axis=0, tiled=True)  178 us
    all_gather x1, waiting for transfers between devices, per_device(): lax.all_gather(w_gate, ('dp', 'fsdp'), axis=0, tiled=True)  177 us
    dot_general x7, matrix products, outer(): lax.dot_general(left, right, (((0,), (0,)), ((), ())), preferred_element_...  108 us
    unnamed x2, blocking collectives  99 us
  transfers between devices with their start and end apart: 12, of which 10 were waited for; matrix products, arithmetic and copies ran while one was open for 8% of the time, Pallas kernels for 0%

commit v1 on v0

v1 whole, which is shorter than its diff:
```python
import math

import jax
import jax.numpy as jnp
from jax import lax
from jax.sharding import PartitionSpec as P

H = 16
HD = 128
EPSILON = 1e-05
F32 = jnp.float32
BF16 = jnp.bfloat16


def rope_tables(length_cap, head_size):
    halfway = head_size // 2
    position = jnp.arange(length_cap, dtype=F32)
    inverse = 10000.0 ** (-2.0 * jnp.arange(halfway, dtype=F32) / head_size)
    angles = position[:, None] * inverse[None, :]
    return jnp.cos(angles)[:, None, :], jnp.sin(angles)[:, None, :]


def rotate(values, cosine, sine):
    halfway = values.shape[-1] // 2
    first_half = values[..., :halfway]
    second_half = values[..., halfway:]
    return jnp.concatenate(
        [first_half * cosine - second_half * sine, second_half * cosine + first_half * sine],
        axis=-1,
    )


def dot_nn(left, right):
    return lax.dot_general(left, right, (((1,), (0,)), ((), ())), preferred_element_type=F32)


def dot_nt(left, right):
    return lax.dot_general(left, right, (((1,), (1,)), ((), ())), preferred_element_type=F32)


def dot_tn(left, right):
    return lax.dot_general(left, right, (((0,), (0,)), ((), ())), preferred_element_type=F32)


def swap(value, offset):
    return lax.ppermute(value, "fsdp", [(i, i ^ offset) for i in range(8)])


def add_low(left, right):
    return (left.astype(F32) + right.astype(F32)).astype(BF16)


def gather_group(rows):
    if lax.axis_size("fsdp") != 8:
        return lax.all_gather(rows, "fsdp", axis=1)
    a, b = {0: rows[0]}, {0: rows[1]}
    a[2], b[4] = swap(a[0], 2), swap(b[0], 4)
    a[1], b[1] = swap(a[0], 1), swap(b[0], 1)
    a[4], b[2] = swap(a[0], 4), swap(b[0], 2)
    a[6], b[6] = swap(a[2], 4), swap(b[4], 2)
    a[3], b[5] = swap(a[2], 1), swap(b[4], 1)
    a[5], b[3] = swap(a[4], 1), swap(b[2], 1)
    a[7], b[7] = swap(a[6], 1), swap(b[6], 1)
    return jnp.stack([a[k] for k in range(8)] + [b[k] for k in range(8)]).reshape(
        (2, 8) + rows.shape[1:]
    )


def scatter_group(parts):
    if lax.axis_size("fsdp") != 8:
        return lax.psum_scatter(parts, "fsdp", scatter_dimension=1).astype(F32)
    pairs = parts.reshape((2, 4, 2) + parts.shape[2:])
    pairs = add_low(pairs[:, :, 0], swap(pairs[:, :, 1], 1))
    a, b = pairs[0], pairs[1]
    a = add_low(a[:2], swap(a[2:], 4))
    b = b.reshape((2, 2) + b.shape[1:])
    b = add_low(b[:, 0], swap(b[:, 1], 2))
    a = a[0].astype(F32) + swap(a[1], 2).astype(F32)
    b = b[0].astype(F32) + swap(b[1], 4).astype(F32)
    return jnp.stack([a, b])


def spread(pieces):
    count, rows, columns = pieces.shape
    return lax.all_to_all(pieces.reshape(count * rows, columns), "fsdp", 0, 0, tiled=True)


def per_device(
    tokens,
    lengths,
    order,
    w_query,
    w_key,
    w_value,
    w_output,
    w_gate,
    w_up,
    w_down,
    gain_attn,
    gain_ffn,
    cotangent,
):
    groups, members = lax.axis_size("dp"), lax.axis_size("fsdp")
    plane, member = lax.axis_index("dp"), lax.axis_index("fsdp")
    micro, _, cap, width = tokens.shape
    own_rows = w_query.shape[0]
    hidden = w_gate.shape[1]
    share = hidden // members
    sharers = HD // own_rows
    kinds = members // sharers
    my_heads = groups // sharers
    head_cols = my_heads * HD
    total = micro * members * cap
    scale = 1.0 / math.sqrt(HD)
    shift = -math.log(cap)

    slots = jnp.arange(order.shape[1], dtype=jnp.int32)
    block = jnp.arange(members, dtype=jnp.int32)
    at = plane * members + (block ^ member if members == 8 else block)
    chosen = jnp.sum(jnp.where(at[None, :, None] == slots, order[:, None, :], 0), axis=-1)
    live = jnp.sum(jnp.where(chosen[:, :, None] == slots, lengths[:, None, :], 0), axis=-1)
    position = jnp.arange(cap, dtype=jnp.int32)
    at_me = plane * members + member
    my_slot = jnp.sum(jnp.where(slots == at_me, order, 0), axis=-1)
    my_live = jnp.sum(jnp.where(slots == my_slot[:, None], lengths, 0), axis=-1)
    my_mask = (position < my_live[:, None]).astype(F32)[:, :, None]

    gain_one = gain_attn.astype(F32)[:, None]
    gain_two = gain_ffn.astype(F32)[:, None]

    def scaled(weight, gain):
        return (weight.astype(F32) * gain).astype(BF16)

    def by_head(weight):
        cut = weight.reshape(own_rows, sharers, my_heads, kinds, HD)
        return cut.transpose(3, 1, 0, 2, 4).reshape(members, own_rows, head_cols)

    def by_unit(weight):
        return weight.reshape(own_rows, members, share).transpose(1, 0, 2)

    def planes(value):
        return lax.all_gather(value, "dp", axis=0, tiled=True)

    wqkv = planes(
        spread(
            jnp.concatenate(
                [by_head(scaled(w, gain_one)) for w in (w_query, w_key, w_value)], axis=2
            )
        )
    )
    wgu = planes(
        spread(jnp.concatenate([by_unit(scaled(w, gain_two)) for w in (w_gate, w_up)], axis=2))
    )
    wd = planes(spread(by_unit(w_down)))
    raw = planes(w_output).reshape(sharers, my_heads, own_rows, width)
    subgroups = [[s * sharers + i for i in range(sharers)] for s in range(kinds)]

    def exchange(value):
        return lax.all_to_all(value, "fsdp", 0, 0, axis_index_groups=subgroups)

    wo = exchange(raw).transpose(1, 0, 2, 3).reshape(head_cols, width)

    x = tokens[:, 0].astype(F32)
    inverse_one = lax.rsqrt(jnp.mean(x * x, axis=-1, keepdims=True) + EPSILON)
    normal_one = x * inverse_one
    n1 = gather_group(normal_one.astype(BF16)).reshape(total, width)
    upstream = cotangent[:, 0].astype(F32) * my_mask
    returned_grad = gather_group(upstream.astype(BF16)).reshape(total, width)

    cosine, sine = rope_tables(cap, HD)
    causal = position[:, None] >= position[None, :]
    allowed = (
        causal[None, None] & (position[None, :] < live.reshape(-1, 1))[:, None, None, :]
    ).astype(F32)
    heads = (micro * members, cap, 3, my_heads, HD)
    qkv = dot_nn(n1, wqkv).reshape(heads)
    queries = rotate(qkv[:, :, 0], cosine, sine).astype(BF16)
    keys = rotate(qkv[:, :, 1], cosine, sine).astype(BF16)
    values = qkv[:, :, 2].astype(BF16)
    logits = (
        jnp.einsum("gqhe,gkhe->ghqk", queries, keys, preferred_element_type=F32) * scale + shift
    )
    gates = jax.nn.sigmoid(logits)
    probs = (gates * allowed).astype(BF16)
    mixed = (
        jnp.einsum("ghqk,gkhe->gqhe", probs, values, preferred_element_type=F32)
        .reshape(total, head_cols)
        .astype(BF16)
    )
    block_shape = (micro, members, cap, width)
    attended = scatter_group(dot_nn(mixed, wo).astype(BF16).reshape(block_shape))
    hidden_one = x + attended

    inverse_two = lax.rsqrt(jnp.mean(hidden_one * hidden_one, axis=-1, keepdims=True) + EPSILON)
    normal_two = hidden_one * inverse_two
    n2 = gather_group(normal_two.astype(BF16)).reshape(total, width)
    gate_up = dot_nn(n2, wgu)
    gate, up = gate_up[:, :share], gate_up[:, share:]
    sigmoid_gate = jax.nn.sigmoid(gate)
    swish = gate * sigmoid_gate
    activated = (swish * up).astype(BF16)
    returned = scatter_group(dot_nt(activated, wd).astype(BF16).reshape(block_shape))
    output = ((hidden_one + returned) * my_mask).astype(BF16)

    grad_activated = dot_nn(returned_grad, wd)
    grad_gate = grad_activated * up * (sigmoid_gate * (1.0 + gate * (1.0 - sigmoid_gate)))
    grad_up = grad_activated * swish
    grad_gu = jnp.concatenate([grad_gate.astype(BF16), grad_up.astype(BF16)], axis=1)
    back_two = scatter_group(dot_nt(grad_gu, wgu).astype(BF16).reshape(block_shape))
    grad_hidden = upstream + inverse_two * (
        back_two - normal_two * jnp.mean(back_two * normal_two, axis=-1, keepdims=True)
    )

    grad_attended = gather_group(grad_hidden.astype(BF16)).reshape(total, width)
    grad_mixed = (
        dot_nt(grad_attended, wo).astype(BF16).reshape(micro * members, cap, my_heads, HD)
    )
    grad_probs = jnp.einsum("gqhe,gkhe->ghqk", grad_mixed, values, preferred_element_type=F32)
    grad_logits = (grad_probs * gates * (1.0 - gates) * allowed).astype(BF16)
    grad_values = jnp.einsum("ghqk,gqhe->gkhe", probs, grad_mixed, preferred_element_type=F32)
    turned_q = (
        jnp.einsum("ghqk,gkhe->gqhe", grad_logits, keys, preferred_element_type=F32) * scale
    )
    turned_k = (
        jnp.einsum("ghqk,gqhe->gkhe", grad_logits, queries, preferred_element_type=F32) * scale
    )
    grad_qkv = jnp.concatenate(
        [
            value.reshape(total, head_cols).astype(BF16)
            for value in (
                rotate(turned_q, cosine, -sine),
                rotate(turned_k, cosine, -sine),
                grad_values,
            )
        ],
        axis=1,
    )
    back_one = scatter_group(dot_nt(grad_qkv, wqkv).astype(BF16).reshape(block_shape))
    grad_tokens = (
        grad_hidden
        + inverse_one
        * (back_one - normal_one * jnp.mean(back_one * normal_one, axis=-1, keepdims=True))
    ).astype(BF16)

    def home(value):
        mine = lax.psum_scatter(value.astype(BF16), "dp", scatter_dimension=0, tiled=True)
        return lax.all_to_all(mine, "fsdp", 0, 0, tiled=True).reshape(members, own_rows, -1)

    sum_d = home(dot_tn(returned_grad, activated))
    sum_gu = home(dot_tn(n2, grad_gu))
    sum_qkv = home(dot_tn(n1, grad_qkv))
    part_o = dot_tn(mixed, grad_attended).astype(BF16)
    part_o = exchange(part_o.reshape(my_heads, sharers, own_rows, width).transpose(1, 0, 2, 3))
    grad_wo = lax.psum_scatter(
        part_o.reshape(groups, own_rows, width), "dp", scatter_dimension=0
    ).astype(F32)

    def from_heads(value):
        cut = value.reshape(kinds, sharers, own_rows, my_heads, HD)
        return cut.transpose(2, 1, 3, 0, 4).reshape(own_rows, width).astype(F32)

    def from_units(value):
        return value.transpose(1, 0, 2).reshape(own_rows, hidden).astype(F32)

    raw_qkv = [
        from_heads(sum_qkv[:, :, i * head_cols : (i + 1) * head_cols]) for i in range(3)
    ]
    raw_gu = [from_units(sum_gu[:, :, i * share : (i + 1) * share]) for i in range(2)]
    grad_gain_one = sum(
        jnp.sum(g * w.astype(F32), axis=1)
        for g, w in zip(raw_qkv, (w_query, w_key, w_value), strict=True)
    )
    grad_gain_two = sum(
        jnp.sum(g * w.astype(F32), axis=1) for g, w in zip(raw_gu, (w_gate, w_up), strict=True)
    )
    return (
        output[:, None],
        grad_tokens[:, None],
        raw_qkv[0] * gain_one,
        raw_qkv[1] * gain_one,
        raw_qkv[2] * gain_one,
        grad_wo,
        raw_gu[0] * gain_two,
        raw_gu[1] * gain_two,
        from_units(sum_d),
        grad_gain_one,
        grad_gain_two,
    )


def solution(mesh):
    both = ("dp", "fsdp")
    sequences = P(None, both, None, None)
    rows = P(both, None)
    in_specs = (sequences, P(), P()) + (rows,) * 7 + (P(both), P(both), sequences)
    out_specs = (sequences, sequences) + (rows,) * 7 + (P(both), P(both))
    return jax.shard_map(
        per_device, mesh=mesh, in_specs=in_specs, out_specs=out_specs, check_vma=False
    )
```

time: 4090 us -> 827 us (0.20)
  waiting for transfers between devices: 3590 us -> 353 us
  matrix products: 274 us -> 172 us
  blocking collectives: 99 us -> 6.64 us
  starting transfers between devices: 0.67 us -> 88.3 us
  local copies, waits for them, and re-layouts: 66.8 us -> 119 us
    reduce_scatter x1 -> x4, waiting for transfers between devices: 2720 us -> 49.8 us  [the longest x3 49.8 us: home(): lax.psum_scatter(value.astype(BF16), 'dp', scatter_dimension=0, tiled=True)]
    all_gather x11 -> x4, waiting for transfers between devices: 859 us -> 0.01 us  [planes(): return lax.all_gather(value, 'dp', axis=0, tiled=True)]
    ppermute x0 -> x76, waiting for transfers between devices: none -> 250 us  [swap(): return lax.ppermute(value, 'fsdp', [(i, i ^ offset) for i in range(8)])]
    dot_general x27 -> x18, matrix products: 274 us -> 172 us  [the longest x4 59.7 us: dot_nn(): lax.dot_general(left, right, (((1,), (0,)), ((), ())), preferred_element_...]
    unnamed x2 -> x0, blocking collectives: 99 us -> none
    unnamed x105 -> x179, local copies, waits for them, and re-layouts: 9.6 us -> 70.4 us
    ppermute x0 -> x76, starting transfers between devices: none -> 56.2 us  [swap(): return lax.ppermute(value, 'fsdp', [(i, i ^ offset) for i in range(8)])]
    all_to_all x0 -> x7, waiting for transfers between devices: none -> 51.7 us  [the longest x3 28 us: home(): lax.all_to_all(mine, 'fsdp', 0, 0, tiled=True)]
  transfers between devices with their start and end apart: 12 -> 91, of which waited for: 10 -> 35; matrix products, arithmetic and copies ran while one was open for 8% -> 35% of each run, Pallas kernels for 0% -> 0%
where the time goes in v1:
time: 827 us; the launch traced here: 818 us
  waiting for transfers between devices  353 us (43%)
  matrix products  172 us (21%)
  local copies, waits for them, and re-layouts  119 us (14%)
  starting transfers between devices  88.3 us (11%)
  other arithmetic  62.8 us (8%)
  between operations  15.8 us (2%)
    ppermute x76, waiting for transfers between devices, swap(): return lax.ppermute(value, 'fsdp', [(i, i ^ offset) for i in range(8)])  250 us
    unnamed x179, local copies, waits for them, and re-layouts  70.4 us
    dot_general x4, matrix products, dot_nn(): lax.dot_general(left, right, (((1,), (0,)), ((), ())), preferred_element_...  59.7 us
    ppermute x76, starting transfers between devices, swap(): return lax.ppermute(value, 'fsdp', [(i, i ^ offset) for i in range(8)])  56.2 us
    dot_general x4, matrix products, dot_tn(): lax.dot_general(left, right, (((0,), (0,)), ((), ())), preferred_element_...  53.9 us
    dot_general x4, matrix products, dot_nt(): lax.dot_general(left, right, (((1,), (1,)), ((), ())), preferred_element_...  51.2 us
    reduce_scatter x3, waiting for transfers between devices, home(): lax.psum_scatter(value.astype(BF16), 'dp', scatter_dimension=0, tiled=True)  49.8 us
    all_to_all x3, waiting for transfers between devices, home(): lax.all_to_all(mine, 'fsdp', 0, 0, tiled=True)  28 us
  transfers between devices with their start and end apart: 91, of which 35 were waited for; matrix products, arithmetic and copies ran while one was open for 35% of the time, Pallas kernels for 0%

profile of v1, /device:TPU:0, one launch (start us, length us, event | category | flops | bytes accessed | tf_op | source)
XLA Modules:
  0.0 817.7 jit_solution(15363287010893997005)
XLA Ops:
  23.6 7.4 all-to-all-done
  52.0 16.2 %all-to-all-done.2 = bf16[8,64,2048]{2,1,0:T(8,128)(2,1)} async-done(((bf16[8,64,2048]{2,1,0:T(8,128)(2,1)}), bf16[8,64,2048]{2,1,0:T(8,128)(2,1)}, u32[]{:S(2)}, u32[]{:S(2)}) %all-to-all-start.2) | async-done | bytes 2097184 | tf_op jit(solution)/shard_map/all_to_all | solution.py:85
  68.2 9.8 %collective-permute-done.1 = bf16[128,2048]{1,0:T(8,128)(2,1)} collective-permute-done((bf16[128,2048]{1,0:T(8,128)(2,1)}, bf16[128,2048]{1,0:T(8,128)(2,1)}, u32[]{:S(2)}, u32[]{:S(2)}) %collective-permute-start.1) | collective-permute-done | bytes 524320 | tf_op jit(solution)/shard_map/ppermute | solution.py:46
  88.4 19.3 %collective-permute-done.5 = bf16[128,2048]{1,0:T(8,128)(2,1)S(1)} collective-permute-done((bf16[128,2048]{1,0:T(8,128)(2,1)}, bf16[128,2048]{1,0:T(8,128)(2,1)S(1)}, u32[]{:S(2)}, u32[]{:S(2)}) %collective-permute-start.5) | collective-permute-done | bytes 524320 | tf_op jit(solution)/shard_map/ppermute | solution.py:46
  117.5 9.2 %collective-permute-done.39 = bf16[128,2048]{1,0:T(8,128)(2,1)} collective-permute-done((bf16[128,2048]{1,0:T(8,128)(2,1)}, bf16[128,2048]{1,0:T(8,128)(2,1)}, u32[]{:S(2)}, u32[]{:S(2)}) %collective-permute-start.39) | collective-permute-done | bytes 524320 | tf_op jit(solution)/shard_map/ppermute | solution.py:46
  128.2 8.9 %collective-permute-done.12 = bf16[128,2048]{1,0:T(8,128)(2,1)S(1)} collective-permute-done((bf16[128,2048]{1,0:T(8,128)(2,1)S(1)}, bf16[128,2048]{1,0:T(8,128)(2,1)S(1)}, u32[]{:S(2)}, u32[]{:S(2)}) %collective-permute-start.12) | collective-permute-done | bytes 524320 | tf_op jit(solution)/shard_map/ppermute | solution.py:46
  158.9 10.1 %fusion.4 = f32[16,128,3,2,128]{1,4,3,2,0:T(8,128)S(1)} fusion(bf16[3,2,128,2048,1]{3,2,1,0,4:T(8,128)(2,1)} %bitcast.588, bf16[16,128,2048]{2,1,0:T(8,128)(2,1)} %bitcast_dynamic-update-slice_fusion.45), kind=kOutput, calls=%fused_computation.9 | convolution fusion | flops 6442450944 | bytes 17825792 | tf_op jit(solution)/shard_map/dot_general | solution.py:34
  220.8 19.3 %collective-permute-done.15 = bf16[2,128,2048]{2,1,0:T(8,128)(2,1)S(1)} collective-permute-done((bf16[2,128,2048]{2,1,0:T(8,128)(2,1)S(1)}, bf16[2,128,2048]{2,1,0:T(8,128)(2,1)S(1)}, u32[]{:S(2)}, u32[]{:S(2)}) %collective-permute-start.15) | collective-permute-done | bytes 1048608 | tf_op jit(solution)/shard_map/ppermute | solution.py:46
  244.6 9.1 %collective-permute-done.16 = bf16[128,2048]{1,0:T(8,128)(2,1)S(1)} collective-permute-done((bf16[128,2048]{1,0:T(8,128)(2,1)S(1)}, bf16[128,2048]{1,0:T(8,128)(2,1)S(1)}, u32[]{:S(2)}, u32[]{:S(2)}) %collective-permute-start.16) | collective-permute-done | bytes 524320 | tf_op jit(solution)/shard_map/ppermute | solution.py:46
  263.1 10.1 %collective-permute-done.20 = bf16[128,2048]{1,0:T(8,128)(2,1)S(1)} collective-permute-done((bf16[128,2048]{1,0:T(8,128)(2,1)S(1)}, bf16[128,2048]{1,0:T(8,128)(2,1)S(1)}, u32[]{:S(2)}, u32[]{:S(2)}) %collective-permute-start.20) | collective-permute-done | bytes 524320 | tf_op jit(solution)/shard_map/ppermute | solution.py:46
  277.2 10.9 %collective-permute-done.22 = bf16[128,2048]{1,0:T(8,128)(2,1)S(1)} collective-permute-done((bf16[128,2048]{1,0:T(8,128)(2,1)S(1)}, bf16[128,2048]{1,0:T(8,128)(2,1)S(1)}, u32[]{:S(2)}, u32[]{:S(2)}) %collective-permute-start.22) | collective-permute-done | bytes 524320 | tf_op jit(solution)/shard_map/ppermute | solution.py:46
  291.8 8.4 %collective-permute-done.31 = bf16[128,2048]{1,0:T(8,128)(2,1)S(1)} collective-permute-done((bf16[128,2048]{1,0:T(8,128)(2,1)S(1)}, bf16[128,2048]{1,0:T(8,128)(2,1)S(1)}, u32[]{:S(2)}, u32[]{:S(2)}) %collective-permute-start.31) | collective-permute-done | bytes 524320 | tf_op jit(solution)/shard_map/ppermute | solution.py:46
  311.2 24.6 %fusion.79 = f32[2048,2048]{0,1:T(8,128)} fusion(bf16[2048,2048]{1,0:T(8,128)(2,1)} %bitcast.67, bf16[2048,2048]{1,0:T(8,128)(2,1)} %all-gather.9.cloned.1.call-done), kind=kOutput, calls=%fused_computation.309 | convolution fusion | flops 17179869184 | bytes 33554432 | tf_op jit(solution)/shard_map/dot_general | solution.py:34
  335.7 22.6 %multiply_convert_fusion.1 = (bf16[2048,1024]{0,1:T(8,128)(2,1)}, bf16[2048,1024]{0,1:T(8,128)(2,1)}, bf16[2048,1024]{0,1:T(8,128)(2,1)}) fusion(f32[2048,2048]{0,1:T(8,128)} %fusion.79, bf16[2048,2048]{1,0:T(8,128)(2,1)} %bitcast.104, bf16[2048,1024]{1,0:T(8,128)(2,1)} %all-gather.11.cloned.1.call-done), kind=kOutput, calls=%fused_computation.12 | convolution fusion | flops 8621391872 | bytes 41943040 | tf_op jit(solution)/shard_map/dot_general | solution.py:34
  358.3 22.6 %convolution_convert_fusion.2 = bf16[2048,2048]{1,0:T(8,128)(2,1)S(1)} fusion(bf16[2048,2048]{1,0:T(8,128)(2,1)} %all-gather.9.cloned.1.call-done, bf16[2048,1024]{0,1:T(8,128)(2,1)} %get-tuple-element.12, bf16[2048,1024]{0,1:T(8,128)(2,1)} %get-tuple-element.11), kind=kOutput, calls=%fused_computation.18 | convolution fusion | flops 17200840704 | bytes 25165824 | tf_op jit(solution)/shard_map/dot_general | solution.py:38
  395.6 22.4 %collective-permute-done.53 = bf16[2,128,2048]{2,1,0:T(8,128)(2,1)S(1)} collective-permute-done((bf16[2,128,2048]{2,1,0:T(8,128)(2,1)S(1)}, bf16[2,128,2048]{2,1,0:T(8,128)(2,1)S(1)}, u32[]{:S(2)}, u32[]{:S(2)}) %collective-permute-start.53) | collective-permute-done | bytes 1048608 | tf_op jit(solution)/shard_map/ppermute | solution.py:46
  421.4 10.2 %collective-permute-done.54 = bf16[128,2048]{1,0:T(8,128)(2,1)S(1)} collective-permute-done((bf16[128,2048]{1,0:T(8,128)(2,1)S(1)}, bf16[128,2048]{1,0:T(8,128)(2,1)S(1)}, u32[]{:S(2)}, u32[]{:S(2)}) %collective-permute-start.54) | collective-permute-done | bytes 524320 | tf_op jit(solution)/shard_map/ppermute | solution.py:46
  438.4 13.0 %convolution_convert_fusion.5 = bf16[2048,1024]{1,0:T(8,128)(2,1)} fusion(bf16[2048,2048]{1,0:T(8,128)(2,1)} %bitcast.104, bf16[2048,1024]{0,1:T(8,128)(2,1)S(1)} %copy-done.58), kind=kOutput, calls=%fused_computation.29 | convolution fusion | flops 8592031744 | bytes 16777216 | tf_op jit(solution)/shard_map/dot_general | solution.py:42
  456.5 9.8 %collective-permute-done.67 = bf16[128,2048]{1,0:T(8,128)(2,1)S(1)} collective-permute-done((bf16[128,2048]{1,0:T(8,128)(2,1)S(1)}, bf16[128,2048]{1,0:T(8,128)(2,1)S(1)}, u32[]{:S(2)}, u32[]{:S(2)}) %collective-permute-start.67) | collective-permute-done | bytes 524320 | tf_op jit(solution)/shard_map/ppermute | solution.py:46
  467.7 9.9 %collective-permute-done.60 = bf16[128,2048]{1,0:T(8,128)(2,1)S(1)} collective-permute-done((bf16[128,2048]{1,0:T(8,128)(2,1)S(1)}, bf16[128,2048]{1,0:T(8,128)(2,1)S(1)}, u32[]{:S(2)}, u32[]{:S(2)}) %collective-permute-start.60) | collective-permute-done | bytes 524320 | tf_op jit(solution)/shard_map/ppermute | solution.py:46
  480.7 10.1 %collective-permute-done.69 = bf16[128,2048]{1,0:T(8,128)(2,1)S(1)} collective-permute-done((bf16[128,2048]{1,0:T(8,128)(2,1)S(1)}, bf16[128,2048]{1,0:T(8,128)(2,1)S(1)}, u32[]{:S(2)}, u32[]{:S(2)}) %collective-permute-start.69) | collective-permute-done | bytes 524320 | tf_op jit(solution)/shard_map/ppermute | solution.py:46
  539.6 11.3 %convolution_convert_fusion.6 = bf16[2048,768]{1,0:T(8,128)(2,1)} fusion(bf16[2048,2048]{1,0:T(8,128)(2,1)} %bitcast.602, bf16[2048,768]{0,1:T(8,128)(2,1)} %bitcast_dynamic-update-slice_fusion), kind=kOutput, calls=%fused_computation.30 | convolution fusion | flops 6444023808 | bytes 14680064 | tf_op jit(solution)/shard_map/dot_general | solution.py:42
  551.2 23.8 %convolution_convert_fusion = bf16[2048,2048]{1,0:T(8,128)(2,1)} fusion(bf16[2048,2048]{1,0:T(8,128)(2,1)} %bitcast.67, bf16[2048,1024]{0,1:T(8,128)(2,1)} %get-tuple-element.12, bf16[2048,1024]{0,1:T(8,128)(2,1)} %get-tuple-element.11), kind=kOutput, calls=%fused_computation.16 | convolution fusion | flops 17200840704 | bytes 25165824 | tf_op jit(solution)/shard_map/dot_general | solution.py:42
  575.0 12.1 %convolution_convert_fusion.3 = bf16[2048,2048]{1,0:T(8,128)(2,1)S(1)} fusion(bf16[2048,1024]{0,1:T(8,128)(2,1)} %get-tuple-element.13, bf16[2048,1024]{1,0:T(8,128)(2,1)} %all-gather.11.cloned.1.call-done), kind=kOutput, calls=%fused_computation.19 | convolution fusion | flops 8594128896 | bytes 16777216 | tf_op jit(solution)/shard_map/dot_general | solution.py:38
  588.2 9.8 %convolution_convert_fusion.1 = bf16[2048,2048]{1,0:T(8,128)(2,1)S(1)} fusion(bf16[2048,768]{0,1:T(8,128)(2,1)} %bitcast_dynamic-update-slice_fusion, bf16[2048,768]{1,0:T(8,128)(2,1)} %all-gather.5.cloned.1.call-done), kind=kOutput, calls=%fused_computation.17 | convolution fusion | flops 6446645248 | bytes 14680064 | tf_op jit(solution)/shard_map/dot_general | solution.py:38
  608.1 22.7 %collective-permute-done.34 = bf16[2,128,2048]{2,1,0:T(8,128)(2,1)S(1)} collective-permute-done((bf16[2,128,2048]{2,1,0:T(8,128)(2,1)S(1)}, bf16[2,128,2048]{2,1,0:T(8,128)(2,1)S(1)}, u32[]{:S(2)}, u32[]{:S(2)}) %collective-permute-start.34) | collective-permute-done | bytes 1048608 | tf_op jit(solution)/shard_map/ppermute | solution.py:46
  634.2 10.6 %collective-permute-done.35 = bf16[128,2048]{1,0:T(8,128)(2,1)S(1)} collective-permute-done((bf16[128,2048]{1,0:T(8,128)(2,1)S(1)}, bf16[128,2048]{1,0:T(8,128)(2,1)S(1)}, u32[]{:S(2)}, u32[]{:S(2)}) %collective-permute-start.35) | collective-permute-done | bytes 524320 | tf_op jit(solution)/shard_map/ppermute | solution.py:46
  667.1 19.4 %collective-permute-done.72 = bf16[2,128,2048]{2,1,0:T(8,128)(2,1)} collective-permute-done((bf16[2,128,2048]{2,1,0:T(8,128)(2,1)}, bf16[2,128,2048]{2,1,0:T(8,128)(2,1)}, u32[]{:S(2)}, u32[]{:S(2)}) %collective-permute-start.72) | collective-permute-done | bytes 1048608 | tf_op jit(solution)/shard_map/ppermute | solution.py:46
  694.7 8.6 %collective-permute-done.73 = bf16[128,2048]{1,0:T(8,128)(2,1)} collective-permute-done((bf16[128,2048]{1,0:T(8,128)(2,1)}, bf16[128,2048]{1,0:T(8,128)(2,1)}, u32[]{:S(2)}, u32[]{:S(2)}) %collective-permute-start.73) | collective-permute-done | bytes 524320 | tf_op jit(solution)/shard_map/ppermute | solution.py:46
  713.5 9.6 %all-to-all-done.4 = bf16[8,64,768]{2,1,0:T(8,128)(2,1)} async-done(((bf16[8,64,768]{2,1,0:T(8,128)(2,1)}), bf16[8,64,768]{2,1,0:T(8,128)(2,1)}, u32[]{:S(2)}, u32[]{:S(2)}) %all-to-all-start.4) | async-done | bytes 786464 | tf_op jit(solution)/shard_map/all_to_all | solution.py:247
  723.0 49.8 %reduce-scatter.9.cloned.1.call-done = bf16[512,2048]{1,0:T(8,128)(2,1)} async-done(((bf16[2048,2048]{1,0:T(8,128)(2,1)}), bf16[512,2048]{1,0:T(8,128)(2,1)}) %reduce-scatter.9.cloned.1.call-update) | async-done | bytes 2097168 | tf_op jit(solution)/shard_map/reduce_scatter | solution.py:246
  788.9 15.0 %all-to-all-done.6 = bf16[8,64,2048]{2,1,0:T(8,128)(2,1)} async-done(((bf16[8,64,2048]{2,1,0:T(8,128)(2,1)}), bf16[8,64,2048]{2,1,0:T(8,128)(2,1)}, u32[]{:S(2)}, u32[]{:S(2)}) %all-to-all-start.6) | async-done | bytes 2097184 | tf_op jit(solution)/shard_map/all_to_all | solution.py:247
  (488 shorter events, 325.4 us)
Async XLA Ops:
  7.2 133.5 %all-gather.7.cloned.1.call-start = ((), (), s32[]{:S(2)}) async-start(), calls=%async_computation.13 | async-start | bytes 1310720 | tf_op jit(solution)/shard_map/all_gather | solution.py:142
  17.8 136.4 %all-gather.5.cloned.1.call-start = ((), (), s32[]{:S(2)}) async-start(), calls=%async_computation.12 | async-start | bytes 3932160 | tf_op jit(solution)/shard_map/all_gather | solution.py:142
  20.1 169.8 %collective-permute-start.48 = (bf16[128,2048]{1,0:T(8,128)(2,1)}, bf16[128,2048]{1,0:T(8,128)(2,1)}, u32[]{:S(2)}, u32[]{:S(2)}) collective-permute-start(bf16[128,2048]{1,0:T(8,128)(2,1)} %get-tuple-element.47), channel_id=1, source_target_pairs={{0,4},{1,5},{2,6},{3,7},{4,0},{5,1},{6,2},{7,3},{8,12},{9,13},{10,... | collective-permute-start | bytes 1572872 | tf_op jit(solution)/shard_map/ppermute | solution.py:46
  22.1 178.3 %collective-permute-start.46 = (bf16[128,2048]{1,0:T(8,128)(2,1)}, bf16[128,2048]{1,0:T(8,128)(2,1)}, u32[]{:S(2)}, u32[]{:S(2)}) collective-permute-start(bf16[128,2048]{1,0:T(8,128)(2,1)} %get-tuple-element.47), channel_id=1, source_target_pairs={{0,2},{1,3},{2,0},{3,1},{4,6},{5,7},{6,4},{7,5},{8,10},{9,11},{10,... | collective-permute-start | bytes 1572872 | tf_op jit(solution)/shard_map/ppermute | solution.py:46
  36.6 31.5 %all-to-all-start.2 = ((bf16[8,64,2048]{2,1,0:T(8,128)(2,1)}), bf16[8,64,2048]{2,1,0:T(8,128)(2,1)}, u32[]{:S(2)}, u32[]{:S(2)}) async-start(bf16[8,64,2048]{2,1,0:T(8,128)(2,1)} %copy.191), calls=%async_computation.2 | async-start | bytes 4194304 | tf_op jit(solution)/shard_map/all_to_all | solution.py:85
  41.0 270.2 %all-gather.9.cloned.1.call-start = ((), (), s32[]{:S(2)}) async-start(), calls=%async_computation.14 | async-start | bytes 10485760 | tf_op jit(solution)/shard_map/all_gather | solution.py:142
  43.6 41.2 %collective-permute-start.3 = (bf16[128,2048]{1,0:T(8,128)(2,1)}, bf16[128,2048]{1,0:T(8,128)(2,1)}, u32[]{:S(2)}, u32[]{:S(2)}) collective-permute-start(bf16[128,2048]{1,0:T(8,128)(2,1)} %get-tuple-element.55), channel_id=1, source_target_pairs={{0,4},{1,5},{2,6},{3,7},{4,0},{5,1},{6,2},{7,3},{8,12},{9,13},{10,... | collective-permute-start | bytes 1572872 | tf_op jit(solution)/shard_map/ppermute | solution.py:46
  45.5 32.5 %collective-permute-start.1 = (bf16[128,2048]{1,0:T(8,128)(2,1)}, bf16[128,2048]{1,0:T(8,128)(2,1)}, u32[]{:S(2)}, u32[]{:S(2)}) collective-permute-start(bf16[128,2048]{1,0:T(8,128)(2,1)} %get-tuple-element.55), channel_id=1, source_target_pairs={{0,2},{1,3},{2,0},{3,1},{4,6},{5,7},{6,4},{7,5},{8,10},{9,11},{10,... | collective-permute-start | bytes 1572872 | tf_op jit(solution)/shard_map/ppermute | solution.py:46
  46.9 31.1 %collective-permute-start = (bf16[128,2048]{1,0:T(8,128)(2,1)}, bf16[128,2048]{1,0:T(8,128)(2,1)}, u32[]{:S(2)}, u32[]{:S(2)}) collective-permute-start(bf16[128,2048]{1,0:T(8,128)(2,1)} %get-tuple-element.55), channel_id=1, source_target_pairs={{0,1},{1,0},{2,3},{3,2},{4,5},{5,4},{6,7},{7,6},{8,9},{9,8},{10,11... | collective-permute-start | bytes 1572872 | tf_op jit(solution)/shard_map/ppermute | solution.py:46
  82.4 29.2 %collective-permute-start.10 = (bf16[128,2048]{1,0:T(8,128)(2,1)}, bf16[128,2048]{1,0:T(8,128)(2,1)S(1)}, u32[]{:S(2)}, u32[]{:S(2)}) collective-permute-start(bf16[128,2048]{1,0:T(8,128)(2,1)} %get-tuple-element.53), channel_id=1, source_target_pairs={{0,4},{1,5},{2,6},{3,7},{4,0},{5,1},{6,2},{7,3},{8,12},{9,13},{10,... | collective-permute-start | bytes 1572872 | tf_op jit(solution)/shard_map/ppermute | solution.py:46
  126.7 57.5 %collective-permute-start.41 = (bf16[128,2048]{1,0:T(8,128)(2,1)}, bf16[128,2048]{1,0:T(8,128)(2,1)}, u32[]{:S(2)}, u32[]{:S(2)}) collective-permute-start(bf16[128,2048]{1,0:T(8,128)(2,1)} %get-tuple-element.49), channel_id=1, source_target_pairs={{0,4},{1,5},{2,6},{3,7},{4,0},{5,1},{6,2},{7,3},{8,12},{9,13},{10,... | collective-permute-start | bytes 1572872 | tf_op jit(solution)/shard_map/ppermute | solution.py:46
  137.1 48.9 %collective-permute-start.40 = (bf16[128,2048]{1,0:T(8,128)(2,1)}, bf16[128,2048]{1,0:T(8,128)(2,1)}, u32[]{:S(2)}, u32[]{:S(2)}) collective-permute-start(bf16[128,2048]{1,0:T(8,128)(2,1)} %collective-permute-done.39), channel_id=1, source_target_pairs={{0,1},{1,0},{2,3},{3,2},{4,5},{5,4},{6,7},{7,6},{8,9},{9,8},{10,11... | collective-permute-start | bytes 1572872 | tf_op jit(solution)/shard_map/ppermute | solution.py:46
  147.3 36.3 %all-to-all-start.3 = ((bf16[8,64,1024]{2,1,0:T(8,128)(2,1)}), bf16[8,64,1024]{2,1,0:T(8,128)(2,1)}, u32[]{:S(2)}, u32[]{:S(2)}) async-start(bf16[8,64,1024]{2,1,0:T(8,128)(2,1)} %copy.192), calls=%async_computation.3 | async-start | bytes 2097152 | tf_op jit(solution)/shard_map/all_to_all | solution.py:85
  151.5 184.2 %all-gather.11.cloned.1.call-start = ((), (), s32[]{:S(2)}) async-start(), calls=%async_computation.15 | async-start | bytes 5242880 | tf_op jit(solution)/shard_map/all_gather | solution.py:142
  181.4 28.0 %collective-permute-start.14 = (bf16[2,4,128,2048]{3,2,1,0:T(8,128)(2,1)}, bf16[2,4,128,2048]{3,2,1,0:T(8,128)(2,1)}, u32[]{:S(2)}, u32[]{:S(2)}) collective-permute-start(bf16[2,4,128,2048]{3,2,1,0:T(8,128)(2,1)} %slice_bitcast_fusion.6), channel_id=1, source_target_pairs={{0,1},{1,0},{2,3},{3,2},{4,5},{5,4},{6,7},{7,6},{8,9},{9,8},{10,11... | collective-permute-start | bytes 12582920 | tf_op jit(solution)/shard_map/ppermute | solution.py:46
  183.7 462.3 %reduce-scatter.11.cloned.1.call-start = ((), (), s32[]{:S(2)}) async-start(), calls=%async_computation.19 | async-start | bytes 5242880 | tf_op jit(solution)/shard_map/reduce_scatter | solution.py:246
  200.3 43.4 %collective-permute-start.49 = (bf16[128,2048]{1,0:T(8,128)(2,1)}, bf16[128,2048]{1,0:T(8,128)(2,1)S(1)}, u32[]{:S(2)}, u32[]{:S(2)}) collective-permute-start(bf16[128,2048]{1,0:T(8,128)(2,1)} %collective-permute-done.48), channel_id=1, source_target_pairs={{0,1},{1,0},{2,3},{3,2},{4,5},{5,4},{6,7},{7,6},{8,9},{9,8},{10,11... | collective-permute-start | bytes 1572872 | tf_op jit(solution)/shard_map/ppermute | solution.py:46
  204.4 56.3 %collective-permute-start.51 = (bf16[128,2048]{1,0:T(8,128)(2,1)S(1)}, bf16[128,2048]{1,0:T(8,128)(2,1)S(1)}, u32[]{:S(2)}, u32[]{:S(2)}) collective-permute-start(bf16[128,2048]{1,0:T(8,128)(2,1)S(1)} %collective-permute-done.50), channel_id=1, source_target_pairs={{0,1},{1,0},{2,3},{3,2},{4,5},{5,4},{6,7},{7,6},{8,9},{9,8},{10,11... | collective-permute-start | bytes 1572872 | tf_op jit(solution)/shard_map/ppermute | solution.py:46
  262.5 28.8 %collective-permute-start.27 = (bf16[128,2048]{1,0:T(8,128)(2,1)S(1)}, bf16[128,2048]{1,0:T(8,128)(2,1)S(1)}, u32[]{:S(2)}, u32[]{:S(2)}) collective-permute-start(bf16[128,2048]{1,0:T(8,128)(2,1)S(1)} %get-tuple-element.50), channel_id=1, source_target_pairs={{0,2},{1,3},{2,0},{3,1},{4,6},{5,7},{6,4},{7,5},{8,10},{9,11},{10,... | collective-permute-start | bytes 1572872 | tf_op jit(solution)/shard_map/ppermute | solution.py:46
  263.1 42.1 %collective-permute-start.26 = (bf16[128,2048]{1,0:T(8,128)(2,1)S(1)}, bf16[128,2048]{1,0:T(8,128)(2,1)S(1)}, u32[]{:S(2)}, u32[]{:S(2)}) collective-permute-start(bf16[128,2048]{1,0:T(8,128)(2,1)S(1)} %get-tuple-element.50), channel_id=1, source_target_pairs={{0,1},{1,0},{2,3},{3,2},{4,5},{5,4},{6,7},{7,6},{8,9},{9,8},{10,11... | collective-permute-start | bytes 1572872 | tf_op jit(solution)/shard_map/ppermute | solution.py:46
  394.1 25.4 %collective-permute-start.55 = (bf16[2,128,2048]{2,1,0:T(8,128)(2,1)S(1)}, bf16[2,128,2048]{2,1,0:T(8,128)(2,1)S(1)}, u32[]{:S(2)}, u32[]{:S(2)}) collective-permute-start(bf16[2,128,2048]{2,1,0:T(8,128)(2,1)S(1)} %slice_bitcast_fusion.14), channel_id=1, source_target_pairs={{0,2},{1,3},{2,0},{3,1},{4,6},{5,7},{6,4},{7,5},{8,10},{9,11},{10,... | collective-permute-start | bytes 3145736 | tf_op jit(solution)/shard_map/ppermute | solution.py:46
  452.9 27.3 %collective-permute-start.65 = (bf16[128,2048]{1,0:T(8,128)(2,1)S(1)}, bf16[128,2048]{1,0:T(8,128)(2,1)S(1)}, u32[]{:S(2)}, u32[]{:S(2)}) collective-permute-start(bf16[128,2048]{1,0:T(8,128)(2,1)S(1)} %get-tuple-element.44), channel_id=1, source_target_pairs={{0,2},{1,3},{2,0},{3,1},{4,6},{5,7},{6,4},{7,5},{8,10},{9,11},{10,... | collective-permute-start | bytes 1572872 | tf_op jit(solution)/shard_map/ppermute | solution.py:46
  454.0 41.9 %collective-permute-start.64 = (bf16[128,2048]{1,0:T(8,128)(2,1)S(1)}, bf16[128,2048]{1,0:T(8,128)(2,1)S(1)}, u32[]{:S(2)}, u32[]{:S(2)}) collective-permute-start(bf16[128,2048]{1,0:T(8,128)(2,1)S(1)} %get-tuple-element.44), channel_id=1, source_target_pairs={{0,1},{1,0},{2,3},{3,2},{4,5},{5,4},{6,7},{7,6},{8,9},{9,8},{10,11... | collective-permute-start | bytes 1572872 | tf_op jit(solution)/shard_map/ppermute | solution.py:46
  529.5 163.4 %reduce-scatter.7.cloned.1.call-start = ((), (), s32[]{:S(2)}) async-start(), calls=%async_computation.17 | async-start | bytes 1310720 | tf_op jit(solution)/shard_map/reduce_scatter | solution.py:254
  537.1 169.0 %reduce-scatter.5.cloned.1.call-start = ((), (), s32[]{:S(2)}) async-start(), calls=%async_computation.16 | async-start | bytes 3932160 | tf_op jit(solution)/shard_map/reduce_scatter | solution.py:246
  551.0 221.9 %reduce-scatter.9.cloned.1.call-start = ((), (), s32[]{:S(2)}) async-start(), calls=%async_computation.18 | async-start | bytes 10485760 | tf_op jit(solution)/shard_map/reduce_scatter | solution.py:246
  602.7 46.8 %collective-permute-start.71 = (bf16[2,4,128,2048]{3,2,1,0:T(8,128)(2,1)}, bf16[2,4,128,2048]{3,2,1,0:T(8,128)(2,1)}, u32[]{:S(2)}, u32[]{:S(2)}) collective-permute-start(bf16[2,4,128,2048]{3,2,1,0:T(8,128)(2,1)} %slice_bitcast_fusion), channel_id=1, source_target_pairs={{0,1},{1,0},{2,3},{3,2},{4,5},{5,4},{6,7},{7,6},{8,9},{9,8},{10,11... | collective-permute-start | bytes 12582920 | tf_op jit(solution)/shard_map/ppermute | solution.py:46
  605.2 25.6 %collective-permute-start.34 = (bf16[2,128,2048]{2,1,0:T(8,128)(2,1)S(1)}, bf16[2,128,2048]{2,1,0:T(8,128)(2,1)S(1)}, u32[]{:S(2)}, u32[]{:S(2)}) collective-permute-start(bf16[2,128,2048]{2,1,0:T(8,128)(2,1)S(1)} %slice_bitcast_fusion.20), channel_id=1, source_target_pairs={{0,4},{1,5},{2,6},{3,7},{4,0},{5,1},{6,2},{7,3},{8,12},{9,13},{10,... | collective-permute-start | bytes 3145736 | tf_op jit(solution)/shard_map/ppermute | solution.py:46
  632.7 25.3 %collective-permute-start.37 = (bf16[128,2048]{1,0:T(8,128)(2,1)S(1)}, bf16[128,2048]{1,0:T(8,128)(2,1)S(1)}, u32[]{:S(2)}, u32[]{:S(2)}) collective-permute-start(bf16[128,2048]{1,0:T(8,128)(2,1)S(1)} %slice_bitcast_fusion.34), channel_id=1, source_target_pairs={{0,4},{1,5},{2,6},{3,7},{4,0},{5,1},{6,2},{7,3},{8,12},{9,13},{10,... | collective-permute-start | bytes 1572872 | tf_op jit(solution)/shard_map/ppermute | solution.py:46
  656.1 30.4 %collective-permute-start.72 = (bf16[2,128,2048]{2,1,0:T(8,128)(2,1)}, bf16[2,128,2048]{2,1,0:T(8,128)(2,1)}, u32[]{:S(2)}, u32[]{:S(2)}) collective-permute-start(bf16[2,128,2048]{2,1,0:T(8,128)(2,1)} %slice_bitcast_fusion.12), channel_id=1, source_target_pairs={{0,4},{1,5},{2,6},{3,7},{4,0},{5,1},{6,2},{7,3},{8,12},{9,13},{10,... | collective-permute-start | bytes 3145736 | tf_op jit(solution)/shard_map/ppermute | solution.py:46
  660.5 30.3 %collective-permute-start.74 = (bf16[2,128,2048]{2,1,0:T(8,128)(2,1)}, bf16[2,128,2048]{2,1,0:T(8,128)(2,1)}, u32[]{:S(2)}, u32[]{:S(2)}) collective-permute-start(bf16[2,128,2048]{2,1,0:T(8,128)(2,1)} %slice_bitcast_fusion.10), channel_id=1, source_target_pairs={{0,2},{1,3},{2,0},{3,1},{4,6},{5,7},{6,4},{7,5},{8,10},{9,11},{10,... | collective-permute-start | bytes 3145736 | tf_op jit(solution)/shard_map/ppermute | solution.py:46
  772.9 31.0 %all-to-all-start.6 = ((bf16[8,64,2048]{2,1,0:T(8,128)(2,1)}), bf16[8,64,2048]{2,1,0:T(8,128)(2,1)}, u32[]{:S(2)}, u32[]{:S(2)}) async-start(bf16[8,64,2048]{2,1,0:T(8,128)(2,1)} %bitcast.589), calls=%async_computation.9 | async-start | bytes 4194304 | tf_op jit(solution)/shard_map/all_to_all | solution.py:247
  (118 other events, 1893.5 us)
Sparse Core Ops, SparseCore 0:
  9.6 30.6 all-gather.6
  41.8 62.9 all-gather.4
  106.4 148.2 all-gather.8
  256.2 78.9 all-gather.10
  451.6 77.2 reduce-scatter.10
  537.2 27.4 reduce-scatter.6
  567.0 58.8 reduce-scatter.4
  628.3 144.4 reduce-scatter.8

commit v2 on v1

v2 whole, which is shorter than its diff:
```python
import math

import jax
import jax.numpy as jnp
from jax import lax
from jax.experimental import pallas as pl
from jax.experimental.pallas import tpu as pltpu
from jax.sharding import PartitionSpec as P

H = 16
HD = 128
EPSILON = 1e-05
F32 = jnp.float32
BF16 = jnp.bfloat16
BOTH = ("dp", "fsdp")
CORE, X, Y = 1, 2, 4
ROWS = 512
SHRINK = 50
VMEM_BYTES = 60 * 1024 * 1024


def rope_tables(length_cap, repeats):
    halfway = HD // 2
    position = jnp.arange(length_cap, dtype=F32)
    inverse = 10000.0 ** (-2.0 * jnp.arange(halfway, dtype=F32) / HD)
    angles = position[:, None] * inverse[None, :]
    cosine, sine = jnp.cos(angles), jnp.sin(angles)
    cosine = jnp.concatenate([cosine, cosine], axis=1)
    sine = jnp.concatenate([-sine, sine], axis=1)
    return jnp.tile(cosine, (repeats, 1)), jnp.tile(sine, (repeats, 1))


def dot_nn(left, right):
    return lax.dot_general(left, right, (((1,), (0,)), ((), ())), preferred_element_type=F32)


def dot_nt(left, right):
    return lax.dot_general(left, right, (((1,), (1,)), ((), ())), preferred_element_type=F32)


def dot_tn(left, right):
    return lax.dot_general(left, right, (((0,), (0,)), ((), ())), preferred_element_type=F32)


def whole_spec(array):
    return pl.BlockSpec(array.shape, lambda i, *_: (0,) * array.ndim, pipeline_mode=pl.Buffered(1))


def part_specs(count, steps, columns):
    def spec(k):
        return pl.BlockSpec(
            (ROWS, columns), lambda i, *_: (jnp.clip(i - k * steps, 0, steps - 1), 0)
        )

    return [spec(k) for k in range(count)]


def row_spec(columns):
    return pl.BlockSpec((ROWS, columns), lambda i, *_: (i, 0))


def by_part(count, steps, work):
    if count == 1:
        work(0)
        return
    for k in range(count):
        pl.when(pl.program_id(0) // steps == k)(lambda k=k: work(k))


def tiles(extent, size):
    size = min(size, extent)
    return [slice(at, at + size) for at in range(0, extent, size)]


def call(body, name, parts, rows, whole, scalars, part_outs, row_outs, flops, scratch=(), shrink=SHRINK):
    count = len(parts)
    steps = parts[0].shape[0] // ROWS if parts else rows[0].shape[0] // ROWS
    cuts = count if parts else 1
    total = steps * max(cuts, 1)
    out_shape, out_specs = [], []
    for columns, dtype, pieces in part_outs:
        per = total // pieces
        out_shape += [jax.ShapeDtypeStruct((per * ROWS, columns), dtype)] * pieces
        out_specs += part_specs(pieces, per, columns)
    for columns, dtype in row_outs:
        out_shape.append(jax.ShapeDtypeStruct((total * ROWS, columns), dtype))
        out_specs.append(row_spec(columns))
    in_specs = part_specs(count, steps, parts[0].shape[1]) if parts else []
    in_specs += [row_spec(r.shape[1]) for r in rows] + [whole_spec(w) for w in whole]
    moved = sum(a.size * a.dtype.itemsize for a in list(parts) + list(rows) + list(whole))
    moved += sum(math.prod(o.shape) * jnp.dtype(o.dtype).itemsize for o in out_shape)
    return pl.pallas_call(
        body,
        out_shape=out_shape,
        grid_spec=pltpu.PrefetchScalarGridSpec(
            num_scalar_prefetch=len(scalars), grid=(total,), in_specs=in_specs, out_specs=out_specs,
            scratch_shapes=list(scratch),
        ),
        compiler_params=pltpu.CompilerParams(
            dimension_semantics=("arbitrary",), vmem_limit_bytes=VMEM_BYTES
        ),
        cost_estimate=pl.CostEstimate(flops=flops // shrink, bytes_accessed=moved // shrink, transcendentals=0),
        name=name,
    )(*scalars, *parts, *rows, *whole)


def turn(value, cosine, sine):
    return value * cosine + pltpu.roll(value, HD // 2, 1) * sine


def allowed_of(live, cap):
    row = lax.broadcasted_iota(jnp.int32, (cap, cap), 0)
    column = lax.broadcasted_iota(jnp.int32, (cap, cap), 1)
    return (row >= column) & (column < live)


def attention_forward(parts, live, wqkv, wo, cosine, sine, cap):
    count, cols, width = len(parts), wo.shape[0], wo.shape[1]
    steps = parts[0].shape[0] // ROWS
    scale, shift = 1.0 / math.sqrt(HD), -math.log(cap)

    def body(live_ref, *refs):
        sources, refs = refs[:count], refs[count:]
        wqkv_ref, wo_ref, cos_ref, sin_ref = refs[:4]
        outs, (qkv_ref, mixed_ref) = refs[4 : 4 + count], refs[4 + count :]
        step = pl.program_id(0)

        def project(part):
            rows = sources[part][...]
            for kind in range(3):
                value = dot_nn(rows, wqkv_ref[:, kind * cols : (kind + 1) * cols])
                for head in tiles(cols, HD):
                    one = value[:, head]
                    if kind < 2:
                        one = turn(one, cos_ref[...], sin_ref[...])
                    at = slice(kind * cols + head.start, kind * cols + head.stop)
                    qkv_ref[:, at] = one.astype(BF16)

        by_part(count, steps, project)
        for k, sequence in enumerate(tiles(ROWS, cap)):
            allowed = allowed_of(live_ref[step * (ROWS // cap) + k], cap)
            for head in tiles(cols, HD):
                query = qkv_ref[sequence, head]
                key = qkv_ref[sequence, cols + head.start : cols + head.stop]
                value = qkv_ref[sequence, 2 * cols + head.start : 2 * cols + head.stop]
                gates = jax.nn.sigmoid(dot_nt(query, key) * scale + shift)
                probs = jnp.where(allowed, gates, 0.0).astype(BF16)
                mixed_ref[sequence, head] = dot_nn(probs, value).astype(BF16)

        def finish(part):
            outs[part][...] = dot_nn(mixed_ref[...], wo_ref[...]).astype(BF16)

        by_part(count, steps, finish)

    total = count * steps * ROWS
    out = call(
        body,
        "attention_forward",
        parts,
        [],
        [wqkv, wo, cosine, sine],
        [live],
        [(width, BF16, count)],
        [(3 * cols, BF16), (cols, BF16)],
        2 * total * width * 4 * cols,
    )
    return out[:count], out[count], out[count + 1]


def attention_backward(parts, live, qkv, wqkv, wo, cosine, sine, cap):
    count, cols, width = len(parts), wo.shape[0], wo.shape[1]
    steps = parts[0].shape[0] // ROWS
    scale, shift = 1.0 / math.sqrt(HD), -math.log(cap)

    def body(live_ref, *refs):
        sources, refs = refs[:count], refs[count:]
        qkv_ref, wqkv_ref, wo_ref, cos_ref, sin_ref = refs[:5]
        outs, (back_ref, mixed_ref) = refs[5 : 5 + count], refs[5 + count :]
        step = pl.program_id(0)

        def enter(part):
            mixed_ref[...] = dot_nt(sources[part][...], wo_ref[...]).astype(BF16)

        by_part(count, steps, enter)
        for k, sequence in enumerate(tiles(ROWS, cap)):
            allowed = allowed_of(live_ref[step * (ROWS // cap) + k], cap)
            cosine_here, sine_here = cos_ref[sequence, :], sin_ref[sequence, :]
            for head in tiles(cols, HD):
                key_at = slice(cols + head.start, cols + head.stop)
                value_at = slice(2 * cols + head.start, 2 * cols + head.stop)
                query, key, value = (
                    qkv_ref[sequence, at] for at in (head, key_at, value_at)
                )
                grad = mixed_ref[sequence, head]
                gates = jax.nn.sigmoid(dot_nt(query, key) * scale + shift)
                probs = jnp.where(allowed, gates, 0.0).astype(BF16)
                grad_logits = dot_nt(grad, value) * gates * (1.0 - gates)
                grad_logits = jnp.where(allowed, grad_logits, 0.0).astype(BF16)
                grad_query = dot_nn(grad_logits, key) * scale
                grad_key = dot_tn(grad_logits, query) * scale
                back_ref[sequence, head] = turn(grad_query, cosine_here, -sine_here).astype(BF16)
                back_ref[sequence, key_at] = turn(grad_key, cosine_here, -sine_here).astype(BF16)
                back_ref[sequence, value_at] = dot_tn(probs, grad).astype(BF16)

        def finish(part):
            outs[part][...] = dot_nt(back_ref[...], wqkv_ref[...]).astype(BF16)

        by_part(count, steps, finish)

    total = count * steps * ROWS
    out = call(
        body,
        "attention_backward",
        parts,
        [qkv],
        [wqkv, wo, cosine, sine],
        [live],
        [(width, BF16, count)],
        [(3 * cols, BF16)],
        2 * total * width * 4 * cols,
        [pltpu.VMEM((ROWS, cols), BF16)],
        1,
    )
    return out[:count], out[count]


def feed_forward(parts, wgu):
    count, width = len(parts), wgu.shape[0]
    share = wgu.shape[1] // 2
    steps = parts[0].shape[0] // ROWS

    def body(*refs):
        sources, (wgu_ref, gate_ref, up_ref, active_ref) = refs[:count], refs[count:]

        def work(part):
            rows = sources[part][...]
            for at in tiles(share, 256):
                gate = dot_nn(rows, wgu_ref[:, at])
                up = dot_nn(rows, wgu_ref[:, share + at.start : share + at.stop])
                gate_ref[:, at] = gate
                up_ref[:, at] = up
                active_ref[:, at] = (gate * jax.nn.sigmoid(gate) * up).astype(BF16)

        by_part(count, steps, work)

    total = count * steps * ROWS
    return call(
        body,
        "feed_forward",
        parts,
        [],
        [wgu],
        [],
        [],
        [(share, F32), (share, F32), (share, BF16)],
        4 * total * width * share,
    )


def feed_back(parts, gate, up, wd, wgu):
    count, width = len(parts), wgu.shape[0]
    share = wgu.shape[1] // 2
    steps = parts[0].shape[0] // ROWS

    def body(*refs):
        sources, refs = refs[:count], refs[count:]
        gate_ref, up_ref, wd_ref, wgu_ref = refs[:4]
        outs, (grad_ref,) = refs[4 : 4 + count], refs[4 + count :]

        def work(part):
            rows = sources[part][...]
            for at in tiles(share, 256):
                grad = dot_nn(rows, wd_ref[:, at])
                gate = gate_ref[:, at]
                open_gate = jax.nn.sigmoid(gate)
                grad_gate = grad * up_ref[:, at] * (open_gate * (1.0 + gate * (1.0 - open_gate)))
                grad_ref[:, at] = grad_gate.astype(BF16)
                grad_up = grad * (gate * open_gate)
                grad_ref[:, share + at.start : share + at.stop] = grad_up.astype(BF16)
            grads = grad_ref[...]
            for at in tiles(width, 512):
                outs[part][:, at] = dot_nt(grads, wgu_ref[at, :]).astype(BF16)

        by_part(count, steps, work)

    total = count * steps * ROWS
    out = call(
        body,
        "feed_back",
        parts,
        [gate, up],
        [wd, wgu],
        [],
        [(width, BF16, count)],
        [(2 * share, BF16)],
        6 * total * width * share,
    )
    return out[:count], out[count]


def feed_down(active, wd, pieces):
    width = wd.shape[0]
    steps = active.shape[0] // ROWS // pieces

    def body(active_ref, wd_ref, *outs):
        def work(part):
            rows = active_ref[...]
            for at in tiles(width, 512):
                outs[part][:, at] = dot_nt(rows, wd_ref[at, :]).astype(BF16)

        by_part(pieces, steps, work)

    return call(
        body,
        "feed_down",
        [],
        [active],
        [wd],
        [],
        [(width, BF16, pieces)],
        [],
        2 * active.size * width,
        shrink=1,
    )


def outer(lefts, rights, block, shrink=SHRINK):
    parts = max(len(lefts), len(rights))
    rows = lefts[0].shape[0] * len(lefts) // parts
    height, width = lefts[0].shape[1], rights[0].shape[1]
    nleft = len(lefts)

    def body(*refs):
        def pieces(group):
            if len(group) == parts:
                return [ref[...] for ref in group]
            return [group[0][k * rows : (k + 1) * rows, :] for k in range(parts)]

        left, right = pieces(refs[:nleft]), pieces(refs[nleft:-1])
        total = dot_tn(left[0], right[0])
        for one, other in zip(left[1:], right[1:], strict=True):
            total += dot_tn(one, other)
        refs[-1][...] = total.astype(BF16)

    return pl.pallas_call(
        body,
        out_shape=jax.ShapeDtypeStruct((height, width), BF16),
        grid=(height // block,),
        in_specs=[pl.BlockSpec((a.shape[0], block), lambda i: (0, i)) for a in lefts]
        + [whole_spec(b) for b in rights],
        out_specs=pl.BlockSpec((block, width), lambda i: (i, 0)),
        compiler_params=pltpu.CompilerParams(
            dimension_semantics=("arbitrary",), vmem_limit_bytes=VMEM_BYTES
        ),
        cost_estimate=pl.CostEstimate(
            flops=2 * parts * rows * height * width // shrink,
            bytes_accessed=2 * (parts * rows * (height + width) + height * width) // shrink,
            transcendentals=0,
        ),
        name="outer",
    )(*lefts, *rights)


def finish(pieces, weights, gain, moves):
    count, rows = len(weights), gain.shape[0]

    def body(*refs):
        pieces_ref, gain_ref, weight_refs = refs[0], refs[1], refs[2 : 2 + count]
        outs, total_ref = refs[2 + count : -1], refs[-1]
        scale = gain_ref[...]
        total = jnp.zeros((rows, HD), F32)
        for sender, source, which, target in moves:
            value = pieces_ref[sender, :, source].astype(F32)
            outs[which][:, target] = value * scale
            product = value * weight_refs[which][:, target].astype(F32)
            for at in tiles(product.shape[1], HD):
                total += product[:, at]
        total_ref[...] = jnp.broadcast_to(jnp.sum(total, axis=1, keepdims=True), (rows, HD))

    out = pl.pallas_call(
        body,
        out_shape=[jax.ShapeDtypeStruct(w.shape, F32) for w in weights]
        + [jax.ShapeDtypeStruct((rows, HD), F32)],
        cost_estimate=pl.CostEstimate(
            flops=pieces.size // SHRINK, bytes_accessed=pieces.size // SHRINK, transcendentals=0
        ),
        compiler_params=pltpu.CompilerParams(vmem_limit_bytes=VMEM_BYTES),
        name="finish",
    )(pieces, gain, *weights)
    return out[:-1], out[-1][:, 0]


def after(value, *earlier):
    return lax.optimization_barrier((value,) + earlier)[0]


def swap(value, mask):
    count = lax.axis_size("dp") * lax.axis_size("fsdp")
    return lax.ppermute(value, BOTH, [(i, i ^ mask) for i in range(count)])


def add_low(left, right):
    return (left.astype(F32) + right.astype(F32)).astype(BF16)


def is_paired():
    return lax.axis_size("dp") == 4 and lax.axis_size("fsdp") == 8


def order_of(first, second):
    return ((0, first, second, first | second), (0, second, first, first | second))


def gather_group(rows, first, second, *meanwhile):
    if not is_paired():
        whole = lax.all_gather(rows, "fsdp", axis=1)
        return [whole.reshape(-1, rows.shape[-1])]
    a, b = rows[0], rows[1]
    a1, b2 = swap(a, first), swap(b, second)
    a2, b1 = swap(a, second), swap(b, first)
    a3, b3 = swap(a1, second), swap(b2, first)
    own = jnp.concatenate([a, a1, a2, a3, b, b2, b1, b3], axis=0)
    return [own, swap(after(own, *meanwhile) if meanwhile else own, CORE)]


def scatter_group(parts, first, second, like, fill=None):
    if not is_paired():
        micro, length, width = like.shape
        blocks = parts[0].reshape(micro, -1, length, width)
        if fill is not None:
            fill(lambda value: value)
        return lax.psum_scatter(blocks, "fsdp", scatter_dimension=1).astype(F32)
    keep, send = (part.reshape((2, 4) + like.shape[1:]) for part in parts)
    got = swap(send, CORE)
    a, a_far = add_low(keep[0, :2], got[0, :2]), add_low(keep[0, 2:], got[0, 2:])
    b, b_far = add_low(keep[1, :2], got[1, :2]), add_low(keep[1, 2:], got[1, 2:])
    if fill is not None:
        fill(lambda value: after(value, a_far, b_far))
    a_got, b_got = swap(a_far, second), swap(b_far, first)
    a, a_far = add_low(a[0], a_got[0]), add_low(a[1], a_got[1])
    b, b_far = add_low(b[0], b_got[0]), add_low(b[1], b_got[1])
    a_got, b_got = swap(a_far, first), swap(b_far, second)
    return jnp.stack([a.astype(F32) + a_got.astype(F32), b.astype(F32) + b_got.astype(F32)])


def per_device(
    tokens,
    lengths,
    order,
    w_query,
    w_key,
    w_value,
    w_output,
    w_gate,
    w_up,
    w_down,
    gain_attn,
    gain_ffn,
    cotangent,
):
    groups, members = lax.axis_size("dp"), lax.axis_size("fsdp")
    plane, member = lax.axis_index("dp"), lax.axis_index("fsdp")
    paired = is_paired()
    micro, _, cap, width = tokens.shape
    own_rows = w_query.shape[0]
    hidden = w_gate.shape[1]
    share = hidden // members
    sharers = HD // own_rows
    kinds = members // sharers
    my_heads = groups // sharers
    head_cols = my_heads * HD

    slots = jnp.arange(order.shape[1], dtype=jnp.int32)
    me = plane * members + member
    position = jnp.arange(cap, dtype=jnp.int32)

    if paired:
        block = jnp.array(
            [mask | core for core in (0, CORE) for masks in order_of(X, Y) for mask in masks]
        )
        devices = (me ^ block).reshape(2, 2, 4)
    else:
        devices = jnp.broadcast_to(plane * members + jnp.arange(members), (1, micro, members))
    placed = jnp.sum(
        jnp.where(devices[..., None] == slots, order[None, :, None, :], 0), axis=-1
    )
    lives = jnp.sum(
        jnp.where(placed[..., None] == slots, lengths[None, :, None, :], 0), axis=-1
    ).reshape(-1)

    my_slot = jnp.sum(jnp.where(slots == me, order, 0), axis=-1)
    my_live = jnp.sum(jnp.where(slots == my_slot[:, None], lengths, 0), axis=-1)
    my_mask = (position < my_live[:, None]).astype(F32)[:, :, None]

    gain_one = gain_attn.astype(F32)[:, None]
    gain_two = gain_ffn.astype(F32)[:, None]

    def scaled(weight, gain):
        return (weight.astype(F32) * gain).astype(BF16)

    def by_head(weight):
        cut = weight.reshape(own_rows, sharers, my_heads, kinds, HD)
        return cut.transpose(3, 1, 0, 2, 4).reshape(members, own_rows, head_cols)

    def by_unit(weight):
        return weight.reshape(own_rows, members, share).transpose(1, 0, 2)

    def planes(value):
        return lax.all_gather(value, "dp", axis=0, tiled=True)

    def over_planes(value):
        return lax.psum_scatter(value, "dp", scatter_dimension=0, tiled=True)

    def spread(pieces):
        count, rows, columns = pieces.shape
        flat = pieces.reshape(count * rows, columns)
        return lax.all_to_all(flat, "fsdp", 0, 0, tiled=True)

    cut_qkv = jnp.concatenate(
        [by_head(scaled(w, gain_one)) for w in (w_query, w_key, w_value)], axis=2
    )
    cut_gu = jnp.concatenate([by_unit(scaled(w, gain_two)) for w in (w_gate, w_up)], axis=2)
    cut_d = by_unit(w_down)
    near_qkv = spread(cut_qkv)
    wqkv = planes(near_qkv)
    raw = planes(w_output).reshape(sharers, my_heads, own_rows, width)
    subgroups = [[s * sharers + i for i in range(sharers)] for s in range(kinds)]

    def exchange(value):
        if not paired:
            return lax.all_to_all(value, "fsdp", 0, 0, axis_index_groups=subgroups)
        odd = (member & CORE) != 0
        mine, send = jnp.where(odd, value[1], value[0]), jnp.where(odd, value[0], value[1])
        got = swap(send, CORE)
        return jnp.stack([jnp.where(odd, got, mine), jnp.where(odd, mine, got)])

    wo = exchange(raw).transpose(1, 0, 2, 3).reshape(head_cols, width)

    x = after(tokens, near_qkv)[:, 0].astype(F32)
    inverse_one = lax.rsqrt(jnp.mean(x * x, axis=-1, keepdims=True) + EPSILON)
    normal_one = x * inverse_one
    n1 = gather_group(normal_one.astype(BF16), X, Y)
    near_gu = spread(after(cut_gu, near_qkv))
    upstream = cotangent[:, 0].astype(F32) * my_mask
    returned_grad = gather_group(after(upstream.astype(BF16), n1[0], near_gu), X, Y)
    near_d = spread(after(cut_d, returned_grad[0]))
    wgu, wd = planes(near_gu), planes(near_d)
    n1[0] = after(n1[0], near_gu)

    cosine, sine = rope_tables(cap, ROWS // cap)
    parts, qkv, mixed = attention_forward(n1, lives, wqkv, wo, cosine, sine, cap)
    parts = [*parts[:-1], after(parts[-1], *returned_grad)]
    attended = scatter_group(parts, X, Y, x)
    hidden_one = x + attended

    inverse_two = lax.rsqrt(jnp.mean(hidden_one * hidden_one, axis=-1, keepdims=True) + EPSILON)
    normal_two = hidden_one * inverse_two
    n2 = gather_group(normal_two.astype(BF16), X, Y, wgu)
    gate, up, activated = feed_forward(n2, wgu)

    part_d = outer(returned_grad, [activated], ROWS)
    returned_grad = list(lax.optimization_barrier((*returned_grad, part_d))[:-1])
    sum_d = over_planes(part_d)
    parts, grad_gu = feed_back(returned_grad, gate, up, wd, wgu)
    travelling = {}

    def fill(tie):
        travelling["gu"] = outer([tie(n2[0]), *n2[1:]], [grad_gu], ROWS, 1)

    back_two = after(scatter_group(parts, X, Y, x, fill), travelling["gu"], sum_d)
    sum_gu = over_planes(travelling["gu"])
    grad_hidden = upstream + inverse_two * (
        back_two - normal_two * jnp.mean(back_two * normal_two, axis=-1, keepdims=True)
    )
    grad_low = grad_hidden.astype(BF16)
    def home(mine):
        return lax.all_to_all(mine, "fsdp", 0, 0, tiled=True).reshape(members, own_rows, -1)

    grad_attended = gather_group(grad_low, X, Y)
    part_o = outer([mixed], grad_attended, HD)
    ties = []
    parts = feed_down(after(activated, grad_low), wd, len(n2))
    returned = scatter_group(parts, X, Y, x, ties.append)
    grad_attended = [ties[0](after(grad_attended[0], part_o)), *grad_attended[1:]]
    parts, grad_qkv = attention_backward(grad_attended, lives, qkv, wqkv, wo, cosine, sine, cap)
    part_o = exchange(part_o.reshape(my_heads, sharers, own_rows, width).transpose(1, 0, 2, 3))
    part_qkv = outer(n1, [grad_qkv], ROWS, 1)
    grad_wo = over_planes(after(part_o.reshape(groups * own_rows, width), sum_gu, part_qkv))
    sum_qkv = over_planes(after(part_qkv, sum_gu))
    sum_d, returned = lax.optimization_barrier((sum_d, returned))
    output = ((hidden_one + returned) * my_mask).astype(BF16)
    sum_dgu = home(jnp.concatenate([sum_d, after(sum_gu, part_qkv)], axis=1))
    back_one = scatter_group(parts, X, Y, x)
    back_one, sum_dgu = lax.optimization_barrier((back_one, sum_dgu))
    sum_d, sum_gu = sum_dgu[:, :, :share], sum_dgu[:, :, share:]
    grad_tokens = (
        grad_hidden
        + inverse_one
        * (back_one - normal_one * jnp.mean(back_one * normal_one, axis=-1, keepdims=True))
    ).astype(BF16)

    sum_qkv = home(after(sum_qkv, sum_dgu))

    def from_units(value):
        return value.transpose(1, 0, 2).reshape(own_rows, hidden).astype(F32)

    moves_qkv = [
        (
            p * sharers + c,
            slice(kind * head_cols + m * HD, kind * head_cols + (m + 1) * HD),
            kind,
            slice(((c * my_heads + m) * kinds + p) * HD, ((c * my_heads + m) * kinds + p + 1) * HD),
        )
        for kind in range(3)
        for p in range(kinds)
        for c in range(sharers)
        for m in range(my_heads)
    ]
    grad_qkv, grad_gain_one = finish(sum_qkv, (w_query, w_key, w_value), gain_one, moves_qkv)
    raw_gu = [from_units(sum_gu[:, :, i * share : (i + 1) * share]) for i in range(2)]
    grad_gain_two = sum(
        jnp.sum(g * w.astype(F32), axis=1) for g, w in zip(raw_gu, (w_gate, w_up), strict=True)
    )
    return (
        output[:, None],
        grad_tokens[:, None],
        *grad_qkv,
        grad_wo.astype(F32),
        raw_gu[0] * gain_two,
        raw_gu[1] * gain_two,
        from_units(sum_d),
        grad_gain_one,
        grad_gain_two,
    )


def solution(mesh):
    sequences = P(None, BOTH, None, None)
    rows = P(BOTH, None)
    in_specs = (sequences, P(), P()) + (rows,) * 7 + (P(BOTH), P(BOTH), sequences)
    out_specs = (sequences, sequences) + (rows,) * 7 + (P(BOTH), P(BOTH))
    return jax.shard_map(
        per_device, mesh=mesh, in_specs=in_specs, out_specs=out_specs, check_vma=False
    )
```

time: 827 us -> 752 us (0.909)
  Pallas kernels: 0 us -> 187 us
  matrix products: 172 us -> 0 us
  local copies, waits for them, and re-layouts: 119 us -> 57.9 us
  waiting for transfers between devices: 353 us -> 339 us
  starting transfers between devices: 88.3 us -> 74.4 us
  other arithmetic: 62.8 us -> 73.3 us
    pallas_call x0 -> x10, Pallas kernels: none -> 187 us  [the longest x5 129 us: call(): pl.pallas_call(body, out_shape=out_shape, grid_spec=pltpu.PrefetchScalarG...]
    dot_general x18 -> x0, matrix products: 172 us -> none  [the longest x4 59.7 us: dot_nn(): lax.dot_general(left, right, (((1,), (0,)), ((), ())), preferred_element_...]
    reduce_scatter x4, waiting for transfers between devices: 49.8 us -> 0.03 us  [over_planes(): return lax.psum_scatter(value, 'dp', scatter_dimension=0, tiled=True)]
    all_gather x4, waiting for transfers between devices: 0.01 us -> 47.7 us  [planes(): return lax.all_gather(value, 'dp', axis=0, tiled=True)]
    unnamed x179 -> x94, local copies, waits for them, and re-layouts: 70.4 us -> 40.9 us
    ppermute x76 -> x50, waiting for transfers between devices: 250 us -> 272 us  [swap(): return lax.ppermute(value, BOTH, [(i, i ^ mask) for i in range(count)])]
    all_to_all x3 -> x2, waiting for transfers between devices: 28 us -> 7.7 us  [home(): lax.all_to_all(mine, 'fsdp', 0, 0, tiled=True)]
    all_to_all x4 -> x3, waiting for transfers between devices: 23.6 us -> 9.73 us  [spread(): return lax.all_to_all(flat, 'fsdp', 0, 0, tiled=True)]
  transfers between devices with their start and end apart: 91 -> 63, of which waited for: 35 -> 33; matrix products, arithmetic and copies ran while one was open for 35% -> 16% of each run, Pallas kernels for 0% -> 25%
where the time goes in v2:
time: 752 us; the launch traced here: 746 us
  waiting for transfers between devices  339 us (45%)
  Pallas kernels  187 us (25%)
  starting transfers between devices  74.4 us (10%)
  other arithmetic  73.3 us (10%)
  local copies, waits for them, and re-layouts  57.9 us (8%)
  between operations  15.1 us (2%)
    ppermute x50, waiting for transfers between devices, swap(): return lax.ppermute(value, BOTH, [(i, i ^ mask) for i in range(count)])  272 us
    pallas_call x5, Pallas kernels, call(): pl.pallas_call(body, out_shape=out_shape, grid_spec=pltpu.PrefetchScalarG...  129 us
    pallas_call x4, Pallas kernels, outer(): pl.pallas_call(body, out_shape=jax.ShapeDtypeStruct((height, width), BF16...  55.1 us
    ppermute x50, starting transfers between devices, swap(): return lax.ppermute(value, BOTH, [(i, i ^ mask) for i in range(count)])  50.8 us
    all_gather x4, waiting for transfers between devices, planes(): return lax.all_gather(value, 'dp', axis=0, tiled=True)  47.7 us
    unnamed x94, local copies, waits for them, and re-layouts  40.9 us
    convert_element_type x12, other arithmetic, add_low(): return (left.astype(F32) + right.astype(F32)).astype(BF16)  26.8 us
  transfers between devices with their start and end apart: 63, of which 33 were waited for; matrix products, arithmetic and copies ran while one was open for 16% of the time, Pallas kernels for 25%

profile of v2, /device:TPU:0, one launch (start us, length us, event | category | flops | bytes accessed | tf_op | source)
XLA Modules:
  0.0 746.1 jit_solution(13461016718767288101)
XLA Ops:
  20.0 9.7 %all-to-all-done = bf16[8,64,768]{2,1,0:T(8,128)(2,1)} async-done(((bf16[8,64,768]{2,1,0:T(8,128)(2,1)}), bf16[8,64,768]{2,1,0:T(8,128)(2,1)}, u32[]{:S(2)}, u32[]{:S(2)}) %all-to-all-start) | async-done | bytes 786464 | tf_op jit(solution)/shard_map/all_to_all | solution.py:517
  36.4 8.0 %collective-permute-done = bf16[128,2048]{1,0:T(8,128)(2,1)} collective-permute-done((bf16[128,2048]{1,0:T(8,128)(2,1)}, bf16[128,2048]{1,0:T(8,128)(2,1)}, u32[]{:S(2)}, u32[]{:S(2)}) %collective-permute-start) | collective-permute-done | bytes 524320 | tf_op jit(solution)/shard_map/ppermute | solution.py:399
  61.1 16.5 %collective-permute-done.2 = bf16[128,2048]{1,0:T(8,128)(2,1)} collective-permute-done((bf16[128,2048]{1,0:T(8,128)(2,1)}, bf16[128,2048]{1,0:T(8,128)(2,1)}, u32[]{:S(2)}, u32[]{:S(2)}) %collective-permute-start.2) | collective-permute-done | bytes 524320 | tf_op jit(solution)/shard_map/ppermute | solution.py:399
  84.1 8.1 %collective-permute-done.5 = bf16[128,2048]{1,0:T(8,128)(2,1)S(1)} collective-permute-done((bf16[128,2048]{1,0:T(8,128)(2,1)}, bf16[128,2048]{1,0:T(8,128)(2,1)S(1)}, u32[]{:S(2)}, u32[]{:S(2)}) %collective-permute-start.5) | collective-permute-done | bytes 524320 | tf_op jit(solution)/shard_map/ppermute | solution.py:399
  97.0 8.1 %collective-permute-done.8 = bf16[128,2048]{1,0:T(8,128)(2,1)S(1)} collective-permute-done((bf16[128,2048]{1,0:T(8,128)(2,1)S(1)}, bf16[128,2048]{1,0:T(8,128)(2,1)S(1)}, u32[]{:S(2)}, u32[]{:S(2)}) %collective-permute-start.8) | collective-permute-done | bytes 524320 | tf_op jit(solution)/shard_map/ppermute | solution.py:399
  111.0 10.1 %collective-permute-done.9 = bf16[128,2048]{1,0:T(8,128)(2,1)S(1)} collective-permute-done((bf16[128,2048]{1,0:T(8,128)(2,1)S(1)}, bf16[128,2048]{1,0:T(8,128)(2,1)S(1)}, u32[]{:S(2)}, u32[]{:S(2)}) %collective-permute-start.9) | collective-permute-done | bytes 524320 | tf_op jit(solution)/shard_map/ppermute | solution.py:399
  121.9 7.2 collective-permute-done.10
  143.9 23.5 %attention_forward.1 = (bf16[1024,2048]{1,0:T(8,128)(2,1)}, bf16[1024,2048]{1,0:T(8,128)(2,1)}, bf16[2048,768]{1,0:T(8,128)(2,1)}, bf16[2048,256]{1,0:T(8,128)(2,1)}) custom-call(s32[16]{0:T(128)} %reshape.397.live_ref, bf16[1024,2048]{1,0:T(8,128)(2,1)} %constant_dynamic-update-slice_fusion.refs_0_, bf16[1024,2048]{1,0:T(8,128)(2,1)} %collective-permute-done.6.refs_1_, ...), custom_call_target="tpu_custom_call" | custom-call | flops 171798688 | bytes 513802 | tf_op jit(solution)/shard_map/attention_forward/pallas_call | solution.py:92
  167.6 7.2 collective-permute-done.15
  180.1 23.0 %collective-permute-done.16 = bf16[2,128,2048]{2,1,0:T(8,128)(2,1)S(1)} collective-permute-done((bf16[2,128,2048]{2,1,0:T(8,128)(2,1)S(1)}, bf16[2,128,2048]{2,1,0:T(8,128)(2,1)S(1)}, u32[]{:S(2)}, u32[]{:S(2)}) %collective-permute-start.16) | collective-permute-done | bytes 1048608 | tf_op jit(solution)/shard_map/ppermute | solution.py:399
  235.5 5.6 collective-permute-done.20
  250.6 8.5 %collective-permute-done.21 = bf16[128,2048]{1,0:T(8,128)(2,1)S(1)} collective-permute-done((bf16[128,2048]{1,0:T(8,128)(2,1)}, bf16[128,2048]{1,0:T(8,128)(2,1)S(1)}, u32[]{:S(2)}, u32[]{:S(2)}) %collective-permute-start.21) | collective-permute-done | bytes 524320 | tf_op jit(solution)/shard_map/ppermute | solution.py:399
  270.0 14.3 %all-gather.9.cloned.1.call-done.refs_2_.refs_5_ = bf16[2048,2048]{1,0:T(8,128)(2,1)} async-done(((bf16[512,2048]{1,0:T(8,128)(2,1)}), bf16[2048,2048]{1,0:T(8,128)(2,1)}) %all-gather.9.cloned.1.call-update) | async-done | bytes 8388624 | tf_op jit(solution)/shard_map/all_gather | solution.py:509
  284.4 7.4 collective-permute-done.26.refs_1_
  291.8 25.7 %feed_forward.1 = (f32[2048,1024]{1,0:T(8,128)}, f32[2048,1024]{1,0:T(8,128)}, bf16[2048,1024]{1,0:T(8,128)(2,1)}) custom-call(bf16[1024,2048]{1,0:T(8,128)(2,1)} %constant_dynamic-update-slice_fusion.16.refs_0_, bf16[1024,2048]{1,0:T(8,128)(2,1)} %collective-permute-done.26.refs_1_, bf16[2048,2048]{1,0:T(8,128)(2,1)} %all-gather.9.cloned.1.call-done.refs_2_.refs_5_), custom_call_target="tpu_custom_call" | custom-call | flops 343597376 | bytes 754974 | tf_op jit(solution)/shard_map/feed_forward/pallas_call | solution.py:92
  317.5 13.3 %outer.4 = bf16[2048,1024]{1,0:T(8,128)(2,1)} custom-call(bf16[1024,2048]{1,0:T(8,128)(2,1)} %constant_dynamic-update-slice_fusion.8.refs_0_, bf16[1024,2048]{1,0:T(8,128)(2,1)} %collective-permute-done.14.refs_1_, bf16[2048,1024]{1,0:T(8,128)(2,1)} %get-tuple-element.71.refs_2_.active_ref), custom_call_target="tpu_custom_call" | custom-call | flops 171798688 | bytes 335544 | tf_op jit(solution)/shard_map/outer/pallas_call | solution.py:345
  331.4 33.4 %all-gather.11.cloned.1.call-done.refs_4_.wd_ref = bf16[2048,1024]{1,0:T(8,128)(2,1)} async-done(((bf16[512,1024]{1,0:T(8,128)(2,1)}), bf16[2048,1024]{1,0:T(8,128)(2,1)}) %all-gather.11.cloned.1.call-update) | async-done | bytes 4194320 | tf_op jit(solution)/shard_map/all_gather | solution.py:509
  364.8 38.5 %feed_back.1 = (bf16[1024,2048]{1,0:T(8,128)(2,1)}, bf16[1024,2048]{1,0:T(8,128)(2,1)}, bf16[2048,2048]{1,0:T(8,128)(2,1)}) custom-call(bf16[1024,2048]{1,0:T(8,128)(2,1)} %constant_dynamic-update-slice_fusion.8.refs_0_, bf16[1024,2048]{1,0:T(8,128)(2,1)} %collective-permute-done.14.refs_1_, f32[2048,1024]{1,0:T(8,128)} %get-tuple-element.63.refs_2_, ...), custom_call_target="tpu_custom_call" | custom-call | flops 515396064 | bytes 1090519 | tf_op jit(solution)/shard_map/feed_back/pallas_call | solution.py:92
  403.3 7.4 collective-permute-done.27
  414.8 23.9 %outer.5 = bf16[2048,2048]{1,0:T(8,128)(2,1)} custom-call(bf16[1024,2048]{1,0:T(8,128)(2,1)} %constant_dynamic-update-slice_fusion.16.refs_0_, bf16[1024,2048]{1,0:T(8,128)(2,1)} %collective-permute-done.26.refs_1_, bf16[2048,2048]{1,0:T(8,128)(2,1)} %get-tuple-element.69.refs_2_), custom_call_target="tpu_custom_call" | custom-call | flops 17179869184 | bytes 25165824 | tf_op jit(solution)/shard_map/outer/pallas_call | solution.py:345
  441.5 22.8 %collective-permute-done.28 = bf16[2,128,2048]{2,1,0:T(8,128)(2,1)S(1)} collective-permute-done((bf16[2,128,2048]{2,1,0:T(8,128)(2,1)}, bf16[2,128,2048]{2,1,0:T(8,128)(2,1)S(1)}, u32[]{:S(2)}, u32[]{:S(2)}) %collective-permute-start.28) | collective-permute-done | bytes 1048608 | tf_op jit(solution)/shard_map/ppermute | solution.py:399
  469.5 9.3 %collective-permute-done.29 = bf16[128,2048]{1,0:T(8,128)(2,1)S(1)} collective-permute-done((bf16[128,2048]{1,0:T(8,128)(2,1)S(1)}, bf16[128,2048]{1,0:T(8,128)(2,1)S(1)}, u32[]{:S(2)}, u32[]{:S(2)}) %collective-permute-start.29) | collective-permute-done | bytes 524320 | tf_op jit(solution)/shard_map/ppermute | solution.py:399
  492.0 10.3 %collective-permute-done.37 = bf16[128,2048]{1,0:T(8,128)(2,1)} collective-permute-done((bf16[128,2048]{1,0:T(8,128)(2,1)}, bf16[128,2048]{1,0:T(8,128)(2,1)}, u32[]{:S(2)}, u32[]{:S(2)}) %collective-permute-start.37) | collective-permute-done | bytes 524320 | tf_op jit(solution)/shard_map/ppermute | solution.py:399
  503.7 14.5 %feed_down.1 = (bf16[1024,2048]{1,0:T(8,128)(2,1)}, bf16[1024,2048]{1,0:T(8,128)(2,1)}) custom-call(bf16[2048,1024]{1,0:T(8,128)(2,1)} %get-tuple-element.71.refs_2_.active_ref, bf16[2048,1024]{1,0:T(8,128)(2,1)} %all-gather.11.cloned.1.call-done.refs_4_.wd_ref), custom_call_target="tpu_custom_call" | custom-call | flops 8589934592 | bytes 16777216 | tf_op jit(solution)/shard_map/feed_down/pallas_call | solution.py:92
  540.9 7.0 outer.6
  547.9 14.0 %collective-permute-done.33 = bf16[2,128,2048]{2,1,0:T(8,128)(2,1)} collective-permute-done((bf16[2,128,2048]{2,1,0:T(8,128)(2,1)}, bf16[2,128,2048]{2,1,0:T(8,128)(2,1)}, u32[]{:S(2)}, u32[]{:S(2)}) %collective-permute-start.33) | collective-permute-done | bytes 1048608 | tf_op jit(solution)/shard_map/ppermute | solution.py:399
  566.2 26.4 %attention_backward.1 = (bf16[1024,2048]{1,0:T(8,128)(2,1)}, bf16[1024,2048]{1,0:T(8,128)(2,1)}, bf16[2048,768]{1,0:T(8,128)(2,1)}) custom-call(s32[16]{0:T(128)} %reshape.397.live_ref, bf16[1024,2048]{1,0:T(8,128)(2,1)} %constant_dynamic-update-slice_fusion.24.refs_1_.refs_0_, bf16[1024,2048]{1,0:T(8,128)(2,1)} %collective-permute-done.43.refs_2_.refs_1_, ...), custom_call_target="tpu_custom_call" | custom-call | flops 8589934592 | bytes 27787264 | tf_op jit(solution)/shard_map/attention_backward/pallas_call | solution.py:92
  596.3 10.9 %outer.7 = bf16[2048,768]{1,0:T(8,128)(2,1)} custom-call(bf16[1024,2048]{1,0:T(8,128)(2,1)} %constant_dynamic-update-slice_fusion.refs_0_, bf16[1024,2048]{1,0:T(8,128)(2,1)} %collective-permute-done.6.refs_1_, bf16[2048,768]{1,0:T(8,128)(2,1)} %get-tuple-element.82.refs_2_), custom_call_target="tpu_custom_call" | custom-call | flops 6442450944 | bytes 14680064 | tf_op jit(solution)/shard_map/outer/pallas_call | solution.py:345
  611.1 12.9 %collective-permute-done.34 = bf16[128,2048]{1,0:T(8,128)(2,1)} collective-permute-done((bf16[128,2048]{1,0:T(8,128)(2,1)}, bf16[128,2048]{1,0:T(8,128)(2,1)}, u32[]{:S(2)}, u32[]{:S(2)}) %collective-permute-start.34) | collective-permute-done | bytes 524320 | tf_op jit(solution)/shard_map/ppermute | solution.py:399
  640.5 17.3 %collective-permute-done.45 = bf16[2,128,2048]{2,1,0:T(8,128)(2,1)} collective-permute-done((bf16[2,128,2048]{2,1,0:T(8,128)(2,1)}, bf16[2,128,2048]{2,1,0:T(8,128)(2,1)}, u32[]{:S(2)}, u32[]{:S(2)}) %collective-permute-start.45) | collective-permute-done | bytes 1048608 | tf_op jit(solution)/shard_map/ppermute | solution.py:399
  665.3 37.3 %collective-permute-done.46 = bf16[128,2048]{1,0:T(8,128)(2,1)} collective-permute-done((bf16[128,2048]{1,0:T(8,128)(2,1)}, bf16[128,2048]{1,0:T(8,128)(2,1)}, u32[]{:S(2)}, u32[]{:S(2)}) %collective-permute-start.46) | collective-permute-done | bytes 524320 | tf_op jit(solution)/shard_map/ppermute | solution.py:399
  727.1 7.7 %all-to-all-done.4.refs_0_ = bf16[8,64,768]{2,1,0:T(8,128)(2,1)} async-done(((bf16[8,64,768]{2,1,0:T(8,128)(2,1)}), bf16[8,64,768]{2,1,0:T(8,128)(2,1)}, u32[]{:S(2)}, u32[]{:S(2)}) %all-to-all-start.4) | async-done | bytes 786464 | tf_op jit(solution)/shard_map/all_to_all | solution.py:577
  (300 shorter events, 241.3 us)
Async XLA Ops:
  17.0 117.6 %all-gather.7.cloned.1.call-start = ((), (), s32[]{:S(2)}) async-start(), calls=%async_computation.10 | async-start | bytes 1310720 | tf_op jit(solution)/shard_map/all_gather | solution.py:509
  34.9 24.3 %collective-permute-start.1 = (bf16[128,2048]{1,0:T(8,128)(2,1)}, bf16[128,2048]{1,0:T(8,128)(2,1)}, u32[]{:S(2)}, u32[]{:S(2)}) collective-permute-start(bf16[128,2048]{1,0:T(8,128)(2,1)} %get-tuple-element.164), channel_id=1, source_target_pairs={{0,4},{1,5},{2,6},{3,7},{4,0},{5,1},{6,2},{7,3},{8,12},{9,13},{10,... | collective-permute-start | bytes 1572872 | tf_op jit(solution)/shard_map/ppermute | solution.py:399
  44.3 33.3 %collective-permute-start.2 = (bf16[128,2048]{1,0:T(8,128)(2,1)}, bf16[128,2048]{1,0:T(8,128)(2,1)}, u32[]{:S(2)}, u32[]{:S(2)}) collective-permute-start(bf16[128,2048]{1,0:T(8,128)(2,1)} %collective-permute-done), channel_id=1, source_target_pairs={{0,4},{1,5},{2,6},{3,7},{4,0},{5,1},{6,2},{7,3},{8,12},{9,13},{10,... | collective-permute-start | bytes 1572872 | tf_op jit(solution)/shard_map/ppermute | solution.py:399
  45.6 36.7 %collective-permute-start.4 = (bf16[128,2048]{1,0:T(8,128)(2,1)}, bf16[128,2048]{1,0:T(8,128)(2,1)}, u32[]{:S(2)}, u32[]{:S(2)}) collective-permute-start(bf16[128,2048]{1,0:T(8,128)(2,1)} %get-tuple-element.163), channel_id=1, source_target_pairs={{0,2},{1,3},{2,0},{3,1},{4,6},{5,7},{6,4},{7,5},{8,10},{9,11},{10,... | collective-permute-start | bytes 1572872 | tf_op jit(solution)/shard_map/ppermute | solution.py:399
  47.3 45.8 %all-to-all-start.1 = ((bf16[8,64,2048]{2,1,0:T(8,128)(2,1)}), bf16[8,64,2048]{2,1,0:T(8,128)(2,1)}, u32[]{:S(2)}, u32[]{:S(2)}) async-start(bf16[8,64,2048]{2,1,0:T(8,128)(2,1)} %pad_maximum_fusion.1), calls=%async_computation.1 | async-start | bytes 4194304 | tf_op jit(solution)/shard_map/all_to_all | solution.py:517
  51.7 90.8 %all-gather.5.cloned.1.call-start = ((), (), s32[]{:S(2)}) async-start(), calls=%async_computation.9 | async-start | bytes 3932160 | tf_op jit(solution)/shard_map/all_gather | solution.py:509
  52.4 231.9 %all-gather.9.cloned.1.call-start = ((), (), s32[]{:S(2)}) async-start(), calls=%async_computation.11 | async-start | bytes 10485760 | tf_op jit(solution)/shard_map/all_gather | solution.py:509
  52.6 39.6 %collective-permute-start.5 = (bf16[128,2048]{1,0:T(8,128)(2,1)}, bf16[128,2048]{1,0:T(8,128)(2,1)S(1)}, u32[]{:S(2)}, u32[]{:S(2)}) collective-permute-start(bf16[128,2048]{1,0:T(8,128)(2,1)} %collective-permute-done.3), channel_id=1, source_target_pairs={{0,2},{1,3},{2,0},{3,1},{4,6},{5,7},{6,4},{7,5},{8,10},{9,11},{10,... | collective-permute-start | bytes 1572872 | tf_op jit(solution)/shard_map/ppermute | solution.py:399
  96.7 45.7 %collective-permute-start.6 = (bf16[1024,2048]{1,0:T(8,128)(2,1)}, bf16[1024,2048]{1,0:T(8,128)(2,1)}, u32[]{:S(2)}, u32[]{:S(2)}) collective-permute-start(bf16[1024,2048]{1,0:T(8,128)(2,1)} %constant_dynamic-update-slice_fusion.refs_0_), channel_id=1, source_target_pairs={{0,1},{1,0},{2,3},{3,2},{4,5},{5,4},{6,7},{7,6},{8,9},{9,8},{10,11... | collective-permute-start | bytes 12582920 | tf_op jit(solution)/shard_map/ppermute | solution.py:399
  96.7 24.4 %collective-permute-start.9 = (bf16[128,2048]{1,0:T(8,128)(2,1)S(1)}, bf16[128,2048]{1,0:T(8,128)(2,1)S(1)}, u32[]{:S(2)}, u32[]{:S(2)}) collective-permute-start(bf16[128,2048]{1,0:T(8,128)(2,1)S(1)} %get-tuple-element.162), channel_id=1, source_target_pairs={{0,4},{1,5},{2,6},{3,7},{4,0},{5,1},{6,2},{7,3},{8,12},{9,13},{10,... | collective-permute-start | bytes 1572872 | tf_op jit(solution)/shard_map/ppermute | solution.py:399
  133.4 34.0 %collective-permute-start.14 = (bf16[1024,2048]{1,0:T(8,128)(2,1)}, bf16[1024,2048]{1,0:T(8,128)(2,1)}, u32[]{:S(2)}, u32[]{:S(2)}) collective-permute-start(bf16[1024,2048]{1,0:T(8,128)(2,1)} %constant_dynamic-update-slice_fusion.8.refs_0_), channel_id=1, source_target_pairs={{0,1},{1,0},{2,3},{3,2},{4,5},{5,4},{6,7},{7,6},{8,9},{9,8},{10,11... | collective-permute-start | bytes 12582920 | tf_op jit(solution)/shard_map/ppermute | solution.py:399
  177.9 25.3 %collective-permute-start.16 = (bf16[2,128,2048]{2,1,0:T(8,128)(2,1)S(1)}, bf16[2,128,2048]{2,1,0:T(8,128)(2,1)S(1)}, u32[]{:S(2)}, u32[]{:S(2)}) collective-permute-start(bf16[2,128,2048]{2,1,0:T(8,128)(2,1)S(1)} %get-tuple-element.141), channel_id=1, source_target_pairs={{0,4},{1,5},{2,6},{3,7},{4,0},{5,1},{6,2},{7,3},{8,12},{9,13},{10,... | collective-permute-start | bytes 3145736 | tf_op jit(solution)/shard_map/ppermute | solution.py:399
  179.7 25.0 %collective-permute-start.18 = (bf16[2,128,2048]{2,1,0:T(8,128)(2,1)S(1)}, bf16[2,128,2048]{2,1,0:T(8,128)(2,1)S(1)}, u32[]{:S(2)}, u32[]{:S(2)}) collective-permute-start(bf16[2,128,2048]{2,1,0:T(8,128)(2,1)S(1)} %get-tuple-element.139), channel_id=1, source_target_pairs={{0,2},{1,3},{2,0},{3,1},{4,6},{5,7},{6,4},{7,5},{8,10},{9,11},{10,... | collective-permute-start | bytes 3145736 | tf_op jit(solution)/shard_map/ppermute | solution.py:399
  209.4 25.5 %all-to-all-start.2 = ((bf16[8,64,1024]{2,1,0:T(8,128)(2,1)}), bf16[8,64,1024]{2,1,0:T(8,128)(2,1)}, u32[]{:S(2)}, u32[]{:S(2)}) async-start(bf16[8,64,1024]{2,1,0:T(8,128)(2,1)} %bitcast.336), calls=%async_computation.3 | async-start | bytes 2097152 | tf_op jit(solution)/shard_map/all_to_all | solution.py:517
  213.6 151.2 %all-gather.11.cloned.1.call-start = ((), (), s32[]{:S(2)}) async-start(), calls=%async_computation.13 | async-start | bytes 5242880 | tf_op jit(solution)/shard_map/all_gather | solution.py:509
  234.9 247.8 %reduce-scatter.5.cloned.1.call-start = ((), (), s32[]{:S(2)}) async-start(), calls=%async_computation.12 | async-start | bytes 5242880 | tf_op jit(solution)/shard_map/reduce_scatter | solution.py:512
  330.9 278.9 %reduce-scatter.7.cloned.1.call-start = ((), (), s32[]{:S(2)}) async-start(), calls=%async_computation.14 | async-start | bytes 10485760 | tf_op jit(solution)/shard_map/reduce_scatter | solution.py:512
  438.7 268.3 %reduce-scatter.11.cloned.1.call-start = ((), (), s32[]{:S(2)}) async-start(), calls=%async_computation.16 | async-start | bytes 1310720 | tf_op jit(solution)/shard_map/reduce_scatter | solution.py:512
  438.8 25.5 %collective-permute-start.28 = (bf16[2,128,2048]{2,1,0:T(8,128)(2,1)}, bf16[2,128,2048]{2,1,0:T(8,128)(2,1)S(1)}, u32[]{:S(2)}, u32[]{:S(2)}) collective-permute-start(bf16[2,128,2048]{2,1,0:T(8,128)(2,1)} %get-tuple-element.137), channel_id=1, source_target_pairs={{0,4},{1,5},{2,6},{3,7},{4,0},{5,1},{6,2},{7,3},{8,12},{9,13},{10,... | collective-permute-start | bytes 3145736 | tf_op jit(solution)/shard_map/ppermute | solution.py:399
  440.0 26.7 %collective-permute-start.30 = (bf16[2,128,2048]{2,1,0:T(8,128)(2,1)}, bf16[2,128,2048]{2,1,0:T(8,128)(2,1)S(1)}, u32[]{:S(2)}, u32[]{:S(2)}) collective-permute-start(bf16[2,128,2048]{2,1,0:T(8,128)(2,1)} %get-tuple-element.135), channel_id=1, source_target_pairs={{0,2},{1,3},{2,0},{3,1},{4,6},{5,7},{6,4},{7,5},{8,10},{9,11},{10,... | collective-permute-start | bytes 3145736 | tf_op jit(solution)/shard_map/ppermute | solution.py:399
  487.9 32.6 %collective-permute-start.38 = (bf16[128,2048]{1,0:T(8,128)(2,1)}, bf16[128,2048]{1,0:T(8,128)(2,1)}, u32[]{:S(2)}, u32[]{:S(2)}) collective-permute-start(bf16[128,2048]{1,0:T(8,128)(2,1)} %get-tuple-element.154), channel_id=1, source_target_pairs={{0,4},{1,5},{2,6},{3,7},{4,0},{5,1},{6,2},{7,3},{8,12},{9,13},{10,... | collective-permute-start | bytes 1572872 | tf_op jit(solution)/shard_map/ppermute | solution.py:399
  489.1 29.1 %collective-permute-start.40 = (bf16[128,2048]{1,0:T(8,128)(2,1)}, bf16[128,2048]{1,0:T(8,128)(2,1)S(1)}, u32[]{:S(2)}, u32[]{:S(2)}) collective-permute-start(bf16[128,2048]{1,0:T(8,128)(2,1)} %get-tuple-element.153), channel_id=1, source_target_pairs={{0,4},{1,5},{2,6},{3,7},{4,0},{5,1},{6,2},{7,3},{8,12},{9,13},{10,... | collective-permute-start | bytes 1572872 | tf_op jit(solution)/shard_map/ppermute | solution.py:399
  489.9 36.2 %collective-permute-start.41 = (bf16[128,2048]{1,0:T(8,128)(2,1)}, bf16[128,2048]{1,0:T(8,128)(2,1)}, u32[]{:S(2)}, u32[]{:S(2)}) collective-permute-start(bf16[128,2048]{1,0:T(8,128)(2,1)} %get-tuple-element.153), channel_id=1, source_target_pairs={{0,2},{1,3},{2,0},{3,1},{4,6},{5,7},{6,4},{7,5},{8,10},{9,11},{10,... | collective-permute-start | bytes 1572872 | tf_op jit(solution)/shard_map/ppermute | solution.py:399
  536.0 25.9 %collective-permute-start.33 = (bf16[2,128,2048]{2,1,0:T(8,128)(2,1)}, bf16[2,128,2048]{2,1,0:T(8,128)(2,1)}, u32[]{:S(2)}, u32[]{:S(2)}) collective-permute-start(bf16[2,128,2048]{2,1,0:T(8,128)(2,1)} %get-tuple-element.133), channel_id=1, source_target_pairs={{0,4},{1,5},{2,6},{3,7},{4,0},{5,1},{6,2},{7,3},{8,12},{9,13},{10,... | collective-permute-start | bytes 3145736 | tf_op jit(solution)/shard_map/ppermute | solution.py:399
  536.4 27.7 %collective-permute-start.35 = (bf16[2,128,2048]{2,1,0:T(8,128)(2,1)}, bf16[2,128,2048]{2,1,0:T(8,128)(2,1)}, u32[]{:S(2)}, u32[]{:S(2)}) collective-permute-start(bf16[2,128,2048]{2,1,0:T(8,128)(2,1)} %get-tuple-element.131), channel_id=1, source_target_pairs={{0,2},{1,3},{2,0},{3,1},{4,6},{5,7},{6,4},{7,5},{8,10},{9,11},{10,... | collective-permute-start | bytes 3145736 | tf_op jit(solution)/shard_map/ppermute | solution.py:399
  592.6 34.6 %collective-permute-start.44 = (bf16[2,4,128,2048]{3,2,1,0:T(8,128)(2,1)}, bf16[2,4,128,2048]{3,2,1,0:T(8,128)(2,1)}, u32[]{:S(2)}, u32[]{:S(2)}) collective-permute-start(bf16[2,4,128,2048]{3,2,1,0:T(8,128)(2,1)} %bitcast.351), channel_id=1, source_target_pairs={{0,1},{1,0},{2,3},{3,2},{4,5},{5,4},{6,7},{7,6},{8,9},{9,8},{10,11... | collective-permute-start | bytes 12582920 | tf_op jit(solution)/shard_map/ppermute | solution.py:399
  609.8 108.2 %reduce-scatter.9.cloned.1.call-start = ((), (), s32[]{:S(2)}) async-start(), calls=%async_computation.15 | async-start | bytes 3932160 | tf_op jit(solution)/shard_map/reduce_scatter | solution.py:512
  631.4 26.5 %collective-permute-start.45 = (bf16[2,128,2048]{2,1,0:T(8,128)(2,1)}, bf16[2,128,2048]{2,1,0:T(8,128)(2,1)}, u32[]{:S(2)}, u32[]{:S(2)}) collective-permute-start(bf16[2,128,2048]{2,1,0:T(8,128)(2,1)} %get-tuple-element.129), channel_id=1, source_target_pairs={{0,4},{1,5},{2,6},{3,7},{4,0},{5,1},{6,2},{7,3},{8,12},{9,13},{10,... | collective-permute-start | bytes 3145736 | tf_op jit(solution)/shard_map/ppermute | solution.py:399
  633.3 28.3 %collective-permute-start.47 = (bf16[2,128,2048]{2,1,0:T(8,128)(2,1)}, bf16[2,128,2048]{2,1,0:T(8,128)(2,1)}, u32[]{:S(2)}, u32[]{:S(2)}) collective-permute-start(bf16[2,128,2048]{2,1,0:T(8,128)(2,1)} %get-tuple-element.127), channel_id=1, source_target_pairs={{0,2},{1,3},{2,0},{3,1},{4,6},{5,7},{6,4},{7,5},{8,10},{9,11},{10,... | collective-permute-start | bytes 3145736 | tf_op jit(solution)/shard_map/ppermute | solution.py:399
  636.1 72.8 %all-to-all-start.3 = ((bf16[8,64,3072]{2,1,0:T(8,128)(2,1)}), bf16[8,64,3072]{2,1,0:T(8,128)(2,1)}, u32[]{:S(2)}, u32[]{:S(2)}) async-start(bf16[8,64,3072]{2,1,0:T(8,128)(2,1)} %bitcast.321), calls=%async_computation.5 | async-start | bytes 6291456 | tf_op jit(solution)/shard_map/all_to_all | solution.py:577
  660.0 42.6 %collective-permute-start.46 = (bf16[128,2048]{1,0:T(8,128)(2,1)}, bf16[128,2048]{1,0:T(8,128)(2,1)}, u32[]{:S(2)}, u32[]{:S(2)}) collective-permute-start(bf16[128,2048]{1,0:T(8,128)(2,1)} %fusion.62), channel_id=1, source_target_pairs={{0,2},{1,3},{2,0},{3,1},{4,6},{5,7},{6,4},{7,5},{8,10},{9,11},{10,... | collective-permute-start | bytes 1572872 | tf_op jit(solution)/shard_map/ppermute | solution.py:399
  663.8 40.4 %collective-permute-start.48 = (bf16[128,2048]{1,0:T(8,128)(2,1)}, bf16[128,2048]{1,0:T(8,128)(2,1)}, u32[]{:S(2)}, u32[]{:S(2)}) collective-permute-start(bf16[128,2048]{1,0:T(8,128)(2,1)} %fusion.64), channel_id=1, source_target_pairs={{0,4},{1,5},{2,6},{3,7},{4,0},{5,1},{6,2},{7,3},{8,12},{9,13},{10,... | collective-permute-start | bytes 1572872 | tf_op jit(solution)/shard_map/ppermute | solution.py:399
  (64 other events, 815.2 us)
Sparse Core Ops, SparseCore 0:
  19.4 29.9 all-gather.6
  54.1 65.4 all-gather.4
  133.6 150.7 all-gather.8
  285.7 78.9 all-gather.10
  366.9 75.2 reduce-scatter.4
  444.5 144.9 reduce-scatter.6
  609.9 23.5 reduce-scatter.10
  635.8 58.8 reduce-scatter.8

commit v3 on v2

--- a/solution.py
+++ b/solution.py
@@ -423,12 +423,14 @@
     return [own, swap(after(own, *meanwhile) if meanwhile else own, CORE)]
 
 
-def scatter_group(parts, first, second, like, fill=None):
+def scatter_group(parts, first, second, like, fill=None, late=None):
     if not is_paired():
         micro, length, width = like.shape
         blocks = parts[0].reshape(micro, -1, length, width)
         if fill is not None:
             fill(lambda value: value)
+        if late is not None:
+            late(lambda value: value)
         return lax.psum_scatter(blocks, "fsdp", scatter_dimension=1).astype(F32)
     keep, send = (part.reshape((2, 4) + like.shape[1:]) for part in parts)
     got = swap(send, CORE)
@@ -437,6 +439,8 @@
     if fill is not None:
         fill(lambda value: after(value, a_far, b_far))
     a_got, b_got = swap(a_far, second), swap(b_far, first)
+    if late is not None:
+        late(lambda value: after(value, a_got, b_got))
     a, a_far = add_low(a[0], a_got[0]), add_low(a[1], a_got[1])
     b, b_far = add_low(b[0], b_got[0]), add_low(b[1], b_got[1])
     a_got, b_got = swap(a_far, first), swap(b_far, second)
@@ -578,20 +582,25 @@
 
     grad_attended = gather_group(grad_low, X, Y)
     part_o = outer([mixed], grad_attended, HD)
-    ties = []
-    parts = feed_down(after(activated, grad_low), wd, len(n2))
-    returned = scatter_group(parts, X, Y, x, ties.append)
-    grad_attended = [ties[0](after(grad_attended[0], part_o)), *grad_attended[1:]]
+    grad_attended = [after(grad_attended[0], part_o), *grad_attended[1:]]
     parts, grad_qkv = attention_backward(grad_attended, lives, qkv, wqkv, wo, cosine, sine, cap)
     part_o = exchange(part_o.reshape(my_heads, sharers, own_rows, width).transpose(1, 0, 2, 3))
     part_qkv = outer(n1, [grad_qkv], ROWS, 1)
     grad_wo = over_planes(after(part_o.reshape(groups * own_rows, width), sum_gu, part_qkv))
     sum_qkv = over_planes(after(part_qkv, sum_gu))
-    sum_d, returned = lax.optimization_barrier((sum_d, returned))
+    ties = []
+    homes = []
+
+    def go_home(tie):
+        homes.append(home(jnp.concatenate([sum_d, tie(sum_gu)], axis=1)))
+
+    back_one = scatter_group(parts, X, Y, x, ties.append, go_home)
+    parts = feed_down(ties[0](after(activated, part_qkv)), wd, len(n2))
+    returned = scatter_group(parts, X, Y, x)
+    back_one, sum_dgu, returned, sum_qkv = lax.optimization_barrier(
+        (back_one, homes[0], returned, sum_qkv)
+    )
     output = ((hidden_one + returned) * my_mask).astype(BF16)
-    sum_dgu = home(jnp.concatenate([sum_d, after(sum_gu, part_qkv)], axis=1))
-    back_one = scatter_group(parts, X, Y, x)
-    back_one, sum_dgu = lax.optimization_barrier((back_one, sum_dgu))
     sum_d, sum_gu = sum_dgu[:, :, :share], sum_dgu[:, :, share:]
     grad_tokens = (
         grad_hidden
@@ -599,7 +608,7 @@
         * (back_one - normal_one * jnp.mean(back_one * normal_one, axis=-1, keepdims=True))
     ).astype(BF16)
 
-    sum_qkv = home(after(sum_qkv, sum_dgu))
+    sum_qkv = home(sum_qkv)
 
     def from_units(value):
         return value.transpose(1, 0, 2).reshape(own_rows, hidden).astype(F32)

time: 752 us -> 751 us (level)
    unnamed x94 -> x114, local copies, waits for them, and re-layouts: 40.9 us -> 35.5 us
  transfers between devices with their start and end apart: 63 -> 63, of which waited for: 33 -> 36; matrix products, arithmetic and copies ran while one was open for 16% -> 15% of each run, Pallas kernels for 25% -> 25%
where the time goes in v3:
time: 751 us; the launch traced here: 746 us
  waiting for transfers between devices  337 us (45%)
  Pallas kernels  186 us (25%)
  other arithmetic  78.6 us (10%)
  starting transfers between devices  75.1 us (10%)
  local copies, waits for them, and re-layouts  53.5 us (7%)
  between operations  15.2 us (2%)
    ppermute x50, waiting for transfers between devices, swap(): return lax.ppermute(value, BOTH, [(i, i ^ mask) for i in range(count)])  274 us
    pallas_call x5, Pallas kernels, call(): pl.pallas_call(body, out_shape=out_shape, grid_spec=pltpu.PrefetchScalarG...  128 us
    pallas_call x4, Pallas kernels, outer(): pl.pallas_call(body, out_shape=jax.ShapeDtypeStruct((height, width), BF16...  55.1 us
    ppermute x50, starting transfers between devices, swap(): return lax.ppermute(value, BOTH, [(i, i ^ mask) for i in range(count)])  51.6 us
    all_gather x4, waiting for transfers between devices, planes(): return lax.all_gather(value, 'dp', axis=0, tiled=True)  47.6 us
    unnamed x114, local copies, waits for them, and re-layouts  35.5 us
    convert_element_type x12, other arithmetic, add_low(): return (left.astype(F32) + right.astype(F32)).astype(BF16)  27.9 us
    another operation x11, other arithmetic, scatter_group(): jnp.stack([a.astype(F32) + a_got.astype(F32), b.astype(F32) + b_got.astyp...  17.5 us
  transfers between devices with their start and end apart: 63, of which 36 were waited for; matrix products, arithmetic and copies ran while one was open for 15% of the time, Pallas kernels for 25%

profile of v3, /device:TPU:0, one launch (start us, length us, event | category | flops | bytes accessed | tf_op | source)
XLA Modules:
  0.0 745.6 jit_solution(14782877764388408738)
XLA Ops:
  20.0 9.7 %all-to-all-done = bf16[8,64,768]{2,1,0:T(8,128)(2,1)} async-done(((bf16[8,64,768]{2,1,0:T(8,128)(2,1)}), bf16[8,64,768]{2,1,0:T(8,128)(2,1)}, u32[]{:S(2)}, u32[]{:S(2)}) %all-to-all-start) | async-done | bytes 786464 | tf_op jit(solution)/shard_map/all_to_all | solution.py:521
  36.4 8.0 %collective-permute-done = bf16[128,2048]{1,0:T(8,128)(2,1)} collective-permute-done((bf16[128,2048]{1,0:T(8,128)(2,1)}, bf16[128,2048]{1,0:T(8,128)(2,1)}, u32[]{:S(2)}, u32[]{:S(2)}) %collective-permute-start) | collective-permute-done | bytes 524320 | tf_op jit(solution)/shard_map/ppermute | solution.py:399
  61.1 16.5 %collective-permute-done.2 = bf16[128,2048]{1,0:T(8,128)(2,1)} collective-permute-done((bf16[128,2048]{1,0:T(8,128)(2,1)}, bf16[128,2048]{1,0:T(8,128)(2,1)}, u32[]{:S(2)}, u32[]{:S(2)}) %collective-permute-start.2) | collective-permute-done | bytes 524320 | tf_op jit(solution)/shard_map/ppermute | solution.py:399
  84.1 8.1 %collective-permute-done.5 = bf16[128,2048]{1,0:T(8,128)(2,1)S(1)} collective-permute-done((bf16[128,2048]{1,0:T(8,128)(2,1)}, bf16[128,2048]{1,0:T(8,128)(2,1)S(1)}, u32[]{:S(2)}, u32[]{:S(2)}) %collective-permute-start.5) | collective-permute-done | bytes 524320 | tf_op jit(solution)/shard_map/ppermute | solution.py:399
  97.0 8.1 %collective-permute-done.8 = bf16[128,2048]{1,0:T(8,128)(2,1)S(1)} collective-permute-done((bf16[128,2048]{1,0:T(8,128)(2,1)S(1)}, bf16[128,2048]{1,0:T(8,128)(2,1)S(1)}, u32[]{:S(2)}, u32[]{:S(2)}) %collective-permute-start.8) | collective-permute-done | bytes 524320 | tf_op jit(solution)/shard_map/ppermute | solution.py:399
  111.0 10.1 %collective-permute-done.9 = bf16[128,2048]{1,0:T(8,128)(2,1)S(1)} collective-permute-done((bf16[128,2048]{1,0:T(8,128)(2,1)S(1)}, bf16[128,2048]{1,0:T(8,128)(2,1)S(1)}, u32[]{:S(2)}, u32[]{:S(2)}) %collective-permute-start.9) | collective-permute-done | bytes 524320 | tf_op jit(solution)/shard_map/ppermute | solution.py:399
  122.0 7.2 collective-permute-done.10
  144.0 23.5 %attention_forward.1 = (bf16[1024,2048]{1,0:T(8,128)(2,1)}, bf16[1024,2048]{1,0:T(8,128)(2,1)}, bf16[2048,768]{1,0:T(8,128)(2,1)}, bf16[2048,256]{1,0:T(8,128)(2,1)}) custom-call(s32[16]{0:T(128)} %reshape.397.live_ref, bf16[1024,2048]{1,0:T(8,128)(2,1)} %constant_dynamic-update-slice_fusion.refs_0_, bf16[1024,2048]{1,0:T(8,128)(2,1)} %collective-permute-done.6.refs_1_, ...), custom_call_target="tpu_custom_call" | custom-call | flops 171798688 | bytes 513802 | tf_op jit(solution)/shard_map/attention_forward/pallas_call | solution.py:92
  167.7 7.2 collective-permute-done.15
  180.2 23.0 %collective-permute-done.16 = bf16[2,128,2048]{2,1,0:T(8,128)(2,1)S(1)} collective-permute-done((bf16[2,128,2048]{2,1,0:T(8,128)(2,1)S(1)}, bf16[2,128,2048]{2,1,0:T(8,128)(2,1)S(1)}, u32[]{:S(2)}, u32[]{:S(2)}) %collective-permute-start.16) | collective-permute-done | bytes 1048608 | tf_op jit(solution)/shard_map/ppermute | solution.py:399
  250.7 8.5 %collective-permute-done.21 = bf16[128,2048]{1,0:T(8,128)(2,1)S(1)} collective-permute-done((bf16[128,2048]{1,0:T(8,128)(2,1)}, bf16[128,2048]{1,0:T(8,128)(2,1)S(1)}, u32[]{:S(2)}, u32[]{:S(2)}) %collective-permute-start.21) | collective-permute-done | bytes 524320 | tf_op jit(solution)/shard_map/ppermute | solution.py:399
  270.2 14.2 %all-gather.9.cloned.1.call-done.refs_2_.refs_5_ = bf16[2048,2048]{1,0:T(8,128)(2,1)} async-done(((bf16[512,2048]{1,0:T(8,128)(2,1)}), bf16[2048,2048]{1,0:T(8,128)(2,1)}) %all-gather.9.cloned.1.call-update) | async-done | bytes 8388624 | tf_op jit(solution)/shard_map/all_gather | solution.py:513
  284.5 7.4 collective-permute-done.26.refs_1_
  291.9 25.8 %feed_forward.1 = (f32[2048,1024]{1,0:T(8,128)}, f32[2048,1024]{1,0:T(8,128)}, bf16[2048,1024]{1,0:T(8,128)(2,1)}) custom-call(bf16[1024,2048]{1,0:T(8,128)(2,1)} %constant_dynamic-update-slice_fusion.16.refs_0_, bf16[1024,2048]{1,0:T(8,128)(2,1)} %collective-permute-done.26.refs_1_, bf16[2048,2048]{1,0:T(8,128)(2,1)} %all-gather.9.cloned.1.call-done.refs_2_.refs_5_), custom_call_target="tpu_custom_call" | custom-call | flops 343597376 | bytes 754974 | tf_op jit(solution)/shard_map/feed_forward/pallas_call | solution.py:92
  317.7 13.3 %outer.4 = bf16[2048,1024]{1,0:T(8,128)(2,1)} custom-call(bf16[1024,2048]{1,0:T(8,128)(2,1)} %constant_dynamic-update-slice_fusion.8.refs_0_, bf16[1024,2048]{1,0:T(8,128)(2,1)} %collective-permute-done.14.refs_1_, bf16[2048,1024]{1,0:T(8,128)(2,1)} %get-tuple-element.78.refs_2_.active_ref), custom_call_target="tpu_custom_call" | custom-call | flops 171798688 | bytes 335544 | tf_op jit(solution)/shard_map/outer/pallas_call | solution.py:345
  331.5 33.3 %all-gather.11.cloned.1.call-done.refs_4_.wd_ref = bf16[2048,1024]{1,0:T(8,128)(2,1)} async-done(((bf16[512,1024]{1,0:T(8,128)(2,1)}), bf16[2048,1024]{1,0:T(8,128)(2,1)}) %all-gather.11.cloned.1.call-update) | async-done | bytes 4194320 | tf_op jit(solution)/shard_map/all_gather | solution.py:513
  364.9 38.5 %feed_back.1 = (bf16[1024,2048]{1,0:T(8,128)(2,1)}, bf16[1024,2048]{1,0:T(8,128)(2,1)}, bf16[2048,2048]{1,0:T(8,128)(2,1)}) custom-call(bf16[1024,2048]{1,0:T(8,128)(2,1)} %constant_dynamic-update-slice_fusion.8.refs_0_, bf16[1024,2048]{1,0:T(8,128)(2,1)} %collective-permute-done.14.refs_1_, f32[2048,1024]{1,0:T(8,128)} %get-tuple-element.62.refs_2_, ...), custom_call_target="tpu_custom_call" | custom-call | flops 515396064 | bytes 1090519 | tf_op jit(solution)/shard_map/feed_back/pallas_call | solution.py:92
  403.3 7.4 collective-permute-done.27
  416.7 22.5 %collective-permute-done.28 = bf16[2,128,2048]{2,1,0:T(8,128)(2,1)S(1)} collective-permute-done((bf16[2,128,2048]{2,1,0:T(8,128)(2,1)S(1)}, bf16[2,128,2048]{2,1,0:T(8,128)(2,1)S(1)}, u32[]{:S(2)}, u32[]{:S(2)}) %collective-permute-start.28) | collective-permute-done | bytes 1048608 | tf_op jit(solution)/shard_map/ppermute | solution.py:399
  444.0 23.8 %outer.5 = bf16[2048,2048]{1,0:T(8,128)(2,1)} custom-call(bf16[1024,2048]{1,0:T(8,128)(2,1)} %constant_dynamic-update-slice_fusion.16.refs_0_, bf16[1024,2048]{1,0:T(8,128)(2,1)} %collective-permute-done.26.refs_1_, bf16[2048,2048]{1,0:T(8,128)(2,1)} %get-tuple-element.68.refs_2_), custom_call_target="tpu_custom_call" | custom-call | flops 17179869184 | bytes 25165824 | tf_op jit(solution)/shard_map/outer/pallas_call | solution.py:345
  478.6 10.2 %collective-permute-done.32 = bf16[128,2048]{1,0:T(8,128)(2,1)S(1)} collective-permute-done((bf16[128,2048]{1,0:T(8,128)(2,1)S(1)}, bf16[128,2048]{1,0:T(8,128)(2,1)S(1)}, u32[]{:S(2)}, u32[]{:S(2)}) %collective-permute-start.32) | collective-permute-done | bytes 524320 | tf_op jit(solution)/shard_map/ppermute | solution.py:399
  493.1 9.6 %collective-permute-done.33 = bf16[128,2048]{1,0:T(8,128)(2,1)S(1)} collective-permute-done((bf16[128,2048]{1,0:T(8,128)(2,1)S(1)}, bf16[128,2048]{1,0:T(8,128)(2,1)S(1)}, u32[]{:S(2)}, u32[]{:S(2)}) %collective-permute-start.33) | collective-permute-done | bytes 524320 | tf_op jit(solution)/shard_map/ppermute | solution.py:399
  502.7 9.3 %collective-permute-done.34 = bf16[128,2048]{1,0:T(8,128)(2,1)S(1)} collective-permute-done((bf16[128,2048]{1,0:T(8,128)(2,1)S(1)}, bf16[128,2048]{1,0:T(8,128)(2,1)S(1)}, u32[]{:S(2)}, u32[]{:S(2)}) %collective-permute-start.34) | collective-permute-done | bytes 524320 | tf_op jit(solution)/shard_map/ppermute | solution.py:399
  515.5 7.2 collective-permute-done.38.refs_2_.refs_1_
  524.7 7.1 outer.6
  531.8 26.2 %attention_backward.1 = (bf16[1024,2048]{1,0:T(8,128)(2,1)}, bf16[1024,2048]{1,0:T(8,128)(2,1)}, bf16[2048,768]{1,0:T(8,128)(2,1)}) custom-call(s32[16]{0:T(128)} %reshape.397.live_ref, bf16[1024,2048]{1,0:T(8,128)(2,1)} %copy-done.14, bf16[1024,2048]{1,0:T(8,128)(2,1)} %copy-done.27, bf16[2048,768]{1,0:T(8,128)(2,1)} %get-tuple-element.72.refs_2_, ...), custom_call_target="tpu_custom_call" | custom-call | flops 8589934592 | bytes 27787264 | tf_op jit(solution)/shard_map/attention_backward/pallas_call | solution.py:92
  558.2 7.1 collective-permute-done.39
  571.6 10.9 %outer.7 = bf16[2048,768]{1,0:T(8,128)(2,1)} custom-call(bf16[1024,2048]{1,0:T(8,128)(2,1)} %constant_dynamic-update-slice_fusion.refs_0_, bf16[1024,2048]{1,0:T(8,128)(2,1)} %collective-permute-done.6.refs_1_, bf16[2048,768]{1,0:T(8,128)(2,1)} %get-tuple-element.76.refs_2_), custom_call_target="tpu_custom_call" | custom-call | flops 6442450944 | bytes 14680064 | tf_op jit(solution)/shard_map/outer/pallas_call | solution.py:345
  585.7 9.3 %collective-permute-done.40 = bf16[2,128,2048]{2,1,0:T(8,128)(2,1)} collective-permute-done((bf16[2,128,2048]{2,1,0:T(8,128)(2,1)}, bf16[2,128,2048]{2,1,0:T(8,128)(2,1)}, u32[]{:S(2)}, u32[]{:S(2)}) %collective-permute-start.40) | collective-permute-done | bytes 1048608 | tf_op jit(solution)/shard_map/ppermute | solution.py:399
  599.0 14.4 %feed_down.1 = (bf16[1024,2048]{1,0:T(8,128)(2,1)}, bf16[1024,2048]{1,0:T(8,128)(2,1)}) custom-call(bf16[2048,1024]{1,0:T(8,128)(2,1)} %get-tuple-element.78.refs_2_.active_ref, bf16[2048,1024]{1,0:T(8,128)(2,1)} %all-gather.11.cloned.1.call-done.refs_4_.wd_ref), custom_call_target="tpu_custom_call" | custom-call | flops 8589934592 | bytes 16777216 | tf_op jit(solution)/shard_map/feed_down/pallas_call | solution.py:92
  643.1 12.6 %collective-permute-done.45 = bf16[2,128,2048]{2,1,0:T(8,128)(2,1)} collective-permute-done((bf16[2,128,2048]{2,1,0:T(8,128)(2,1)}, bf16[2,128,2048]{2,1,0:T(8,128)(2,1)}, u32[]{:S(2)}, u32[]{:S(2)}) %collective-permute-start.45) | collective-permute-done | bytes 1048608 | tf_op jit(solution)/shard_map/ppermute | solution.py:399
  666.1 38.2 %collective-permute-done.46 = bf16[128,2048]{1,0:T(8,128)(2,1)} collective-permute-done((bf16[128,2048]{1,0:T(8,128)(2,1)}, bf16[128,2048]{1,0:T(8,128)(2,1)}, u32[]{:S(2)}, u32[]{:S(2)}) %collective-permute-start.46) | collective-permute-done | bytes 524320 | tf_op jit(solution)/shard_map/ppermute | solution.py:399
  (320 shorter events, 252.0 us)
Async XLA Ops:
  17.0 117.7 %all-gather.7.cloned.1.call-start = ((), (), s32[]{:S(2)}) async-start(), calls=%async_computation.10 | async-start | bytes 1310720 | tf_op jit(solution)/shard_map/all_gather | solution.py:513
  34.9 24.3 %collective-permute-start.1 = (bf16[128,2048]{1,0:T(8,128)(2,1)}, bf16[128,2048]{1,0:T(8,128)(2,1)}, u32[]{:S(2)}, u32[]{:S(2)}) collective-permute-start(bf16[128,2048]{1,0:T(8,128)(2,1)} %get-tuple-element.162), channel_id=1, source_target_pairs={{0,4},{1,5},{2,6},{3,7},{4,0},{5,1},{6,2},{7,3},{8,12},{9,13},{10,... | collective-permute-start | bytes 1572872 | tf_op jit(solution)/shard_map/ppermute | solution.py:399
  44.3 33.3 %collective-permute-start.2 = (bf16[128,2048]{1,0:T(8,128)(2,1)}, bf16[128,2048]{1,0:T(8,128)(2,1)}, u32[]{:S(2)}, u32[]{:S(2)}) collective-permute-start(bf16[128,2048]{1,0:T(8,128)(2,1)} %collective-permute-done), channel_id=1, source_target_pairs={{0,4},{1,5},{2,6},{3,7},{4,0},{5,1},{6,2},{7,3},{8,12},{9,13},{10,... | collective-permute-start | bytes 1572872 | tf_op jit(solution)/shard_map/ppermute | solution.py:399
  45.5 36.7 %collective-permute-start.4 = (bf16[128,2048]{1,0:T(8,128)(2,1)}, bf16[128,2048]{1,0:T(8,128)(2,1)}, u32[]{:S(2)}, u32[]{:S(2)}) collective-permute-start(bf16[128,2048]{1,0:T(8,128)(2,1)} %get-tuple-element.161), channel_id=1, source_target_pairs={{0,2},{1,3},{2,0},{3,1},{4,6},{5,7},{6,4},{7,5},{8,10},{9,11},{10,... | collective-permute-start | bytes 1572872 | tf_op jit(solution)/shard_map/ppermute | solution.py:399
  47.3 45.8 %all-to-all-start.1 = ((bf16[8,64,2048]{2,1,0:T(8,128)(2,1)}), bf16[8,64,2048]{2,1,0:T(8,128)(2,1)}, u32[]{:S(2)}, u32[]{:S(2)}) async-start(bf16[8,64,2048]{2,1,0:T(8,128)(2,1)} %pad_maximum_fusion.1), calls=%async_computation.1 | async-start | bytes 4194304 | tf_op jit(solution)/shard_map/all_to_all | solution.py:521
  51.7 90.9 %all-gather.5.cloned.1.call-start = ((), (), s32[]{:S(2)}) async-start(), calls=%async_computation.9 | async-start | bytes 3932160 | tf_op jit(solution)/shard_map/all_gather | solution.py:513
  52.4 232.0 %all-gather.9.cloned.1.call-start = ((), (), s32[]{:S(2)}) async-start(), calls=%async_computation.11 | async-start | bytes 10485760 | tf_op jit(solution)/shard_map/all_gather | solution.py:513
  52.6 39.6 %collective-permute-start.5 = (bf16[128,2048]{1,0:T(8,128)(2,1)}, bf16[128,2048]{1,0:T(8,128)(2,1)S(1)}, u32[]{:S(2)}, u32[]{:S(2)}) collective-permute-start(bf16[128,2048]{1,0:T(8,128)(2,1)} %collective-permute-done.3), channel_id=1, source_target_pairs={{0,2},{1,3},{2,0},{3,1},{4,6},{5,7},{6,4},{7,5},{8,10},{9,11},{10,... | collective-permute-start | bytes 1572872 | tf_op jit(solution)/shard_map/ppermute | solution.py:399
  96.8 45.8 %collective-permute-start.6 = (bf16[1024,2048]{1,0:T(8,128)(2,1)}, bf16[1024,2048]{1,0:T(8,128)(2,1)}, u32[]{:S(2)}, u32[]{:S(2)}) collective-permute-start(bf16[1024,2048]{1,0:T(8,128)(2,1)} %constant_dynamic-update-slice_fusion.refs_0_), channel_id=1, source_target_pairs={{0,1},{1,0},{2,3},{3,2},{4,5},{5,4},{6,7},{7,6},{8,9},{9,8},{10,11... | collective-permute-start | bytes 12582920 | tf_op jit(solution)/shard_map/ppermute | solution.py:399
  96.8 24.4 %collective-permute-start.9 = (bf16[128,2048]{1,0:T(8,128)(2,1)S(1)}, bf16[128,2048]{1,0:T(8,128)(2,1)S(1)}, u32[]{:S(2)}, u32[]{:S(2)}) collective-permute-start(bf16[128,2048]{1,0:T(8,128)(2,1)S(1)} %get-tuple-element.160), channel_id=1, source_target_pairs={{0,4},{1,5},{2,6},{3,7},{4,0},{5,1},{6,2},{7,3},{8,12},{9,13},{10,... | collective-permute-start | bytes 1572872 | tf_op jit(solution)/shard_map/ppermute | solution.py:399
  133.5 34.0 %collective-permute-start.14 = (bf16[1024,2048]{1,0:T(8,128)(2,1)}, bf16[1024,2048]{1,0:T(8,128)(2,1)}, u32[]{:S(2)}, u32[]{:S(2)}) collective-permute-start(bf16[1024,2048]{1,0:T(8,128)(2,1)} %constant_dynamic-update-slice_fusion.8.refs_0_), channel_id=1, source_target_pairs={{0,1},{1,0},{2,3},{3,2},{4,5},{5,4},{6,7},{7,6},{8,9},{9,8},{10,11... | collective-permute-start | bytes 12582920 | tf_op jit(solution)/shard_map/ppermute | solution.py:399
  177.9 25.3 %collective-permute-start.16 = (bf16[2,128,2048]{2,1,0:T(8,128)(2,1)S(1)}, bf16[2,128,2048]{2,1,0:T(8,128)(2,1)S(1)}, u32[]{:S(2)}, u32[]{:S(2)}) collective-permute-start(bf16[2,128,2048]{2,1,0:T(8,128)(2,1)S(1)} %get-tuple-element.139), channel_id=1, source_target_pairs={{0,4},{1,5},{2,6},{3,7},{4,0},{5,1},{6,2},{7,3},{8,12},{9,13},{10,... | collective-permute-start | bytes 3145736 | tf_op jit(solution)/shard_map/ppermute | solution.py:399
  179.8 25.0 %collective-permute-start.18 = (bf16[2,128,2048]{2,1,0:T(8,128)(2,1)S(1)}, bf16[2,128,2048]{2,1,0:T(8,128)(2,1)S(1)}, u32[]{:S(2)}, u32[]{:S(2)}) collective-permute-start(bf16[2,128,2048]{2,1,0:T(8,128)(2,1)S(1)} %get-tuple-element.137), channel_id=1, source_target_pairs={{0,2},{1,3},{2,0},{3,1},{4,6},{5,7},{6,4},{7,5},{8,10},{9,11},{10,... | collective-permute-start | bytes 3145736 | tf_op jit(solution)/shard_map/ppermute | solution.py:399
  209.4 25.5 %all-to-all-start.2 = ((bf16[8,64,1024]{2,1,0:T(8,128)(2,1)}), bf16[8,64,1024]{2,1,0:T(8,128)(2,1)}, u32[]{:S(2)}, u32[]{:S(2)}) async-start(bf16[8,64,1024]{2,1,0:T(8,128)(2,1)} %bitcast.336), calls=%async_computation.2 | async-start | bytes 2097152 | tf_op jit(solution)/shard_map/all_to_all | solution.py:521
  213.7 151.2 %all-gather.11.cloned.1.call-start = ((), (), s32[]{:S(2)}) async-start(), calls=%async_computation.12 | async-start | bytes 5242880 | tf_op jit(solution)/shard_map/all_gather | solution.py:513
  235.0 237.7 %reduce-scatter.5.cloned.1.call-start = ((), (), s32[]{:S(2)}) async-start(), calls=%async_computation.13 | async-start | bytes 5242880 | tf_op jit(solution)/shard_map/reduce_scatter | solution.py:516
  331.1 284.8 %reduce-scatter.7.cloned.1.call-start = ((), (), s32[]{:S(2)}) async-start(), calls=%async_computation.14 | async-start | bytes 10485760 | tf_op jit(solution)/shard_map/reduce_scatter | solution.py:516
  413.9 25.3 %collective-permute-start.28 = (bf16[2,128,2048]{2,1,0:T(8,128)(2,1)S(1)}, bf16[2,128,2048]{2,1,0:T(8,128)(2,1)S(1)}, u32[]{:S(2)}, u32[]{:S(2)}) collective-permute-start(bf16[2,128,2048]{2,1,0:T(8,128)(2,1)S(1)} %get-tuple-element.135), channel_id=1, source_target_pairs={{0,4},{1,5},{2,6},{3,7},{4,0},{5,1},{6,2},{7,3},{8,12},{9,13},{10,... | collective-permute-start | bytes 3145736 | tf_op jit(solution)/shard_map/ppermute | solution.py:399
  415.2 26.2 %collective-permute-start.30 = (bf16[2,128,2048]{2,1,0:T(8,128)(2,1)S(1)}, bf16[2,128,2048]{2,1,0:T(8,128)(2,1)S(1)}, u32[]{:S(2)}, u32[]{:S(2)}) collective-permute-start(bf16[2,128,2048]{2,1,0:T(8,128)(2,1)S(1)} %get-tuple-element.133), channel_id=1, source_target_pairs={{0,2},{1,3},{2,0},{3,1},{4,6},{5,7},{6,4},{7,5},{8,10},{9,11},{10,... | collective-permute-start | bytes 3145736 | tf_op jit(solution)/shard_map/ppermute | solution.py:399
  440.2 27.6 %collective-permute-start.29 = (bf16[128,2048]{1,0:T(8,128)(2,1)}, bf16[128,2048]{1,0:T(8,128)(2,1)}, u32[]{:S(2)}, u32[]{:S(2)}) collective-permute-start(bf16[128,2048]{1,0:T(8,128)(2,1)} %fusion.54), channel_id=1, source_target_pairs={{0,2},{1,3},{2,0},{3,1},{4,6},{5,7},{6,4},{7,5},{8,10},{9,11},{10,... | collective-permute-start | bytes 1572872 | tf_op jit(solution)/shard_map/ppermute | solution.py:399
  442.5 27.1 %collective-permute-start.31 = (bf16[128,2048]{1,0:T(8,128)(2,1)}, bf16[128,2048]{1,0:T(8,128)(2,1)}, u32[]{:S(2)}, u32[]{:S(2)}) collective-permute-start(bf16[128,2048]{1,0:T(8,128)(2,1)} %fusion.56), channel_id=1, source_target_pairs={{0,4},{1,5},{2,6},{3,7},{4,0},{5,1},{6,2},{7,3},{8,12},{9,13},{10,... | collective-permute-start | bytes 1572872 | tf_op jit(solution)/shard_map/ppermute | solution.py:399
  467.8 196.5 %reduce-scatter.11.cloned.1.call-start = ((), (), s32[]{:S(2)}) async-start(), calls=%async_computation.16 | async-start | bytes 1310720 | tf_op jit(solution)/shard_map/reduce_scatter | solution.py:516
  477.6 25.0 %collective-permute-start.33 = (bf16[128,2048]{1,0:T(8,128)(2,1)S(1)}, bf16[128,2048]{1,0:T(8,128)(2,1)S(1)}, u32[]{:S(2)}, u32[]{:S(2)}) collective-permute-start(bf16[128,2048]{1,0:T(8,128)(2,1)S(1)} %get-tuple-element.152), channel_id=1, source_target_pairs={{0,4},{1,5},{2,6},{3,7},{4,0},{5,1},{6,2},{7,3},{8,12},{9,13},{10,... | collective-permute-start | bytes 1572872 | tf_op jit(solution)/shard_map/ppermute | solution.py:399
  569.5 25.6 %collective-permute-start.40 = (bf16[2,128,2048]{2,1,0:T(8,128)(2,1)}, bf16[2,128,2048]{2,1,0:T(8,128)(2,1)}, u32[]{:S(2)}, u32[]{:S(2)}) collective-permute-start(bf16[2,128,2048]{2,1,0:T(8,128)(2,1)} %get-tuple-element.131), channel_id=1, source_target_pairs={{0,4},{1,5},{2,6},{3,7},{4,0},{5,1},{6,2},{7,3},{8,12},{9,13},{10,... | collective-permute-start | bytes 3145736 | tf_op jit(solution)/shard_map/ppermute | solution.py:399
  569.9 27.2 %collective-permute-start.42 = (bf16[2,128,2048]{2,1,0:T(8,128)(2,1)}, bf16[2,128,2048]{2,1,0:T(8,128)(2,1)}, u32[]{:S(2)}, u32[]{:S(2)}) collective-permute-start(bf16[2,128,2048]{2,1,0:T(8,128)(2,1)} %get-tuple-element.129), channel_id=1, source_target_pairs={{0,2},{1,3},{2,0},{3,1},{4,6},{5,7},{6,4},{7,5},{8,10},{9,11},{10,... | collective-permute-start | bytes 3145736 | tf_op jit(solution)/shard_map/ppermute | solution.py:399
  585.7 27.7 %collective-permute-start.49 = (bf16[2,64,2048]{2,1,0:T(8,128)(2,1)}, bf16[2,64,2048]{2,1,0:T(8,128)(2,1)S(1)}, u32[]{:S(2)}, u32[]{:S(2)}) collective-permute-start(bf16[2,64,2048]{2,1,0:T(8,128)(2,1)} %select_bitcast_fusion), channel_id=1, source_target_pairs={{0,1},{1,0},{2,3},{3,2},{4,5},{5,4},{6,7},{7,6},{8,9},{9,8},{10,11... | collective-permute-start | bytes 1572872 | tf_op jit(solution)/shard_map/ppermute | solution.py:399
  615.8 92.9 %reduce-scatter.9.cloned.1.call-start = ((), (), s32[]{:S(2)}) async-start(), calls=%async_computation.15 | async-start | bytes 3932160 | tf_op jit(solution)/shard_map/reduce_scatter | solution.py:516
  626.6 29.1 %collective-permute-start.45 = (bf16[2,128,2048]{2,1,0:T(8,128)(2,1)}, bf16[2,128,2048]{2,1,0:T(8,128)(2,1)}, u32[]{:S(2)}, u32[]{:S(2)}) collective-permute-start(bf16[2,128,2048]{2,1,0:T(8,128)(2,1)} %get-tuple-element.127), channel_id=1, source_target_pairs={{0,4},{1,5},{2,6},{3,7},{4,0},{5,1},{6,2},{7,3},{8,12},{9,13},{10,... | collective-permute-start | bytes 3145736 | tf_op jit(solution)/shard_map/ppermute | solution.py:399
  634.1 26.4 %collective-permute-start.47 = (bf16[2,128,2048]{2,1,0:T(8,128)(2,1)}, bf16[2,128,2048]{2,1,0:T(8,128)(2,1)}, u32[]{:S(2)}, u32[]{:S(2)}) collective-permute-start(bf16[2,128,2048]{2,1,0:T(8,128)(2,1)} %get-tuple-element.125), channel_id=1, source_target_pairs={{0,2},{1,3},{2,0},{3,1},{4,6},{5,7},{6,4},{7,5},{8,10},{9,11},{10,... | collective-permute-start | bytes 3145736 | tf_op jit(solution)/shard_map/ppermute | solution.py:399
  636.9 71.9 %all-to-all-start.3 = ((bf16[8,64,3072]{2,1,0:T(8,128)(2,1)}), bf16[8,64,3072]{2,1,0:T(8,128)(2,1)}, u32[]{:S(2)}, u32[]{:S(2)}) async-start(bf16[8,64,3072]{2,1,0:T(8,128)(2,1)} %bitcast.321), calls=%async_computation.5 | async-start | bytes 6291456 | tf_op jit(solution)/shard_map/all_to_all | solution.py:581
  657.7 46.6 %collective-permute-start.46 = (bf16[128,2048]{1,0:T(8,128)(2,1)}, bf16[128,2048]{1,0:T(8,128)(2,1)}, u32[]{:S(2)}, u32[]{:S(2)}) collective-permute-start(bf16[128,2048]{1,0:T(8,128)(2,1)} %fusion.62), channel_id=1, source_target_pairs={{0,2},{1,3},{2,0},{3,1},{4,6},{5,7},{6,4},{7,5},{8,10},{9,11},{10,... | collective-permute-start | bytes 1572872 | tf_op jit(solution)/shard_map/ppermute | solution.py:399
  662.4 43.5 %collective-permute-start.48 = (bf16[128,2048]{1,0:T(8,128)(2,1)}, bf16[128,2048]{1,0:T(8,128)(2,1)}, u32[]{:S(2)}, u32[]{:S(2)}) collective-permute-start(bf16[128,2048]{1,0:T(8,128)(2,1)} %fusion.64), channel_id=1, source_target_pairs={{0,4},{1,5},{2,6},{3,7},{4,0},{5,1},{6,2},{7,3},{8,12},{9,13},{10,... | collective-permute-start | bytes 1572872 | tf_op jit(solution)/shard_map/ppermute | solution.py:399
  (74 other events, 940.4 us)
Sparse Core Ops, SparseCore 0:
  19.4 29.9 all-gather.6
  54.1 65.4 all-gather.4
  133.6 150.7 all-gather.8
  285.8 78.9 all-gather.10
  367.0 75.2 reduce-scatter.4
  467.9 141.1 reduce-scatter.6
  616.0 25.1 reduce-scatter.10
  643.4 58.8 reduce-scatter.8

commit v4 on v3

--- a/solution.py
+++ b/solution.py
@@ -597,9 +597,7 @@
     back_one = scatter_group(parts, X, Y, x, ties.append, go_home)
     parts = feed_down(ties[0](after(activated, part_qkv)), wd, len(n2))
     returned = scatter_group(parts, X, Y, x)
-    back_one, sum_dgu, returned, sum_qkv = lax.optimization_barrier(
-        (back_one, homes[0], returned, sum_qkv)
-    )
+    sum_dgu, sum_qkv = lax.optimization_barrier((homes[0], sum_qkv))
     output = ((hidden_one + returned) * my_mask).astype(BF16)
     sum_d, sum_gu = sum_dgu[:, :, :share], sum_dgu[:, :, share:]
     grad_tokens = (

time: 751 us -> 750 us (level)
    another operation x11 -> x9, other arithmetic: 17.5 us -> 15.1 us  [scatter_group(): jnp.stack([a.astype(F32) + a_got.astype(F32), b.astype(F32) + b_got.astyp...]
    unnamed x114 -> x116, local copies, waits for them, and re-layouts: 35.5 us -> 36.7 us
  transfers between devices with their start and end apart: 63 -> 63, of which waited for: 36 -> 37; matrix products, arithmetic and copies ran while one was open for 15% -> 15% of each run, Pallas kernels for 25% -> 25%
where the time goes in v4:
time: 750 us; the launch traced here: 745 us
  waiting for transfers between devices  339 us (45%)
  Pallas kernels  187 us (25%)
  starting transfers between devices  76.7 us (10%)
  other arithmetic  75.3 us (10%)
  local copies, waits for them, and re-layouts  52 us (7%)
  between operations  15.2 us (2%)
    ppermute x50, waiting for transfers between devices, swap(): return lax.ppermute(value, BOTH, [(i, i ^ mask) for i in range(count)])  270 us
    pallas_call x5, Pallas kernels, call(): pl.pallas_call(body, out_shape=out_shape, grid_spec=pltpu.PrefetchScalarG...  128 us
    pallas_call x4, Pallas kernels, outer(): pl.pallas_call(body, out_shape=jax.ShapeDtypeStruct((height, width), BF16...  55.2 us
    ppermute x50, starting transfers between devices, swap(): return lax.ppermute(value, BOTH, [(i, i ^ mask) for i in range(count)])  53.8 us
    all_gather x4, waiting for transfers between devices, planes(): return lax.all_gather(value, 'dp', axis=0, tiled=True)  48.3 us
    unnamed x116, local copies, waits for them, and re-layouts  36.7 us
    convert_element_type x12, other arithmetic, add_low(): return (left.astype(F32) + right.astype(F32)).astype(BF16)  27.6 us
    another operation x9, other arithmetic, scatter_group(): jnp.stack([a.astype(F32) + a_got.astype(F32), b.astype(F32) + b_got.astyp...  15.1 us
  transfers between devices with their start and end apart: 63, of which 37 were waited for; matrix products, arithmetic and copies ran while one was open for 15% of the time, Pallas kernels for 25%

profile of v4, /device:TPU:0, one launch (start us, length us, event | category | flops | bytes accessed | tf_op | source)
XLA Modules:
  0.0 744.8 jit_solution(13284538422207858935)
XLA Ops:
  20.0 9.7 %all-to-all-done = bf16[8,64,768]{2,1,0:T(8,128)(2,1)} async-done(((bf16[8,64,768]{2,1,0:T(8,128)(2,1)}), bf16[8,64,768]{2,1,0:T(8,128)(2,1)}, u32[]{:S(2)}, u32[]{:S(2)}) %all-to-all-start) | async-done | bytes 786464 | tf_op jit(solution)/shard_map/all_to_all | solution.py:521
  36.3 8.0 %collective-permute-done = bf16[128,2048]{1,0:T(8,128)(2,1)} collective-permute-done((bf16[128,2048]{1,0:T(8,128)(2,1)}, bf16[128,2048]{1,0:T(8,128)(2,1)}, u32[]{:S(2)}, u32[]{:S(2)}) %collective-permute-start) | collective-permute-done | bytes 524320 | tf_op jit(solution)/shard_map/ppermute | solution.py:399
  61.0 16.5 %collective-permute-done.2 = bf16[128,2048]{1,0:T(8,128)(2,1)} collective-permute-done((bf16[128,2048]{1,0:T(8,128)(2,1)}, bf16[128,2048]{1,0:T(8,128)(2,1)}, u32[]{:S(2)}, u32[]{:S(2)}) %collective-permute-start.2) | collective-permute-done | bytes 524320 | tf_op jit(solution)/shard_map/ppermute | solution.py:399
  84.0 8.1 %collective-permute-done.5 = bf16[128,2048]{1,0:T(8,128)(2,1)S(1)} collective-permute-done((bf16[128,2048]{1,0:T(8,128)(2,1)}, bf16[128,2048]{1,0:T(8,128)(2,1)S(1)}, u32[]{:S(2)}, u32[]{:S(2)}) %collective-permute-start.5) | collective-permute-done | bytes 524320 | tf_op jit(solution)/shard_map/ppermute | solution.py:399
  97.0 8.1 %collective-permute-done.8 = bf16[128,2048]{1,0:T(8,128)(2,1)S(1)} collective-permute-done((bf16[128,2048]{1,0:T(8,128)(2,1)S(1)}, bf16[128,2048]{1,0:T(8,128)(2,1)S(1)}, u32[]{:S(2)}, u32[]{:S(2)}) %collective-permute-start.8) | collective-permute-done | bytes 524320 | tf_op jit(solution)/shard_map/ppermute | solution.py:399
  110.9 10.1 %collective-permute-done.9 = bf16[128,2048]{1,0:T(8,128)(2,1)S(1)} collective-permute-done((bf16[128,2048]{1,0:T(8,128)(2,1)S(1)}, bf16[128,2048]{1,0:T(8,128)(2,1)S(1)}, u32[]{:S(2)}, u32[]{:S(2)}) %collective-permute-start.9) | collective-permute-done | bytes 524320 | tf_op jit(solution)/shard_map/ppermute | solution.py:399
  121.9 7.2 collective-permute-done.10
  143.9 23.5 %attention_forward.1 = (bf16[1024,2048]{1,0:T(8,128)(2,1)}, bf16[1024,2048]{1,0:T(8,128)(2,1)}, bf16[2048,768]{1,0:T(8,128)(2,1)}, bf16[2048,256]{1,0:T(8,128)(2,1)}) custom-call(s32[16]{0:T(128)} %reshape.405.live_ref, bf16[1024,2048]{1,0:T(8,128)(2,1)} %constant_dynamic-update-slice_fusion.refs_0_, bf16[1024,2048]{1,0:T(8,128)(2,1)} %collective-permute-done.6.refs_1_, ...), custom_call_target="tpu_custom_call" | custom-call | flops 171798688 | bytes 513802 | tf_op jit(solution)/shard_map/attention_forward/pallas_call | solution.py:92
  167.6 7.2 collective-permute-done.15
  180.2 23.0 %collective-permute-done.18 = bf16[2,128,2048]{2,1,0:T(8,128)(2,1)S(1)} collective-permute-done((bf16[2,128,2048]{2,1,0:T(8,128)(2,1)S(1)}, bf16[2,128,2048]{2,1,0:T(8,128)(2,1)S(1)}, u32[]{:S(2)}, u32[]{:S(2)}) %collective-permute-start.18) | collective-permute-done | bytes 1048608 | tf_op jit(solution)/shard_map/ppermute | solution.py:399
  235.3 7.5 %collective-permute-done.20 = bf16[128,2048]{1,0:T(8,128)(2,1)} collective-permute-done((bf16[128,2048]{1,0:T(8,128)(2,1)}, bf16[128,2048]{1,0:T(8,128)(2,1)}, u32[]{:S(2)}, u32[]{:S(2)}) %collective-permute-start.20) | collective-permute-done | bytes 524320 | tf_op jit(solution)/shard_map/ppermute | solution.py:399
  255.6 7.9 %collective-permute-done.22 = bf16[128,2048]{1,0:T(8,128)(2,1)S(1)} collective-permute-done((bf16[128,2048]{1,0:T(8,128)(2,1)}, bf16[128,2048]{1,0:T(8,128)(2,1)S(1)}, u32[]{:S(2)}, u32[]{:S(2)}) %collective-permute-start.22) | collective-permute-done | bytes 524320 | tf_op jit(solution)/shard_map/ppermute | solution.py:399
  269.3 15.0 %all-gather.9.cloned.1.call-done.refs_2_.refs_5_ = bf16[2048,2048]{1,0:T(8,128)(2,1)} async-done(((bf16[512,2048]{1,0:T(8,128)(2,1)}), bf16[2048,2048]{1,0:T(8,128)(2,1)}) %all-gather.9.cloned.1.call-update) | async-done | bytes 8388624 | tf_op jit(solution)/shard_map/all_gather | solution.py:513
  284.4 7.4 collective-permute-done.26.refs_1_
  291.8 25.7 %feed_forward.1 = (f32[2048,1024]{1,0:T(8,128)}, f32[2048,1024]{1,0:T(8,128)}, bf16[2048,1024]{1,0:T(8,128)(2,1)}) custom-call(bf16[1024,2048]{1,0:T(8,128)(2,1)} %constant_dynamic-update-slice_fusion.16.refs_0_, bf16[1024,2048]{1,0:T(8,128)(2,1)} %collective-permute-done.26.refs_1_, bf16[2048,2048]{1,0:T(8,128)(2,1)} %all-gather.9.cloned.1.call-done.refs_2_.refs_5_), custom_call_target="tpu_custom_call" | custom-call | flops 343597376 | bytes 754974 | tf_op jit(solution)/shard_map/feed_forward/pallas_call | solution.py:92
  317.6 13.3 %outer.4 = bf16[2048,1024]{1,0:T(8,128)(2,1)} custom-call(bf16[1024,2048]{1,0:T(8,128)(2,1)} %constant_dynamic-update-slice_fusion.8.refs_0_, bf16[1024,2048]{1,0:T(8,128)(2,1)} %collective-permute-done.14.refs_1_, bf16[2048,1024]{1,0:T(8,128)(2,1)} %get-tuple-element.75.refs_2_.active_ref), custom_call_target="tpu_custom_call" | custom-call | flops 171798688 | bytes 335544 | tf_op jit(solution)/shard_map/outer/pallas_call | solution.py:345
  331.4 33.4 %all-gather.11.cloned.1.call-done.refs_4_.wd_ref = bf16[2048,1024]{1,0:T(8,128)(2,1)} async-done(((bf16[512,1024]{1,0:T(8,128)(2,1)}), bf16[2048,1024]{1,0:T(8,128)(2,1)}) %all-gather.11.cloned.1.call-update) | async-done | bytes 4194320 | tf_op jit(solution)/shard_map/all_gather | solution.py:513
  364.8 38.5 %feed_back.1 = (bf16[1024,2048]{1,0:T(8,128)(2,1)}, bf16[1024,2048]{1,0:T(8,128)(2,1)}, bf16[2048,2048]{1,0:T(8,128)(2,1)}) custom-call(bf16[1024,2048]{1,0:T(8,128)(2,1)} %constant_dynamic-update-slice_fusion.8.refs_0_, bf16[1024,2048]{1,0:T(8,128)(2,1)} %collective-permute-done.14.refs_1_, f32[2048,1024]{1,0:T(8,128)} %get-tuple-element.60.refs_2_, ...), custom_call_target="tpu_custom_call" | custom-call | flops 515396064 | bytes 1090519 | tf_op jit(solution)/shard_map/feed_back/pallas_call | solution.py:92
  403.3 7.4 collective-permute-done.27
  416.6 22.5 %collective-permute-done.30 = bf16[2,128,2048]{2,1,0:T(8,128)(2,1)S(1)} collective-permute-done((bf16[2,128,2048]{2,1,0:T(8,128)(2,1)S(1)}, bf16[2,128,2048]{2,1,0:T(8,128)(2,1)S(1)}, u32[]{:S(2)}, u32[]{:S(2)}) %collective-permute-start.30) | collective-permute-done | bytes 1048608 | tf_op jit(solution)/shard_map/ppermute | solution.py:399
  443.9 23.8 %outer.5 = bf16[2048,2048]{1,0:T(8,128)(2,1)} custom-call(bf16[1024,2048]{1,0:T(8,128)(2,1)} %constant_dynamic-update-slice_fusion.16.refs_0_, bf16[1024,2048]{1,0:T(8,128)(2,1)} %collective-permute-done.26.refs_1_, bf16[2048,2048]{1,0:T(8,128)(2,1)} %get-tuple-element.66.refs_2_), custom_call_target="tpu_custom_call" | custom-call | flops 17179869184 | bytes 25165824 | tf_op jit(solution)/shard_map/outer/pallas_call | solution.py:345
  478.5 10.2 %collective-permute-done.32 = bf16[128,2048]{1,0:T(8,128)(2,1)S(1)} collective-permute-done((bf16[128,2048]{1,0:T(8,128)(2,1)S(1)}, bf16[128,2048]{1,0:T(8,128)(2,1)S(1)}, u32[]{:S(2)}, u32[]{:S(2)}) %collective-permute-start.32) | collective-permute-done | bytes 524320 | tf_op jit(solution)/shard_map/ppermute | solution.py:399
  493.0 9.6 %collective-permute-done.33 = bf16[128,2048]{1,0:T(8,128)(2,1)S(1)} collective-permute-done((bf16[128,2048]{1,0:T(8,128)(2,1)S(1)}, bf16[128,2048]{1,0:T(8,128)(2,1)S(1)}, u32[]{:S(2)}, u32[]{:S(2)}) %collective-permute-start.33) | collective-permute-done | bytes 524320 | tf_op jit(solution)/shard_map/ppermute | solution.py:399
  502.7 9.3 %collective-permute-done.34 = bf16[128,2048]{1,0:T(8,128)(2,1)S(1)} collective-permute-done((bf16[128,2048]{1,0:T(8,128)(2,1)S(1)}, bf16[128,2048]{1,0:T(8,128)(2,1)S(1)}, u32[]{:S(2)}, u32[]{:S(2)}) %collective-permute-start.34) | collective-permute-done | bytes 524320 | tf_op jit(solution)/shard_map/ppermute | solution.py:399
  531.6 26.3 %attention_backward.1 = (bf16[1024,2048]{1,0:T(8,128)(2,1)}, bf16[1024,2048]{1,0:T(8,128)(2,1)}, bf16[2048,768]{1,0:T(8,128)(2,1)}) custom-call(s32[16]{0:T(128)} %reshape.405.live_ref, bf16[1024,2048]{1,0:T(8,128)(2,1)} %copy-done.11, bf16[1024,2048]{1,0:T(8,128)(2,1)} %copy-done.23, bf16[2048,768]{1,0:T(8,128)(2,1)} %get-tuple-element.70.refs_2_, ...), custom_call_target="tpu_custom_call" | custom-call | flops 8589934592 | bytes 27787264 | tf_op jit(solution)/shard_map/attention_backward/pallas_call | solution.py:92
  571.5 11.0 %outer.7 = bf16[2048,768]{1,0:T(8,128)(2,1)} custom-call(bf16[1024,2048]{1,0:T(8,128)(2,1)} %constant_dynamic-update-slice_fusion.refs_0_, bf16[1024,2048]{1,0:T(8,128)(2,1)} %collective-permute-done.6.refs_1_, bf16[2048,768]{1,0:T(8,128)(2,1)} %get-tuple-element.71.refs_2_), custom_call_target="tpu_custom_call" | custom-call | flops 6442450944 | bytes 14680064 | tf_op jit(solution)/shard_map/outer/pallas_call | solution.py:345
  585.8 9.2 %collective-permute-done.40 = bf16[2,128,2048]{2,1,0:T(8,128)(2,1)} collective-permute-done((bf16[2,128,2048]{2,1,0:T(8,128)(2,1)}, bf16[2,128,2048]{2,1,0:T(8,128)(2,1)}, u32[]{:S(2)}, u32[]{:S(2)}) %collective-permute-start.40) | collective-permute-done | bytes 1048608 | tf_op jit(solution)/shard_map/ppermute | solution.py:399
  599.0 14.5 %feed_down.1 = (bf16[1024,2048]{1,0:T(8,128)(2,1)}, bf16[1024,2048]{1,0:T(8,128)(2,1)}) custom-call(bf16[2048,1024]{1,0:T(8,128)(2,1)} %get-tuple-element.75.refs_2_.active_ref, bf16[2048,1024]{1,0:T(8,128)(2,1)} %all-gather.11.cloned.1.call-done.refs_4_.wd_ref), custom_call_target="tpu_custom_call" | custom-call | flops 8589934592 | bytes 16777216 | tf_op jit(solution)/shard_map/feed_down/pallas_call | solution.py:92
  619.4 11.9 %collective-permute-done.48 = bf16[128,2048]{1,0:T(8,128)(2,1)} collective-permute-done((bf16[128,2048]{1,0:T(8,128)(2,1)}, bf16[128,2048]{1,0:T(8,128)(2,1)}, u32[]{:S(2)}, u32[]{:S(2)}) %collective-permute-start.48) | collective-permute-done | bytes 524320 | tf_op jit(solution)/shard_map/ppermute | solution.py:399
  649.8 15.5 %collective-permute-done.45 = bf16[2,128,2048]{2,1,0:T(8,128)(2,1)} collective-permute-done((bf16[2,128,2048]{2,1,0:T(8,128)(2,1)}, bf16[2,128,2048]{2,1,0:T(8,128)(2,1)}, u32[]{:S(2)}, u32[]{:S(2)}) %collective-permute-start.45) | collective-permute-done | bytes 1048608 | tf_op jit(solution)/shard_map/ppermute | solution.py:399
  670.6 9.5 %collective-permute-start.44 = (bf16[128,2048]{1,0:T(8,128)(2,1)}, bf16[128,2048]{1,0:T(8,128)(2,1)}, u32[]{:S(2)}, u32[]{:S(2)}) collective-permute-start(bf16[128,2048]{1,0:T(8,128)(2,1)} %fusion.67), channel_id=1, source_target_pairs={{0,2},{1,3},{2,0},{3,1},{4,6},{5,7},{6,4},{7,5},{8,10},{9,11},{10,... | collective-permute-start | bytes 1572872 | tf_op jit(solution)/shard_map/ppermute | solution.py:399
  685.5 26.4 %collective-permute-done.46 = bf16[128,2048]{1,0:T(8,128)(2,1)} collective-permute-done((bf16[128,2048]{1,0:T(8,128)(2,1)}, bf16[128,2048]{1,0:T(8,128)(2,1)}, u32[]{:S(2)}, u32[]{:S(2)}) %collective-permute-start.46) | collective-permute-done | bytes 524320 | tf_op jit(solution)/shard_map/ppermute | solution.py:399
  (321 shorter events, 252.3 us)
Async XLA Ops:
  17.0 117.6 %all-gather.7.cloned.1.call-start = ((), (), s32[]{:S(2)}) async-start(), calls=%async_computation.10 | async-start | bytes 1310720 | tf_op jit(solution)/shard_map/all_gather | solution.py:513
  34.8 24.4 %collective-permute-start.1 = (bf16[128,2048]{1,0:T(8,128)(2,1)}, bf16[128,2048]{1,0:T(8,128)(2,1)}, u32[]{:S(2)}, u32[]{:S(2)}) collective-permute-start(bf16[128,2048]{1,0:T(8,128)(2,1)} %get-tuple-element.160), channel_id=1, source_target_pairs={{0,4},{1,5},{2,6},{3,7},{4,0},{5,1},{6,2},{7,3},{8,12},{9,13},{10,... | collective-permute-start | bytes 1572872 | tf_op jit(solution)/shard_map/ppermute | solution.py:399
  44.3 33.2 %collective-permute-start.2 = (bf16[128,2048]{1,0:T(8,128)(2,1)}, bf16[128,2048]{1,0:T(8,128)(2,1)}, u32[]{:S(2)}, u32[]{:S(2)}) collective-permute-start(bf16[128,2048]{1,0:T(8,128)(2,1)} %collective-permute-done), channel_id=1, source_target_pairs={{0,4},{1,5},{2,6},{3,7},{4,0},{5,1},{6,2},{7,3},{8,12},{9,13},{10,... | collective-permute-start | bytes 1572872 | tf_op jit(solution)/shard_map/ppermute | solution.py:399
  45.5 36.7 %collective-permute-start.4 = (bf16[128,2048]{1,0:T(8,128)(2,1)}, bf16[128,2048]{1,0:T(8,128)(2,1)}, u32[]{:S(2)}, u32[]{:S(2)}) collective-permute-start(bf16[128,2048]{1,0:T(8,128)(2,1)} %get-tuple-element.159), channel_id=1, source_target_pairs={{0,2},{1,3},{2,0},{3,1},{4,6},{5,7},{6,4},{7,5},{8,10},{9,11},{10,... | collective-permute-start | bytes 1572872 | tf_op jit(solution)/shard_map/ppermute | solution.py:399
  47.2 45.8 %all-to-all-start.1 = ((bf16[8,64,2048]{2,1,0:T(8,128)(2,1)}), bf16[8,64,2048]{2,1,0:T(8,128)(2,1)}, u32[]{:S(2)}, u32[]{:S(2)}) async-start(bf16[8,64,2048]{2,1,0:T(8,128)(2,1)} %pad_maximum_fusion.1), calls=%async_computation.1 | async-start | bytes 4194304 | tf_op jit(solution)/shard_map/all_to_all | solution.py:521
  51.6 90.9 %all-gather.5.cloned.1.call-start = ((), (), s32[]{:S(2)}) async-start(), calls=%async_computation.9 | async-start | bytes 3932160 | tf_op jit(solution)/shard_map/all_gather | solution.py:513
  52.3 232.0 %all-gather.9.cloned.1.call-start = ((), (), s32[]{:S(2)}) async-start(), calls=%async_computation.11 | async-start | bytes 10485760 | tf_op jit(solution)/shard_map/all_gather | solution.py:513
  52.6 39.6 %collective-permute-start.5 = (bf16[128,2048]{1,0:T(8,128)(2,1)}, bf16[128,2048]{1,0:T(8,128)(2,1)S(1)}, u32[]{:S(2)}, u32[]{:S(2)}) collective-permute-start(bf16[128,2048]{1,0:T(8,128)(2,1)} %collective-permute-done.3), channel_id=1, source_target_pairs={{0,2},{1,3},{2,0},{3,1},{4,6},{5,7},{6,4},{7,5},{8,10},{9,11},{10,... | collective-permute-start | bytes 1572872 | tf_op jit(solution)/shard_map/ppermute | solution.py:399
  96.7 45.8 %collective-permute-start.6 = (bf16[1024,2048]{1,0:T(8,128)(2,1)}, bf16[1024,2048]{1,0:T(8,128)(2,1)}, u32[]{:S(2)}, u32[]{:S(2)}) collective-permute-start(bf16[1024,2048]{1,0:T(8,128)(2,1)} %constant_dynamic-update-slice_fusion.refs_0_), channel_id=1, source_target_pairs={{0,1},{1,0},{2,3},{3,2},{4,5},{5,4},{6,7},{7,6},{8,9},{9,8},{10,11... | collective-permute-start | bytes 12582920 | tf_op jit(solution)/shard_map/ppermute | solution.py:399
  96.7 24.3 %collective-permute-start.9 = (bf16[128,2048]{1,0:T(8,128)(2,1)S(1)}, bf16[128,2048]{1,0:T(8,128)(2,1)S(1)}, u32[]{:S(2)}, u32[]{:S(2)}) collective-permute-start(bf16[128,2048]{1,0:T(8,128)(2,1)S(1)} %get-tuple-element.154), channel_id=1, source_target_pairs={{0,4},{1,5},{2,6},{3,7},{4,0},{5,1},{6,2},{7,3},{8,12},{9,13},{10,... | collective-permute-start | bytes 1572872 | tf_op jit(solution)/shard_map/ppermute | solution.py:399
  133.4 34.0 %collective-permute-start.14 = (bf16[1024,2048]{1,0:T(8,128)(2,1)}, bf16[1024,2048]{1,0:T(8,128)(2,1)}, u32[]{:S(2)}, u32[]{:S(2)}) collective-permute-start(bf16[1024,2048]{1,0:T(8,128)(2,1)} %constant_dynamic-update-slice_fusion.8.refs_0_), channel_id=1, source_target_pairs={{0,1},{1,0},{2,3},{3,2},{4,5},{5,4},{6,7},{7,6},{8,9},{9,8},{10,11... | collective-permute-start | bytes 12582920 | tf_op jit(solution)/shard_map/ppermute | solution.py:399
  177.9 25.3 %collective-permute-start.18 = (bf16[2,128,2048]{2,1,0:T(8,128)(2,1)S(1)}, bf16[2,128,2048]{2,1,0:T(8,128)(2,1)S(1)}, u32[]{:S(2)}, u32[]{:S(2)}) collective-permute-start(bf16[2,128,2048]{2,1,0:T(8,128)(2,1)S(1)} %get-tuple-element.133), channel_id=1, source_target_pairs={{0,2},{1,3},{2,0},{3,1},{4,6},{5,7},{6,4},{7,5},{8,10},{9,11},{10,... | collective-permute-start | bytes 3145736 | tf_op jit(solution)/shard_map/ppermute | solution.py:399
  178.5 26.6 %collective-permute-start.16 = (bf16[2,128,2048]{2,1,0:T(8,128)(2,1)S(1)}, bf16[2,128,2048]{2,1,0:T(8,128)(2,1)S(1)}, u32[]{:S(2)}, u32[]{:S(2)}) collective-permute-start(bf16[2,128,2048]{2,1,0:T(8,128)(2,1)S(1)} %get-tuple-element.135), channel_id=1, source_target_pairs={{0,4},{1,5},{2,6},{3,7},{4,0},{5,1},{6,2},{7,3},{8,12},{9,13},{10,... | collective-permute-start | bytes 3145736 | tf_op jit(solution)/shard_map/ppermute | solution.py:399
  208.6 24.6 %all-to-all-start.2 = ((bf16[8,64,1024]{2,1,0:T(8,128)(2,1)}), bf16[8,64,1024]{2,1,0:T(8,128)(2,1)}, u32[]{:S(2)}, u32[]{:S(2)}) async-start(bf16[8,64,1024]{2,1,0:T(8,128)(2,1)} %bitcast.344), calls=%async_computation.2 | async-start | bytes 2097152 | tf_op jit(solution)/shard_map/all_to_all | solution.py:521
  212.8 151.9 %all-gather.11.cloned.1.call-start = ((), (), s32[]{:S(2)}) async-start(), calls=%async_computation.12 | async-start | bytes 5242880 | tf_op jit(solution)/shard_map/all_gather | solution.py:513
  233.2 239.4 %reduce-scatter.5.cloned.1.call-start = ((), (), s32[]{:S(2)}) async-start(), calls=%async_computation.13 | async-start | bytes 5242880 | tf_op jit(solution)/shard_map/reduce_scatter | solution.py:516
  330.9 284.9 %reduce-scatter.7.cloned.1.call-start = ((), (), s32[]{:S(2)}) async-start(), calls=%async_computation.14 | async-start | bytes 10485760 | tf_op jit(solution)/shard_map/reduce_scatter | solution.py:516
  413.8 25.3 %collective-permute-start.30 = (bf16[2,128,2048]{2,1,0:T(8,128)(2,1)S(1)}, bf16[2,128,2048]{2,1,0:T(8,128)(2,1)S(1)}, u32[]{:S(2)}, u32[]{:S(2)}) collective-permute-start(bf16[2,128,2048]{2,1,0:T(8,128)(2,1)S(1)} %get-tuple-element.129), channel_id=1, source_target_pairs={{0,2},{1,3},{2,0},{3,1},{4,6},{5,7},{6,4},{7,5},{8,10},{9,11},{10,... | collective-permute-start | bytes 3145736 | tf_op jit(solution)/shard_map/ppermute | solution.py:399
  415.1 26.3 %collective-permute-start.28 = (bf16[2,128,2048]{2,1,0:T(8,128)(2,1)S(1)}, bf16[2,128,2048]{2,1,0:T(8,128)(2,1)S(1)}, u32[]{:S(2)}, u32[]{:S(2)}) collective-permute-start(bf16[2,128,2048]{2,1,0:T(8,128)(2,1)S(1)} %get-tuple-element.131), channel_id=1, source_target_pairs={{0,4},{1,5},{2,6},{3,7},{4,0},{5,1},{6,2},{7,3},{8,12},{9,13},{10,... | collective-permute-start | bytes 3145736 | tf_op jit(solution)/shard_map/ppermute | solution.py:399
  440.2 27.6 %collective-permute-start.31 = (bf16[128,2048]{1,0:T(8,128)(2,1)}, bf16[128,2048]{1,0:T(8,128)(2,1)}, u32[]{:S(2)}, u32[]{:S(2)}) collective-permute-start(bf16[128,2048]{1,0:T(8,128)(2,1)} %fusion.63), channel_id=1, source_target_pairs={{0,4},{1,5},{2,6},{3,7},{4,0},{5,1},{6,2},{7,3},{8,12},{9,13},{10,... | collective-permute-start | bytes 1572872 | tf_op jit(solution)/shard_map/ppermute | solution.py:399
  442.4 27.1 %collective-permute-start.29 = (bf16[128,2048]{1,0:T(8,128)(2,1)}, bf16[128,2048]{1,0:T(8,128)(2,1)}, u32[]{:S(2)}, u32[]{:S(2)}) collective-permute-start(bf16[128,2048]{1,0:T(8,128)(2,1)} %fusion.61), channel_id=1, source_target_pairs={{0,2},{1,3},{2,0},{3,1},{4,6},{5,7},{6,4},{7,5},{8,10},{9,11},{10,... | collective-permute-start | bytes 1572872 | tf_op jit(solution)/shard_map/ppermute | solution.py:399
  467.7 215.9 %reduce-scatter.11.cloned.1.call-start = ((), (), s32[]{:S(2)}) async-start(), calls=%async_computation.16 | async-start | bytes 1310720 | tf_op jit(solution)/shard_map/reduce_scatter | solution.py:516
  477.6 25.0 %collective-permute-start.33 = (bf16[128,2048]{1,0:T(8,128)(2,1)S(1)}, bf16[128,2048]{1,0:T(8,128)(2,1)S(1)}, u32[]{:S(2)}, u32[]{:S(2)}) collective-permute-start(bf16[128,2048]{1,0:T(8,128)(2,1)S(1)} %get-tuple-element.150), channel_id=1, source_target_pairs={{0,4},{1,5},{2,6},{3,7},{4,0},{5,1},{6,2},{7,3},{8,12},{9,13},{10,... | collective-permute-start | bytes 1572872 | tf_op jit(solution)/shard_map/ppermute | solution.py:399
  569.4 25.6 %collective-permute-start.40 = (bf16[2,128,2048]{2,1,0:T(8,128)(2,1)}, bf16[2,128,2048]{2,1,0:T(8,128)(2,1)}, u32[]{:S(2)}, u32[]{:S(2)}) collective-permute-start(bf16[2,128,2048]{2,1,0:T(8,128)(2,1)} %get-tuple-element.126), channel_id=1, source_target_pairs={{0,4},{1,5},{2,6},{3,7},{4,0},{5,1},{6,2},{7,3},{8,12},{9,13},{10,... | collective-permute-start | bytes 3145736 | tf_op jit(solution)/shard_map/ppermute | solution.py:399
  569.8 27.1 %collective-permute-start.41 = (bf16[2,128,2048]{2,1,0:T(8,128)(2,1)}, bf16[2,128,2048]{2,1,0:T(8,128)(2,1)}, u32[]{:S(2)}, u32[]{:S(2)}) collective-permute-start(bf16[2,128,2048]{2,1,0:T(8,128)(2,1)} %get-tuple-element.125), channel_id=1, source_target_pairs={{0,2},{1,3},{2,0},{3,1},{4,6},{5,7},{6,4},{7,5},{8,10},{9,11},{10,... | collective-permute-start | bytes 3145736 | tf_op jit(solution)/shard_map/ppermute | solution.py:399
  585.8 27.7 %collective-permute-start.49 = (bf16[2,64,2048]{2,1,0:T(8,128)(2,1)}, bf16[2,64,2048]{2,1,0:T(8,128)(2,1)S(1)}, u32[]{:S(2)}, u32[]{:S(2)}) collective-permute-start(bf16[2,64,2048]{2,1,0:T(8,128)(2,1)} %select_bitcast_fusion), channel_id=1, source_target_pairs={{0,1},{1,0},{2,3},{3,2},{4,5},{5,4},{6,7},{7,6},{8,9},{9,8},{10,11... | collective-permute-start | bytes 1572872 | tf_op jit(solution)/shard_map/ppermute | solution.py:399
  615.8 100.7 %reduce-scatter.9.cloned.1.call-start = ((), (), s32[]{:S(2)}) async-start(), calls=%async_computation.15 | async-start | bytes 3932160 | tf_op jit(solution)/shard_map/reduce_scatter | solution.py:516
  638.8 26.4 %collective-permute-start.45 = (bf16[2,128,2048]{2,1,0:T(8,128)(2,1)}, bf16[2,128,2048]{2,1,0:T(8,128)(2,1)}, u32[]{:S(2)}, u32[]{:S(2)}) collective-permute-start(bf16[2,128,2048]{2,1,0:T(8,128)(2,1)} %get-tuple-element.121), channel_id=1, source_target_pairs={{0,2},{1,3},{2,0},{3,1},{4,6},{5,7},{6,4},{7,5},{8,10},{9,11},{10,... | collective-permute-start | bytes 3145736 | tf_op jit(solution)/shard_map/ppermute | solution.py:399
  642.1 26.4 %collective-permute-start.43 = (bf16[2,128,2048]{2,1,0:T(8,128)(2,1)}, bf16[2,128,2048]{2,1,0:T(8,128)(2,1)}, u32[]{:S(2)}, u32[]{:S(2)}) collective-permute-start(bf16[2,128,2048]{2,1,0:T(8,128)(2,1)} %get-tuple-element.123), channel_id=1, source_target_pairs={{0,4},{1,5},{2,6},{3,7},{4,0},{5,1},{6,2},{7,3},{8,12},{9,13},{10,... | collective-permute-start | bytes 3145736 | tf_op jit(solution)/shard_map/ppermute | solution.py:399
  645.2 71.2 %all-to-all-start.3 = ((bf16[8,64,3072]{2,1,0:T(8,128)(2,1)}), bf16[8,64,3072]{2,1,0:T(8,128)(2,1)}, u32[]{:S(2)}, u32[]{:S(2)}) async-start(bf16[8,64,3072]{2,1,0:T(8,128)(2,1)} %bitcast.350), calls=%async_computation.5 | async-start | bytes 6291456 | tf_op jit(solution)/shard_map/all_to_all | solution.py:581
  667.4 44.4 %collective-permute-start.46 = (bf16[128,2048]{1,0:T(8,128)(2,1)}, bf16[128,2048]{1,0:T(8,128)(2,1)}, u32[]{:S(2)}, u32[]{:S(2)}) collective-permute-start(bf16[128,2048]{1,0:T(8,128)(2,1)} %fusion.69), channel_id=1, source_target_pairs={{0,4},{1,5},{2,6},{3,7},{4,0},{5,1},{6,2},{7,3},{8,12},{9,13},{10,... | collective-permute-start | bytes 1572872 | tf_op jit(solution)/shard_map/ppermute | solution.py:399
  670.6 42.8 %collective-permute-start.44 = (bf16[128,2048]{1,0:T(8,128)(2,1)}, bf16[128,2048]{1,0:T(8,128)(2,1)}, u32[]{:S(2)}, u32[]{:S(2)}) collective-permute-start(bf16[128,2048]{1,0:T(8,128)(2,1)} %fusion.67), channel_id=1, source_target_pairs={{0,2},{1,3},{2,0},{3,1},{4,6},{5,7},{6,4},{7,5},{8,10},{9,11},{10,... | collective-permute-start | bytes 1572872 | tf_op jit(solution)/shard_map/ppermute | solution.py:399
  (75 other events, 944.3 us)
Sparse Core Ops, SparseCore 0:
  19.4 29.9 all-gather.6
  54.0 65.4 all-gather.4
  133.6 150.7 all-gather.8
  285.7 78.9 all-gather.10
  366.9 75.2 reduce-scatter.4
  467.8 141.1 reduce-scatter.6
  615.9 25.1 reduce-scatter.10
  643.5 58.8 reduce-scatter.8
